TPU v7x, 32 devices: a whole 2x2x4 slice. The times are simulated.
32 devices in a mesh: seg: 8 (over z, core), patch: 4 (over y, x).
Axes of the slice: x: 2, y: 2, z: 4, core: 2. Of those that a mesh axis runs over, the one named last changes fastest.
Arguments:
- incident: bfloat16 [8, 64, 4096], P('seg', None, 'patch'), may hold values from -6 to 6
- wall_axial: float32 [8, 4096], P('seg'), may hold values from 0 to 1
- wall_angle: float32 [8, 4096], P('seg'), may hold values from -3.140625 to 3.140625
- wall_area: float32 [8, 4096], P('seg'), may hold values from 0.5 to 2
- visibility: int32 [8, 2, 32, 32], P('seg', None, 'patch'), may hold values 0 or 1
- end_reflection: float32 [2, 32], replicated, may hold values from -0.9 to 0.9
Outputs:
- currents: bfloat16 [8, 64, 4096], P('seg', None, 'patch')
Inputs may be any that keep to these rules, and one draw needn't show every extreme that they name: `visibility`: 1 where the source block is lit for the target block, 0 where it is in shadow.
All inputs are finite; a program needn't handle non-finite values.
Results may differ from a plain program's by a relative error of at most 0.0034.
Values may be sent and summed in bfloat16 or wider, within the bound.
No kernel may reach another device: no remote copies, remote signals or barrier semaphores. Data moves between devices by JAX's collectives and lax.ppermute only.
A program may use at most 64 MiB of HBM per device.

v0:
```python
import math

import jax
import jax.numpy as jnp
from jax import lax
from jax.sharding import PartitionSpec as P

ITERS = 2


WAVENUMBER = 40.0
RADIUS = 0.5
SOFTENING = 0.25


def extended(x, sides, width):
    for axis, dim in sides:
        count, length = (lax.axis_size(axis), x.shape[dim])
        up = [(i, (i + 1) % count) for i in range(count - 1)]
        down = [(j, i) for i, j in up]
        last = lax.slice_in_dim(x, length - width, length, axis=dim)
        leading = lax.slice_in_dim(x, 0, width, axis=dim)
        before = lax.ppermute(last, axis, up)
        after = lax.ppermute(leading, axis, down)
        x = jnp.concatenate([before, x, after], axis=dim)
    return x


def from_behind(value, axis, steps):
    count = lax.axis_size(axis)
    leading, last = (max(0, -steps), min(count, count - steps))
    return lax.ppermute(value, axis, [(source, source + steps) for source in range(leading, last)])


def kernel_piece(target, source, offset, visible, patches):
    axial_gap = offset + target[0][:, None] - source[0][None, :]
    chord = 2.0 * RADIUS * RADIUS * (1.0 - jnp.cos(target[1][:, None] - source[1][None, :]))
    squared = axial_gap * axial_gap + chord
    magnitude = (
        source[2][None, :] * visible.astype(jnp.float32) / jnp.sqrt(patches * (squared + SOFTENING))
    )
    phases = WAVENUMBER * jnp.sqrt(squared)
    kernel_re = (magnitude * jnp.cos(phases)).astype(jnp.bfloat16)
    kernel_im = (-magnitude * jnp.sin(phases)).astype(jnp.bfloat16)
    return (kernel_re, kernel_im)


def couple(sources, kernel_re, kernel_im, angles):
    contract = (((1,), (1,)), ((), ()))
    prod_re = lax.dot_general(sources, kernel_re, contract, preferred_element_type=jnp.float32)
    prod_im = lax.dot_general(sources, kernel_im, contract, preferred_element_type=jnp.float32)
    return jnp.concatenate(
        [prod_re[:angles] - prod_im[angles:], prod_re[angles:] + prod_im[:angles]], 0
    )


def reflect(coef, values, angles):
    coef_re = coef[:angles][:, None]
    coef_im = coef[angles:][:, None]
    real_part = values[:angles]
    imag_part = values[angles:]
    return jnp.concatenate(
        [coef_re * real_part - coef_im * imag_part, coef_re * imag_part + coef_im * real_part], 0
    )


def on_device(incident, wall_axial, wall_angle, wall_area, visibility, end_reflection):
    channel_count = incident.shape[1]
    target_rows = incident.shape[2]
    patches = wall_axial.shape[1]
    angles = channel_count // 4
    block_size = patches // visibility.shape[3]
    seg_count = lax.axis_size("seg")
    seg_index = lax.axis_index("seg")
    patch_index = lax.axis_index("patch")
    geometry = jnp.stack([wall_axial[0], wall_angle[0], wall_area[0]])[None]
    nearby = extended(geometry, (("seg", 0),), 1)
    before_geo = nearby[0]
    after_geo = nearby[2]
    target = lax.dynamic_slice_in_dim(geometry[0], patch_index * target_rows, target_rows, 1)
    lit_rows = jnp.repeat(visibility[0], block_size, axis=1)
    gen_rows = math.gcd(32, target_rows)

    def build_block(block_index):
        row_start = block_index * gen_rows
        target_block = lax.dynamic_slice_in_dim(target, row_start, gen_rows, 1)
        lit_block = lax.dynamic_slice_in_dim(lit_rows, row_start, gen_rows, 1)
        lit_block = jnp.repeat(lit_block, block_size, axis=2)
        fore_re, fore_im = kernel_piece(target_block, before_geo, 1.0, lit_block[0], patches)
        back_re, back_im = kernel_piece(target_block, after_geo, -1.0, lit_block[1], patches)
        return (fore_re, fore_im, back_re, back_im)

    tables = lax.map(build_block, jnp.arange(target_rows // gen_rows, dtype=jnp.int32))
    fore_re, fore_im, back_re, back_im = [table.reshape(target_rows, patches) for table in tables]
    at_first = seg_index == 0
    at_last = seg_index == seg_count - 1
    state = incident
    for sweep in range(ITERS):
        before_cur = from_behind(state[0, : 2 * angles], "seg", 1)
        after_cur = from_behind(state[0, 2 * angles :], "seg", -1)
        forward = couple(
            lax.all_gather(before_cur, "patch", axis=1, tiled=True), fore_re, fore_im, angles
        )
        backward = couple(
            lax.all_gather(after_cur, "patch", axis=1, tiled=True), back_re, back_im, angles
        )
        coupled = jnp.concatenate([forward, backward], 0)
        previous = state[0].astype(jnp.float32)
        first_end = reflect(end_reflection[0], previous[2 * angles :], angles)
        last_end = reflect(end_reflection[1], previous[: 2 * angles], angles)
        mirrored = jnp.concatenate(
            [jnp.where(at_first, first_end, 0.0), jnp.where(at_last, last_end, 0.0)], 0
        )
        state = (incident[0].astype(jnp.float32) + coupled + mirrored).astype(jnp.bfloat16)[None]
    return state


def solution(mesh):
    return jax.shard_map(
        on_device,
        mesh=mesh,
        in_specs=(
            P("seg", None, "patch"),
            P("seg", None),
            P("seg", None),
            P("seg", None),
            P("seg", None, "patch", None),
            P(),
        ),
        out_specs=P("seg", None, "patch"),
        check_vma=False,
    )
```

profile of v0, /device:TPU:17, one launch (start us, length us, event | category | flops | bytes accessed | tf_op | source)
XLA Modules:
  0.0 440.3 jit_solution(801477270826677213)
XLA Ops:
  0.8 3.8 collective-permute-start
  10.5 3.1 collective-permute-start.2
  16.5 357.9 %while.16 = (s32[]{:T(128)}, bf16[32,32,4096]{2,1,0:T(8,128)(2,1)}, bf16[32,32,4096]{2,1,0:T(8,128)(2,1)}, bf16[32,32,4096]{2,1,0:T(8,128)(2,1)}, bf16[32,32,409...) while((s32[]{:T(128)}, bf16[32,32,4096]{2,1,0:T(8,128)(2,1)}, ...), condition=%wide.region_1.2_spmd, body=%wide.region_0.1_spmd.sunk | while | flops 4196423 | bytes 5564395 | solution.py:93
  18.6 9.0 %fusion.45 = (bf16[32,32,4096]{2,1,0:T(8,128)(2,1)}, bf16[32,32,4096]{2,1,0:T(8,128)(2,1)}, bf16[32,32,4096]{2,1,0:T(8,128)(2,1)}, bf16[32,32,4096]{2,1,0:T(8,128)(2,1)}) fusion(bf16[32,32,4096]{2,1,0:T(8,128)(2,1)} %get-tuple-element.248, s32[]{:T(128)S(6)} %copy.16, f32[4096]{0:T(1024)S(1)} %bitcast.161, f32[4096]{0:T(1024)S(1)} %bitcast.162, ...), kind=kLoop, calls=%fused_computation.13.clone.1 | loop fusion | flops 4194304 | bytes 2195844 | tf_op jit(solution)/shard_map/while/body/jit(dynamic_update_index_in_dim)/dynamic_update_slice | solution.py:93
  29.8 9.0 %fusion.45 = (bf16[32,32,4096]{2,1,0:T(8,128)(2,1)}, bf16[32,32,4096]{2,1,0:T(8,128)(2,1)}, bf16[32,32,4096]{2,1,0:T(8,128)(2,1)}, bf16[32,32,4096]{2,1,0:T(8,128)(2,1)}) fusion(bf16[32,32,4096]{2,1,0:T(8,128)(2,1)} %get-tuple-element.248, s32[]{:T(128)S(6)} %copy.16, f32[4096]{0:T(1024)S(1)} %bitcast.161, f32[4096]{0:T(1024)S(1)} %bitcast.162, ...), kind=kLoop, calls=%fused_computation.13.clone.1 | loop fusion | flops 4194304 | bytes 2195844 | tf_op jit(solution)/shard_map/while/body/jit(dynamic_update_index_in_dim)/dynamic_update_slice | solution.py:93
  41.0 9.0 %fusion.45 = (bf16[32,32,4096]{2,1,0:T(8,128)(2,1)}, bf16[32,32,4096]{2,1,0:T(8,128)(2,1)}, bf16[32,32,4096]{2,1,0:T(8,128)(2,1)}, bf16[32,32,4096]{2,1,0:T(8,128)(2,1)}) fusion(bf16[32,32,4096]{2,1,0:T(8,128)(2,1)} %get-tuple-element.248, s32[]{:T(128)S(6)} %copy.16, f32[4096]{0:T(1024)S(1)} %bitcast.161, f32[4096]{0:T(1024)S(1)} %bitcast.162, ...), kind=kLoop, calls=%fused_computation.13.clone.1 | loop fusion | flops 4194304 | bytes 2195844 | tf_op jit(solution)/shard_map/while/body/jit(dynamic_update_index_in_dim)/dynamic_update_slice | solution.py:93
  52.2 9.0 %fusion.45 = (bf16[32,32,4096]{2,1,0:T(8,128)(2,1)}, bf16[32,32,4096]{2,1,0:T(8,128)(2,1)}, bf16[32,32,4096]{2,1,0:T(8,128)(2,1)}, bf16[32,32,4096]{2,1,0:T(8,128)(2,1)}) fusion(bf16[32,32,4096]{2,1,0:T(8,128)(2,1)} %get-tuple-element.248, s32[]{:T(128)S(6)} %copy.16, f32[4096]{0:T(1024)S(1)} %bitcast.161, f32[4096]{0:T(1024)S(1)} %bitcast.162, ...), kind=kLoop, calls=%fused_computation.13.clone.1 | loop fusion | flops 4194304 | bytes 2195844 | tf_op jit(solution)/shard_map/while/body/jit(dynamic_update_index_in_dim)/dynamic_update_slice | solution.py:93
  63.3 9.1 %fusion.45 = (bf16[32,32,4096]{2,1,0:T(8,128)(2,1)}, bf16[32,32,4096]{2,1,0:T(8,128)(2,1)}, bf16[32,32,4096]{2,1,0:T(8,128)(2,1)}, bf16[32,32,4096]{2,1,0:T(8,128)(2,1)}) fusion(bf16[32,32,4096]{2,1,0:T(8,128)(2,1)} %get-tuple-element.248, s32[]{:T(128)S(6)} %copy.16, f32[4096]{0:T(1024)S(1)} %bitcast.161, f32[4096]{0:T(1024)S(1)} %bitcast.162, ...), kind=kLoop, calls=%fused_computation.13.clone.1 | loop fusion | flops 4194304 | bytes 2195844 | tf_op jit(solution)/shard_map/while/body/jit(dynamic_update_index_in_dim)/dynamic_update_slice | solution.py:93
  74.5 9.1 %fusion.45 = (bf16[32,32,4096]{2,1,0:T(8,128)(2,1)}, bf16[32,32,4096]{2,1,0:T(8,128)(2,1)}, bf16[32,32,4096]{2,1,0:T(8,128)(2,1)}, bf16[32,32,4096]{2,1,0:T(8,128)(2,1)}) fusion(bf16[32,32,4096]{2,1,0:T(8,128)(2,1)} %get-tuple-element.248, s32[]{:T(128)S(6)} %copy.16, f32[4096]{0:T(1024)S(1)} %bitcast.161, f32[4096]{0:T(1024)S(1)} %bitcast.162, ...), kind=kLoop, calls=%fused_computation.13.clone.1 | loop fusion | flops 4194304 | bytes 2195844 | tf_op jit(solution)/shard_map/while/body/jit(dynamic_update_index_in_dim)/dynamic_update_slice | solution.py:93
  85.7 9.1 %fusion.45 = (bf16[32,32,4096]{2,1,0:T(8,128)(2,1)}, bf16[32,32,4096]{2,1,0:T(8,128)(2,1)}, bf16[32,32,4096]{2,1,0:T(8,128)(2,1)}, bf16[32,32,4096]{2,1,0:T(8,128)(2,1)}) fusion(bf16[32,32,4096]{2,1,0:T(8,128)(2,1)} %get-tuple-element.248, s32[]{:T(128)S(6)} %copy.16, f32[4096]{0:T(1024)S(1)} %bitcast.161, f32[4096]{0:T(1024)S(1)} %bitcast.162, ...), kind=kLoop, calls=%fused_computation.13.clone.1 | loop fusion | flops 4194304 | bytes 2195844 | tf_op jit(solution)/shard_map/while/body/jit(dynamic_update_index_in_dim)/dynamic_update_slice | solution.py:93
  97.0 9.1 %fusion.45 = (bf16[32,32,4096]{2,1,0:T(8,128)(2,1)}, bf16[32,32,4096]{2,1,0:T(8,128)(2,1)}, bf16[32,32,4096]{2,1,0:T(8,128)(2,1)}, bf16[32,32,4096]{2,1,0:T(8,128)(2,1)}) fusion(bf16[32,32,4096]{2,1,0:T(8,128)(2,1)} %get-tuple-element.248, s32[]{:T(128)S(6)} %copy.16, f32[4096]{0:T(1024)S(1)} %bitcast.161, f32[4096]{0:T(1024)S(1)} %bitcast.162, ...), kind=kLoop, calls=%fused_computation.13.clone.1 | loop fusion | flops 4194304 | bytes 2195844 | tf_op jit(solution)/shard_map/while/body/jit(dynamic_update_index_in_dim)/dynamic_update_slice | solution.py:93
  108.2 9.0 %fusion.45 = (bf16[32,32,4096]{2,1,0:T(8,128)(2,1)}, bf16[32,32,4096]{2,1,0:T(8,128)(2,1)}, bf16[32,32,4096]{2,1,0:T(8,128)(2,1)}, bf16[32,32,4096]{2,1,0:T(8,128)(2,1)}) fusion(bf16[32,32,4096]{2,1,0:T(8,128)(2,1)} %get-tuple-element.248, s32[]{:T(128)S(6)} %copy.16, f32[4096]{0:T(1024)S(1)} %bitcast.161, f32[4096]{0:T(1024)S(1)} %bitcast.162, ...), kind=kLoop, calls=%fused_computation.13.clone.1 | loop fusion | flops 4194304 | bytes 2195844 | tf_op jit(solution)/shard_map/while/body/jit(dynamic_update_index_in_dim)/dynamic_update_slice | solution.py:93
  119.3 9.0 %fusion.45 = (bf16[32,32,4096]{2,1,0:T(8,128)(2,1)}, bf16[32,32,4096]{2,1,0:T(8,128)(2,1)}, bf16[32,32,4096]{2,1,0:T(8,128)(2,1)}, bf16[32,32,4096]{2,1,0:T(8,128)(2,1)}) fusion(bf16[32,32,4096]{2,1,0:T(8,128)(2,1)} %get-tuple-element.248, s32[]{:T(128)S(6)} %copy.16, f32[4096]{0:T(1024)S(1)} %bitcast.161, f32[4096]{0:T(1024)S(1)} %bitcast.162, ...), kind=kLoop, calls=%fused_computation.13.clone.1 | loop fusion | flops 4194304 | bytes 2195844 | tf_op jit(solution)/shard_map/while/body/jit(dynamic_update_index_in_dim)/dynamic_update_slice | solution.py:93
  130.5 9.0 %fusion.45 = (bf16[32,32,4096]{2,1,0:T(8,128)(2,1)}, bf16[32,32,4096]{2,1,0:T(8,128)(2,1)}, bf16[32,32,4096]{2,1,0:T(8,128)(2,1)}, bf16[32,32,4096]{2,1,0:T(8,128)(2,1)}) fusion(bf16[32,32,4096]{2,1,0:T(8,128)(2,1)} %get-tuple-element.248, s32[]{:T(128)S(6)} %copy.16, f32[4096]{0:T(1024)S(1)} %bitcast.161, f32[4096]{0:T(1024)S(1)} %bitcast.162, ...), kind=kLoop, calls=%fused_computation.13.clone.1 | loop fusion | flops 4194304 | bytes 2195844 | tf_op jit(solution)/shard_map/while/body/jit(dynamic_update_index_in_dim)/dynamic_update_slice | solution.py:93
  141.7 9.0 %fusion.45 = (bf16[32,32,4096]{2,1,0:T(8,128)(2,1)}, bf16[32,32,4096]{2,1,0:T(8,128)(2,1)}, bf16[32,32,4096]{2,1,0:T(8,128)(2,1)}, bf16[32,32,4096]{2,1,0:T(8,128)(2,1)}) fusion(bf16[32,32,4096]{2,1,0:T(8,128)(2,1)} %get-tuple-element.248, s32[]{:T(128)S(6)} %copy.16, f32[4096]{0:T(1024)S(1)} %bitcast.161, f32[4096]{0:T(1024)S(1)} %bitcast.162, ...), kind=kLoop, calls=%fused_computation.13.clone.1 | loop fusion | flops 4194304 | bytes 2195844 | tf_op jit(solution)/shard_map/while/body/jit(dynamic_update_index_in_dim)/dynamic_update_slice | solution.py:93
  152.9 9.0 %fusion.45 = (bf16[32,32,4096]{2,1,0:T(8,128)(2,1)}, bf16[32,32,4096]{2,1,0:T(8,128)(2,1)}, bf16[32,32,4096]{2,1,0:T(8,128)(2,1)}, bf16[32,32,4096]{2,1,0:T(8,128)(2,1)}) fusion(bf16[32,32,4096]{2,1,0:T(8,128)(2,1)} %get-tuple-element.248, s32[]{:T(128)S(6)} %copy.16, f32[4096]{0:T(1024)S(1)} %bitcast.161, f32[4096]{0:T(1024)S(1)} %bitcast.162, ...), kind=kLoop, calls=%fused_computation.13.clone.1 | loop fusion | flops 4194304 | bytes 2195844 | tf_op jit(solution)/shard_map/while/body/jit(dynamic_update_index_in_dim)/dynamic_update_slice | solution.py:93
  164.1 9.0 %fusion.45 = (bf16[32,32,4096]{2,1,0:T(8,128)(2,1)}, bf16[32,32,4096]{2,1,0:T(8,128)(2,1)}, bf16[32,32,4096]{2,1,0:T(8,128)(2,1)}, bf16[32,32,4096]{2,1,0:T(8,128)(2,1)}) fusion(bf16[32,32,4096]{2,1,0:T(8,128)(2,1)} %get-tuple-element.248, s32[]{:T(128)S(6)} %copy.16, f32[4096]{0:T(1024)S(1)} %bitcast.161, f32[4096]{0:T(1024)S(1)} %bitcast.162, ...), kind=kLoop, calls=%fused_computation.13.clone.1 | loop fusion | flops 4194304 | bytes 2195844 | tf_op jit(solution)/shard_map/while/body/jit(dynamic_update_index_in_dim)/dynamic_update_slice | solution.py:93
  175.2 9.0 %fusion.45 = (bf16[32,32,4096]{2,1,0:T(8,128)(2,1)}, bf16[32,32,4096]{2,1,0:T(8,128)(2,1)}, bf16[32,32,4096]{2,1,0:T(8,128)(2,1)}, bf16[32,32,4096]{2,1,0:T(8,128)(2,1)}) fusion(bf16[32,32,4096]{2,1,0:T(8,128)(2,1)} %get-tuple-element.248, s32[]{:T(128)S(6)} %copy.16, f32[4096]{0:T(1024)S(1)} %bitcast.161, f32[4096]{0:T(1024)S(1)} %bitcast.162, ...), kind=kLoop, calls=%fused_computation.13.clone.1 | loop fusion | flops 4194304 | bytes 2195844 | tf_op jit(solution)/shard_map/while/body/jit(dynamic_update_index_in_dim)/dynamic_update_slice | solution.py:93
  186.4 9.1 %fusion.45 = (bf16[32,32,4096]{2,1,0:T(8,128)(2,1)}, bf16[32,32,4096]{2,1,0:T(8,128)(2,1)}, bf16[32,32,4096]{2,1,0:T(8,128)(2,1)}, bf16[32,32,4096]{2,1,0:T(8,128)(2,1)}) fusion(bf16[32,32,4096]{2,1,0:T(8,128)(2,1)} %get-tuple-element.248, s32[]{:T(128)S(6)} %copy.16, f32[4096]{0:T(1024)S(1)} %bitcast.161, f32[4096]{0:T(1024)S(1)} %bitcast.162, ...), kind=kLoop, calls=%fused_computation.13.clone.1 | loop fusion | flops 4194304 | bytes 2195844 | tf_op jit(solution)/shard_map/while/body/jit(dynamic_update_index_in_dim)/dynamic_update_slice | solution.py:93
  197.6 9.0 %fusion.45 = (bf16[32,32,4096]{2,1,0:T(8,128)(2,1)}, bf16[32,32,4096]{2,1,0:T(8,128)(2,1)}, bf16[32,32,4096]{2,1,0:T(8,128)(2,1)}, bf16[32,32,4096]{2,1,0:T(8,128)(2,1)}) fusion(bf16[32,32,4096]{2,1,0:T(8,128)(2,1)} %get-tuple-element.248, s32[]{:T(128)S(6)} %copy.16, f32[4096]{0:T(1024)S(1)} %bitcast.161, f32[4096]{0:T(1024)S(1)} %bitcast.162, ...), kind=kLoop, calls=%fused_computation.13.clone.1 | loop fusion | flops 4194304 | bytes 2195844 | tf_op jit(solution)/shard_map/while/body/jit(dynamic_update_index_in_dim)/dynamic_update_slice | solution.py:93
  208.8 9.0 %fusion.45 = (bf16[32,32,4096]{2,1,0:T(8,128)(2,1)}, bf16[32,32,4096]{2,1,0:T(8,128)(2,1)}, bf16[32,32,4096]{2,1,0:T(8,128)(2,1)}, bf16[32,32,4096]{2,1,0:T(8,128)(2,1)}) fusion(bf16[32,32,4096]{2,1,0:T(8,128)(2,1)} %get-tuple-element.248, s32[]{:T(128)S(6)} %copy.16, f32[4096]{0:T(1024)S(1)} %bitcast.161, f32[4096]{0:T(1024)S(1)} %bitcast.162, ...), kind=kLoop, calls=%fused_computation.13.clone.1 | loop fusion | flops 4194304 | bytes 2195844 | tf_op jit(solution)/shard_map/while/body/jit(dynamic_update_index_in_dim)/dynamic_update_slice | solution.py:93
  220.0 9.0 %fusion.45 = (bf16[32,32,4096]{2,1,0:T(8,128)(2,1)}, bf16[32,32,4096]{2,1,0:T(8,128)(2,1)}, bf16[32,32,4096]{2,1,0:T(8,128)(2,1)}, bf16[32,32,4096]{2,1,0:T(8,128)(2,1)}) fusion(bf16[32,32,4096]{2,1,0:T(8,128)(2,1)} %get-tuple-element.248, s32[]{:T(128)S(6)} %copy.16, f32[4096]{0:T(1024)S(1)} %bitcast.161, f32[4096]{0:T(1024)S(1)} %bitcast.162, ...), kind=kLoop, calls=%fused_computation.13.clone.1 | loop fusion | flops 4194304 | bytes 2195844 | tf_op jit(solution)/shard_map/while/body/jit(dynamic_update_index_in_dim)/dynamic_update_slice | solution.py:93
  231.2 9.0 %fusion.45 = (bf16[32,32,4096]{2,1,0:T(8,128)(2,1)}, bf16[32,32,4096]{2,1,0:T(8,128)(2,1)}, bf16[32,32,4096]{2,1,0:T(8,128)(2,1)}, bf16[32,32,4096]{2,1,0:T(8,128)(2,1)}) fusion(bf16[32,32,4096]{2,1,0:T(8,128)(2,1)} %get-tuple-element.248, s32[]{:T(128)S(6)} %copy.16, f32[4096]{0:T(1024)S(1)} %bitcast.161, f32[4096]{0:T(1024)S(1)} %bitcast.162, ...), kind=kLoop, calls=%fused_computation.13.clone.1 | loop fusion | flops 4194304 | bytes 2195844 | tf_op jit(solution)/shard_map/while/body/jit(dynamic_update_index_in_dim)/dynamic_update_slice | solution.py:93
  242.4 9.1 %fusion.45 = (bf16[32,32,4096]{2,1,0:T(8,128)(2,1)}, bf16[32,32,4096]{2,1,0:T(8,128)(2,1)}, bf16[32,32,4096]{2,1,0:T(8,128)(2,1)}, bf16[32,32,4096]{2,1,0:T(8,128)(2,1)}) fusion(bf16[32,32,4096]{2,1,0:T(8,128)(2,1)} %get-tuple-element.248, s32[]{:T(128)S(6)} %copy.16, f32[4096]{0:T(1024)S(1)} %bitcast.161, f32[4096]{0:T(1024)S(1)} %bitcast.162, ...), kind=kLoop, calls=%fused_computation.13.clone.1 | loop fusion | flops 4194304 | bytes 2195844 | tf_op jit(solution)/shard_map/while/body/jit(dynamic_update_index_in_dim)/dynamic_update_slice | solution.py:93
  253.6 9.0 %fusion.45 = (bf16[32,32,4096]{2,1,0:T(8,128)(2,1)}, bf16[32,32,4096]{2,1,0:T(8,128)(2,1)}, bf16[32,32,4096]{2,1,0:T(8,128)(2,1)}, bf16[32,32,4096]{2,1,0:T(8,128)(2,1)}) fusion(bf16[32,32,4096]{2,1,0:T(8,128)(2,1)} %get-tuple-element.248, s32[]{:T(128)S(6)} %copy.16, f32[4096]{0:T(1024)S(1)} %bitcast.161, f32[4096]{0:T(1024)S(1)} %bitcast.162, ...), kind=kLoop, calls=%fused_computation.13.clone.1 | loop fusion | flops 4194304 | bytes 2195844 | tf_op jit(solution)/shard_map/while/body/jit(dynamic_update_index_in_dim)/dynamic_update_slice | solution.py:93
  264.7 9.0 %fusion.45 = (bf16[32,32,4096]{2,1,0:T(8,128)(2,1)}, bf16[32,32,4096]{2,1,0:T(8,128)(2,1)}, bf16[32,32,4096]{2,1,0:T(8,128)(2,1)}, bf16[32,32,4096]{2,1,0:T(8,128)(2,1)}) fusion(bf16[32,32,4096]{2,1,0:T(8,128)(2,1)} %get-tuple-element.248, s32[]{:T(128)S(6)} %copy.16, f32[4096]{0:T(1024)S(1)} %bitcast.161, f32[4096]{0:T(1024)S(1)} %bitcast.162, ...), kind=kLoop, calls=%fused_computation.13.clone.1 | loop fusion | flops 4194304 | bytes 2195844 | tf_op jit(solution)/shard_map/while/body/jit(dynamic_update_index_in_dim)/dynamic_update_slice | solution.py:93
  275.9 9.1 %fusion.45 = (bf16[32,32,4096]{2,1,0:T(8,128)(2,1)}, bf16[32,32,4096]{2,1,0:T(8,128)(2,1)}, bf16[32,32,4096]{2,1,0:T(8,128)(2,1)}, bf16[32,32,4096]{2,1,0:T(8,128)(2,1)}) fusion(bf16[32,32,4096]{2,1,0:T(8,128)(2,1)} %get-tuple-element.248, s32[]{:T(128)S(6)} %copy.16, f32[4096]{0:T(1024)S(1)} %bitcast.161, f32[4096]{0:T(1024)S(1)} %bitcast.162, ...), kind=kLoop, calls=%fused_computation.13.clone.1 | loop fusion | flops 4194304 | bytes 2195844 | tf_op jit(solution)/shard_map/while/body/jit(dynamic_update_index_in_dim)/dynamic_update_slice | solution.py:93
  287.1 9.0 %fusion.45 = (bf16[32,32,4096]{2,1,0:T(8,128)(2,1)}, bf16[32,32,4096]{2,1,0:T(8,128)(2,1)}, bf16[32,32,4096]{2,1,0:T(8,128)(2,1)}, bf16[32,32,4096]{2,1,0:T(8,128)(2,1)}) fusion(bf16[32,32,4096]{2,1,0:T(8,128)(2,1)} %get-tuple-element.248, s32[]{:T(128)S(6)} %copy.16, f32[4096]{0:T(1024)S(1)} %bitcast.161, f32[4096]{0:T(1024)S(1)} %bitcast.162, ...), kind=kLoop, calls=%fused_computation.13.clone.1 | loop fusion | flops 4194304 | bytes 2195844 | tf_op jit(solution)/shard_map/while/body/jit(dynamic_update_index_in_dim)/dynamic_update_slice | solution.py:93
  298.3 9.0 %fusion.45 = (bf16[32,32,4096]{2,1,0:T(8,128)(2,1)}, bf16[32,32,4096]{2,1,0:T(8,128)(2,1)}, bf16[32,32,4096]{2,1,0:T(8,128)(2,1)}, bf16[32,32,4096]{2,1,0:T(8,128)(2,1)}) fusion(bf16[32,32,4096]{2,1,0:T(8,128)(2,1)} %get-tuple-element.248, s32[]{:T(128)S(6)} %copy.16, f32[4096]{0:T(1024)S(1)} %bitcast.161, f32[4096]{0:T(1024)S(1)} %bitcast.162, ...), kind=kLoop, calls=%fused_computation.13.clone.1 | loop fusion | flops 4194304 | bytes 2195844 | tf_op jit(solution)/shard_map/while/body/jit(dynamic_update_index_in_dim)/dynamic_update_slice | solution.py:93
  309.5 9.0 %fusion.45 = (bf16[32,32,4096]{2,1,0:T(8,128)(2,1)}, bf16[32,32,4096]{2,1,0:T(8,128)(2,1)}, bf16[32,32,4096]{2,1,0:T(8,128)(2,1)}, bf16[32,32,4096]{2,1,0:T(8,128)(2,1)}) fusion(bf16[32,32,4096]{2,1,0:T(8,128)(2,1)} %get-tuple-element.248, s32[]{:T(128)S(6)} %copy.16, f32[4096]{0:T(1024)S(1)} %bitcast.161, f32[4096]{0:T(1024)S(1)} %bitcast.162, ...), kind=kLoop, calls=%fused_computation.13.clone.1 | loop fusion | flops 4194304 | bytes 2195844 | tf_op jit(solution)/shard_map/while/body/jit(dynamic_update_index_in_dim)/dynamic_update_slice | solution.py:93
  320.7 9.0 %fusion.45 = (bf16[32,32,4096]{2,1,0:T(8,128)(2,1)}, bf16[32,32,4096]{2,1,0:T(8,128)(2,1)}, bf16[32,32,4096]{2,1,0:T(8,128)(2,1)}, bf16[32,32,4096]{2,1,0:T(8,128)(2,1)}) fusion(bf16[32,32,4096]{2,1,0:T(8,128)(2,1)} %get-tuple-element.248, s32[]{:T(128)S(6)} %copy.16, f32[4096]{0:T(1024)S(1)} %bitcast.161, f32[4096]{0:T(1024)S(1)} %bitcast.162, ...), kind=kLoop, calls=%fused_computation.13.clone.1 | loop fusion | flops 4194304 | bytes 2195844 | tf_op jit(solution)/shard_map/while/body/jit(dynamic_update_index_in_dim)/dynamic_update_slice | solution.py:93
  331.8 9.0 %fusion.45 = (bf16[32,32,4096]{2,1,0:T(8,128)(2,1)}, bf16[32,32,4096]{2,1,0:T(8,128)(2,1)}, bf16[32,32,4096]{2,1,0:T(8,128)(2,1)}, bf16[32,32,4096]{2,1,0:T(8,128)(2,1)}) fusion(bf16[32,32,4096]{2,1,0:T(8,128)(2,1)} %get-tuple-element.248, s32[]{:T(128)S(6)} %copy.16, f32[4096]{0:T(1024)S(1)} %bitcast.161, f32[4096]{0:T(1024)S(1)} %bitcast.162, ...), kind=kLoop, calls=%fused_computation.13.clone.1 | loop fusion | flops 4194304 | bytes 2195844 | tf_op jit(solution)/shard_map/while/body/jit(dynamic_update_index_in_dim)/dynamic_update_slice | solution.py:93
  343.0 9.0 %fusion.45 = (bf16[32,32,4096]{2,1,0:T(8,128)(2,1)}, bf16[32,32,4096]{2,1,0:T(8,128)(2,1)}, bf16[32,32,4096]{2,1,0:T(8,128)(2,1)}, bf16[32,32,4096]{2,1,0:T(8,128)(2,1)}) fusion(bf16[32,32,4096]{2,1,0:T(8,128)(2,1)} %get-tuple-element.248, s32[]{:T(128)S(6)} %copy.16, f32[4096]{0:T(1024)S(1)} %bitcast.161, f32[4096]{0:T(1024)S(1)} %bitcast.162, ...), kind=kLoop, calls=%fused_computation.13.clone.1 | loop fusion | flops 4194304 | bytes 2195844 | tf_op jit(solution)/shard_map/while/body/jit(dynamic_update_index_in_dim)/dynamic_update_slice | solution.py:93
  354.2 9.0 %fusion.45 = (bf16[32,32,4096]{2,1,0:T(8,128)(2,1)}, bf16[32,32,4096]{2,1,0:T(8,128)(2,1)}, bf16[32,32,4096]{2,1,0:T(8,128)(2,1)}, bf16[32,32,4096]{2,1,0:T(8,128)(2,1)}) fusion(bf16[32,32,4096]{2,1,0:T(8,128)(2,1)} %get-tuple-element.248, s32[]{:T(128)S(6)} %copy.16, f32[4096]{0:T(1024)S(1)} %bitcast.161, f32[4096]{0:T(1024)S(1)} %bitcast.162, ...), kind=kLoop, calls=%fused_computation.13.clone.1 | loop fusion | flops 4194304 | bytes 2195844 | tf_op jit(solution)/shard_map/while/body/jit(dynamic_update_index_in_dim)/dynamic_update_slice | solution.py:93
  365.4 9.0 %fusion.45 = (bf16[32,32,4096]{2,1,0:T(8,128)(2,1)}, bf16[32,32,4096]{2,1,0:T(8,128)(2,1)}, bf16[32,32,4096]{2,1,0:T(8,128)(2,1)}, bf16[32,32,4096]{2,1,0:T(8,128)(2,1)}) fusion(bf16[32,32,4096]{2,1,0:T(8,128)(2,1)} %get-tuple-element.248, s32[]{:T(128)S(6)} %copy.16, f32[4096]{0:T(1024)S(1)} %bitcast.161, f32[4096]{0:T(1024)S(1)} %bitcast.162, ...), kind=kLoop, calls=%fused_computation.13.clone.1 | loop fusion | flops 4194304 | bytes 2195844 | tf_op jit(solution)/shard_map/while/body/jit(dynamic_update_index_in_dim)/dynamic_update_slice | solution.py:93
  374.4 7.9 %all_gather.13 = bf16[32,4096]{1,0:T(8,128)(2,1)S(1)} all-gather(bf16[32,1024]{1,0:T(8,128)(2,1)S(1)} %collective-permute-done.3), channel_id=1, replica_groups=mesh['seg'=8,'patch'=4] {'patch'}, dimensions={1}, use_global_device_ids=true | all-gather | bytes 327680 | tf_op jit(solution)/shard_map/all_gather | solution.py:105
  382.3 6.0 %convolution_bitcast_fusion = f32[32,1024]{1,0:T(8,128)S(1)} fusion(bf16[1024,4096]{1,0:T(8,128)(2,1)} %bitcast.147, bf16[32,4096]{1,0:T(8,128)(2,1)S(1)} %all_gather.13), kind=kOutput, calls=%fused_computation.22 | convolution fusion | flops 268435456 | bytes 8781824 | tf_op jit(solution)/shard_map/dot_general | solution.py:51
  388.3 2.6 convolution_bitcast_fusion.1
  390.9 7.2 %all_gather.12 = bf16[32,4096]{1,0:T(8,128)(2,1)S(1)} all-gather(bf16[32,1024]{1,0:T(8,128)(2,1)S(1)} %collective-permute-done.2), channel_id=1, replica_groups=mesh['seg'=8,'patch'=4] {'patch'}, dimensions={1}, use_global_device_ids=true | all-gather | bytes 327680 | tf_op jit(solution)/shard_map/all_gather | solution.py:102
  398.2 2.6 convolution_bitcast_fusion.2
  400.8 2.6 convolution_bitcast_fusion.3
  403.5 5.1 %collective-permute-start.5 = (bf16[32,1024]{1,0:T(8,128)(2,1)S(1)}, bf16[32,1024]{1,0:T(8,128)(2,1)S(1)}, u32[]{:S(2)}, u32[]{:S(2)}) collective-permute-start(bf16[32,1024]{1,0:T(8,128)(2,1)S(1)} %get-tuple-element.125), channel_id=1, source_target_pairs={{4,0},{8,4},{12,8},{16,12},{20,16},{24,20},{28,24},{5,1},{9,5},{13... | collective-permute-start | bytes 196616 | tf_op jit(solution)/shard_map/ppermute | solution.py:32
  408.6 3.0 collective-permute-start.4
  411.8 6.9 %all_gather.15 = bf16[32,4096]{1,0:T(8,128)(2,1)S(1)} all-gather(bf16[32,1024]{1,0:T(8,128)(2,1)S(1)} %collective-permute-done.5), channel_id=1, replica_groups=mesh['seg'=8,'patch'=4] {'patch'}, dimensions={1}, use_global_device_ids=true | all-gather | bytes 327680 | tf_op jit(solution)/shard_map/all_gather | solution.py:105
  418.7 6.0 %fusion.23 = f32[32,1024]{1,0:T(8,128)S(1)} fusion(bf16[32,4096]{1,0:T(8,128)(2,1)S(1)} %all_gather.15, bf16[1024,4096]{1,0:T(8,128)(2,1)} %bitcast.148), kind=kOutput, calls=%fused_computation.82 | convolution fusion | flops 268435456 | bytes 8781824 | tf_op jit(solution)/shard_map/dot_general | solution.py:51
  424.7 2.6 fusion.22
  427.3 7.1 %all_gather.14 = bf16[32,4096]{1,0:T(8,128)(2,1)S(1)} all-gather(bf16[32,1024]{1,0:T(8,128)(2,1)S(1)} %collective-permute-done.4), channel_id=1, replica_groups=mesh['seg'=8,'patch'=4] {'patch'}, dimensions={1}, use_global_device_ids=true | all-gather | bytes 327680 | tf_op jit(solution)/shard_map/all_gather | solution.py:102
  437.0 2.6 fusion.20
  (336 shorter events, 58.1 us)
Async XLA Ops:
  0.8 14.9 %collective-permute-start = (f32[1,3,4096]{2,1,0:T(4,128)S(1)}, f32[1,3,4096]{2,1,0:T(4,128)S(1)}, u32[]{:S(2)}, u32[]{:S(2)}) collective-permute-start(f32[1,3,4096]{2,1,0:T(4,128)S(1)} %get-tuple-element.129), channel_id=1, source_target_pairs={{0,4},{4,8},{8,12},{12,16},{16,20},{20,24},{24,28},{1,5},{5,9},{9,... | collective-permute-start | bytes 147464 | tf_op jit(solution)/shard_map/ppermute | solution.py:23
  4.6 11.1 %collective-permute-start.1 = (f32[1,3,4096]{2,1,0:T(4,128)S(1)}, f32[1,3,4096]{2,1,0:T(4,128)S(1)}, u32[]{:S(2)}, u32[]{:S(2)}) collective-permute-start(f32[1,3,4096]{2,1,0:T(4,128)S(1)} %get-tuple-element.129), channel_id=1, source_target_pairs={{4,0},{8,4},{12,8},{16,12},{20,16},{24,20},{28,24},{5,1},{9,5},{13... | collective-permute-start | bytes 147464 | tf_op jit(solution)/shard_map/ppermute | solution.py:24
  8.0 366.4 %collective-permute-start.3 = (bf16[32,1024]{1,0:T(8,128)(2,1)}, bf16[32,1024]{1,0:T(8,128)(2,1)S(1)}, u32[]{:S(2)}, u32[]{:S(2)}) collective-permute-start(bf16[32,1024]{1,0:T(8,128)(2,1)} %get-tuple-element.127), channel_id=1, source_target_pairs={{4,0},{8,4},{12,8},{16,12},{20,16},{24,20},{28,24},{5,1},{9,5},{13... | collective-permute-start | bytes 196616 | tf_op jit(solution)/shard_map/ppermute | solution.py:32
  10.5 380.4 %collective-permute-start.2 = (bf16[32,1024]{1,0:T(8,128)(2,1)}, bf16[32,1024]{1,0:T(8,128)(2,1)S(1)}, u32[]{:S(2)}, u32[]{:S(2)}) collective-permute-start(bf16[32,1024]{1,0:T(8,128)(2,1)} %get-tuple-element.126), channel_id=1, source_target_pairs={{0,4},{4,8},{8,12},{12,16},{16,20},{20,24},{24,28},{1,5},{5,9},{9,... | collective-permute-start | bytes 196616 | tf_op jit(solution)/shard_map/ppermute | solution.py:32
  374.4 13.9 %copy-start = (bf16[32,32,4096]{2,1,0:T(8,128)(2,1)S(1)}, bf16[32,32,4096]{2,1,0:T(8,128)(2,1)}, u32[]{:S(2)}) copy-start(bf16[32,32,4096]{2,1,0:T(8,128)(2,1)} %get-tuple-element.62) | copy-start | bytes 25165828
  374.4 23.7 %slice-start.2 = ((s8[8388608]{0:T(1024)(128)(4,1)}), s8[4194304]{0:T(1024)(128)(4,1)S(1)}, s32[]{:S(2)}) async-start(s8[8388608]{0:T(1024)(128)(4,1)} %bitcast.141), calls=%async_computation.2 | async-start | bytes 8388608
  388.3 9.9 %slice-start.3 = ((s8[8388608]{0:T(1024)(128)(4,1)}), s8[4194304]{0:T(1024)(128)(4,1)S(1)}, s32[]{:S(2)}) async-start(s8[8388608]{0:T(1024)(128)(4,1)} %bitcast.141), calls=%async_computation.3 | async-start | bytes 8388608
  388.3 12.5 %slice-start = ((s8[8388608]{0:T(1024)(128)(4,1)}), s8[4194304]{0:T(1024)(128)(4,1)S(1)}, s32[]{:S(2)}) async-start(s8[8388608]{0:T(1024)(128)(4,1)} %bitcast.137), calls=%async_computation | async-start | bytes 8388608
  390.9 9.9 %slice-start.1 = ((s8[8388608]{0:T(1024)(128)(4,1)}), s8[4194304]{0:T(1024)(128)(4,1)S(1)}, s32[]{:S(2)}) async-start(s8[8388608]{0:T(1024)(128)(4,1)} %bitcast.137), calls=%async_computation.1 | async-start | bytes 8388608
  398.1 5.3 %copy-start.1 = (bf16[1,64,1024]{2,1,0:T(8,128)(2,1)S(1)}, bf16[1,64,1024]{2,1,0:T(8,128)(2,1)}, u32[]{:S(2)}) copy-start(bf16[1,64,1024]{2,1,0:T(8,128)(2,1)} %param.8) | copy-start | bytes 393220
  403.5 8.3 %collective-permute-start.5 = (bf16[32,1024]{1,0:T(8,128)(2,1)S(1)}, bf16[32,1024]{1,0:T(8,128)(2,1)S(1)}, u32[]{:S(2)}, u32[]{:S(2)}) collective-permute-start(bf16[32,1024]{1,0:T(8,128)(2,1)S(1)} %get-tuple-element.125), channel_id=1, source_target_pairs={{4,0},{8,4},{12,8},{16,12},{20,16},{24,20},{28,24},{5,1},{9,5},{13... | collective-permute-start | bytes 196616 | tf_op jit(solution)/shard_map/ppermute | solution.py:32
  408.6 18.7 %collective-permute-start.4 = (bf16[32,1024]{1,0:T(8,128)(2,1)S(1)}, bf16[32,1024]{1,0:T(8,128)(2,1)S(1)}, u32[]{:S(2)}, u32[]{:S(2)}) collective-permute-start(bf16[32,1024]{1,0:T(8,128)(2,1)S(1)} %get-tuple-element.124), channel_id=1, source_target_pairs={{0,4},{4,8},{8,12},{12,16},{16,20},{20,24},{24,28},{1,5},{5,9},{9,... | collective-permute-start | bytes 196616 | tf_op jit(solution)/shard_map/ppermute | solution.py:32
where the time goes:
time: 445 us; the launch traced here: 440 us
  other arithmetic  293 us (66%)
  local copies, waits for them, and re-layouts  47.8 us (11%)
  blocking collectives  29.1 us (7%)
  matrix products  27.4 us (6%)
  loops' own time  23.6 us (5%)
  starting transfers between devices  19.3 us (4%)
    dynamic_update_slice x32, other arithmetic, on_device(): lax.map(build_block, jnp.arange(target_rows // gen_rows, dtype=jnp.int32))  289 us
    another operation x1, loops' own time, on_device(): lax.map(build_block, jnp.arange(target_rows // gen_rows, dtype=jnp.int32))  23.6 us
    dynamic_slice x32, local copies, waits for them, and re-layouts, on_device(): lax.map(build_block, jnp.arange(target_rows // gen_rows, dtype=jnp.int32))  21.3 us
    dot_general x4, matrix products, couple(): lax.dot_general(sources, kernel_im, contract, preferred_element_type=jnp....  17.1 us
    all_gather x2, blocking collectives, on_device(): lax.all_gather(after_cur, 'patch', axis=1, tiled=True)  14.8 us
    all_gather x2, blocking collectives, on_device(): lax.all_gather(before_cur, 'patch', axis=1, tiled=True)  14.3 us
    ppermute x4, starting transfers between devices, from_behind(): lax.ppermute(value, axis, [(source, source + steps) for source in range(l...  13.6 us
    broadcast_in_dim x64, local copies, waits for them, and re-layouts, build_block(): lit_block = jnp.repeat(lit_block, block_size, axis=2)  12.1 us
  transfers between devices with their start and end apart: 6, of which 0 were waited for; matrix products, arithmetic and copies ran while one was open for 81% of the time, Pallas kernels for 0%

commit v1 on v0

v1 whole, which is shorter than its diff:
```python
import functools
import math

import jax
import jax.numpy as jnp
from jax import lax
from jax.experimental import pallas as pl
from jax.experimental.pallas import tpu as pltpu
from jax.sharding import PartitionSpec as P

ITERS = 2

WAVENUMBER = 40.0
RADIUS = 0.5
SOFTENING = 0.25

KAPPA = WAVENUMBER / (2.0 * math.pi)
HALF_CHORD = 2.0 * RADIUS * RADIUS * KAPPA * KAPPA
SINE = (4.442867903112522, -7.307443423342558, 3.5947880930735288, -0.7843740618048793)
COSINE = (1.4142040804693898, -6.9776420568649025, 5.7152383957142225, -1.728348664791446)

FEATURES = 32
UNROLL = 4
BF = jnp.bfloat16
F32 = jnp.float32


def leading(x):
    wide = x * 65537.0
    return wide - (wide - x)


def split3(x):
    high = leading(x)
    rest = x - high
    mid = leading(rest)
    return high, mid, rest - mid


def near_side(geo, direction):
    return (geo[0:1] if direction == 0 else 1.0 - geo[0:1]) * KAPPA


def far_side(geo, direction):
    return (1.0 - geo[0:1] if direction == 0 else geo[0:1]) * KAPPA


def pad_rows(rows):
    width = rows[0].shape[1]
    rows = rows + [jnp.zeros((FEATURES - len(rows), width), F32)]
    return jnp.concatenate(rows, 0)


def target_features(geo, direction):
    u = near_side(geo, direction)
    one = jnp.ones_like(u)
    rows = list(split3(u * u + HALF_CHORD)) + [one, one, one]
    for value in (2.0 * u, -HALF_CHORD * geo[1:2], -HALF_CHORD * geo[2:3]):
        h, m, l = split3(value)
        rows += [h, h, m, m, h, l]
    return pad_rows(rows)


def source_features(geo, direction):
    v = far_side(geo, direction)
    one = jnp.ones_like(v)
    rows = [one, one, one] + list(split3(v * v))
    for value in (v, geo[1:2], geo[2:3]):
        h, m, l = split3(value)
        rows += [h, m, h, m, l, h]
    return pad_rows(rows)


def plan_kernel(per_chunk, vis_ref, list_ref, count_ref):
    targets, sources = vis_ref.shape[2], vis_ref.shape[3]
    chunks = sources // per_chunk
    size = per_chunk * targets
    for direction in range(2):
        for chunk in range(chunks):
            row = direction * chunks + chunk

            def step(n, lit, direction=direction, chunk=chunk, row=row):
                src = n // targets
                tgt = n % targets
                flag = vis_ref[0, direction, tgt, chunk * per_chunk + src]
                place = jnp.where(flag > 0, lit, size - 1 - (n - lit))
                list_ref[row, place] = n
                return lit + flag

            count_ref[row] = lax.fori_loop(0, size, step, jnp.int32(0))


def make_plan(visibility, per_chunk):
    targets, sources = visibility.shape[2], visibility.shape[3]
    chunks = sources // per_chunk
    return pl.pallas_call(
        functools.partial(plan_kernel, per_chunk),
        out_shape=(
            jax.ShapeDtypeStruct((2 * chunks, per_chunk * targets), jnp.int32),
            jax.ShapeDtypeStruct((2 * chunks,), jnp.int32),
        ),
        in_specs=[pl.BlockSpec(memory_space=pltpu.SMEM)],
        out_specs=[pl.BlockSpec(memory_space=pltpu.SMEM)] * 2,
        name="plan",
    )(visibility)


def table_block(q):
    q = jnp.maximum(q, 1e-12)
    turns = q * lax.rsqrt(q)
    f = turns - jnp.round(turns)
    mag = lax.rsqrt(q + SOFTENING * KAPPA * KAPPA)
    z = f * f
    s = (((SINE[3] * z + SINE[2]) * z + SINE[1]) * z + SINE[0]) * f
    c = ((COSINE[3] * z + COSINE[2]) * z + COSINE[1]) * z + COSINE[0]
    real = mag - (s * s) * mag
    imag = (mag * s) * c
    return real.astype(BF), imag.astype(BF)


def build_chunk(direction, row, block, targets, list_ref, count_ref, tf_ref, sf_ref, base, k_ref):
    count = count_ref[row]
    size = list_ref.shape[1]

    def body(step, carry):
        for u in range(UNROLL):
            code = list_ref[row, jnp.minimum(step * UNROLL + u, count - 1)]
            src, tgt = code // targets, code % targets
            cols = pl.ds(pl.multiple_of(tgt * block, block), block)
            feats = sf_ref[pl.ds(pl.multiple_of(base + src * block, block), block), :]
            q = jnp.dot(feats, tf_ref[:, cols], preferred_element_type=F32)
            top = pl.multiple_of(src * (2 * block), 2 * block)
            part = 32
            for h in range(0, block, part):
                real, imag = table_block(q[h : h + part])
                k_ref[pl.ds(pl.multiple_of(top + h, part), part), cols] = real
                k_ref[pl.ds(pl.multiple_of(top + block + h, part), part), cols] = imag
        return carry

    lax.fori_loop(0, (count + UNROLL - 1) // UNROLL, body, 0)

    def clear(n, carry):
        code = list_ref[row, n]
        src, tgt = code // targets, code % targets
        cols = pl.ds(pl.multiple_of(tgt * block, block), block)
        rows = pl.ds(pl.multiple_of(src * (2 * block), 2 * block), 2 * block)
        k_ref[rows, cols] = jnp.zeros((2 * block, block), BF)
        return carry

    lax.fori_loop(count, size, clear, 0)


def build_features(direction, block, tgeo_ref, sgeo_ref, tf_ref, sf_ref):
    tf_ref[...] = target_features(tgeo_ref[...], direction).astype(BF)
    feats = source_features(sgeo_ref[...], direction)
    sf_ref[...] = feats.T.astype(BF)


def build_kernel(direction, block, per_chunk, list_ref, count_ref, tgeo_ref, sgeo_ref, k_ref, tf_ref, sf_ref):
    chunk = pl.program_id(0)
    chunks = pl.num_programs(0)
    targets = tgeo_ref.shape[1] // block

    @pl.when(chunk == 0)
    def _():
        build_features(direction, block, tgeo_ref, sgeo_ref, tf_ref, sf_ref)

    build_chunk(
        direction, direction * chunks + chunk, block, targets, list_ref, count_ref, tf_ref, sf_ref,
        chunk * (per_chunk * block), k_ref,
    )


def call_build(direction, block, per_chunk, plan, tgeo, sgeo):
    patches, rows = sgeo.shape[1], tgeo.shape[1]
    chunks = patches // (block * per_chunk)
    chunk_rows = 2 * block * per_chunk
    whole = lambda shape: pl.BlockSpec(shape, lambda c: (0, 0))
    return pl.pallas_call(
        functools.partial(build_kernel, direction, block, per_chunk),
        grid=(chunks,),
        out_shape=jax.ShapeDtypeStruct((2 * patches, rows), BF),
        in_specs=[
            pl.BlockSpec(memory_space=pltpu.SMEM),
            pl.BlockSpec(memory_space=pltpu.SMEM),
            whole(tgeo.shape),
            whole(sgeo.shape),
        ],
        out_specs=pl.BlockSpec((chunk_rows, rows), lambda c: (c, 0)),
        scratch_shapes=[pltpu.VMEM((FEATURES, rows), BF), pltpu.VMEM((patches, FEATURES), BF)],
        compiler_params=pltpu.CompilerParams(dimension_semantics=("arbitrary",)),
        name=f"build{direction}",
    )(*plan, tgeo, sgeo)


def load_sources(where_ref, piece_refs, before_ref, after_ref, left_ref, scale, block):
    channels = piece_refs[0].shape[0] // 2
    half = channels // 2
    width = piece_refs[0].shape[1]
    for k, piece in enumerate(piece_refs):
        start = where_ref[k] * width
        for d, geo_ref in enumerate((before_ref, after_ref)):
            for n in range(width // block):
                cur = piece[d * channels : (d + 1) * channels, n * block : (n + 1) * block].astype(F32)
                lanes = pl.ds(pl.multiple_of(start + n * block, block), block)
                cur = cur * (geo_ref[3:4, lanes] * scale)
                high = leading(cur)
                low = (cur - high).astype(BF)
                high = high.astype(BF)
                a = jnp.concatenate([high, low], 0)
                b = jnp.concatenate([high[half:], -high[:half], low[half:], -low[:half]], 0)
                top = pl.multiple_of(2 * (start + n * block), 2 * block)
                left_ref[d, :, pl.ds(top, block)] = a
                left_ref[d, :, pl.ds(pl.multiple_of(top + block, block), block)] = b


def finish(acc_ref, inc_ref, prev_ref, coef_ref, out_ref):
    channels = inc_ref.shape[0] // 2
    half = channels // 2
    prev = prev_ref[...].astype(F32)
    for d in range(2):
        total = acc_ref[d, :channels] + acc_ref[d, channels:]
        other = prev[(1 - d) * channels : (2 - d) * channels]
        cre = coef_ref[d, :half]
        cim = coef_ref[d, half:]
        mirrored = jnp.concatenate(
            [cre * other[:half] - cim * other[half:], cre * other[half:] + cim * other[:half]], 0
        )
        rows = slice(d * channels, (d + 1) * channels)
        out_ref[rows] = (inc_ref[rows].astype(F32) + total + mirrored).astype(BF)


def accumulate(acc_ref, left_ref, d, chunk, k_ref):
    rows = k_ref.shape[0]
    cols = pl.ds(pl.multiple_of(chunk * rows, rows), rows)
    part = jnp.dot(left_ref[d, :, cols], k_ref[...], preferred_element_type=F32)

    @pl.when(chunk == 0)
    def _():
        acc_ref[d] = part

    @pl.when(chunk > 0)
    def _():
        acc_ref[d] += part


def build_sweep_kernel(
    block, per_chunk, pieces, scale,
    list_ref, count_ref, where_ref, tgeo_ref, before_ref, after_ref, inc_ref, coef_ref, k0_ref, *rest
):
    piece_refs = rest[:pieces]
    k_ref, out_ref, tf_ref, sf_ref, left_ref, acc_ref = rest[pieces:]
    chunk = pl.program_id(0)
    chunks = pl.num_programs(0)
    targets = tgeo_ref.shape[1] // block

    @pl.when(chunk == 0)
    def _():
        build_features(1, block, tgeo_ref, after_ref, tf_ref, sf_ref)
        load_sources(where_ref, piece_refs, before_ref, after_ref, left_ref, scale, block)

    build_chunk(
        1, chunks + chunk, block, targets, list_ref, count_ref, tf_ref, sf_ref,
        chunk * (per_chunk * block), k_ref,
    )
    accumulate(acc_ref, left_ref, 0, chunk, k0_ref)
    accumulate(acc_ref, left_ref, 1, chunk, k_ref)

    @pl.when(chunk == chunks - 1)
    def _():
        finish(acc_ref, inc_ref, inc_ref, coef_ref, out_ref)


def call_build_sweep(block, per_chunk, scale, plan, where, tgeo, before, after, inc, coef, k0, pieces):
    patches, rows = before.shape[1], tgeo.shape[1]
    chunks = patches // (block * per_chunk)
    chunk_rows = 2 * block * per_chunk
    whole = lambda x: pl.BlockSpec(x.shape, lambda c: (0,) * x.ndim)
    smem = pl.BlockSpec(memory_space=pltpu.SMEM)
    channels = inc.shape[0]
    return pl.pallas_call(
        functools.partial(build_sweep_kernel, block, per_chunk, len(pieces), scale),
        grid=(chunks,),
        out_shape=(
            jax.ShapeDtypeStruct((2 * patches, rows), BF),
            jax.ShapeDtypeStruct((channels, rows), BF),
        ),
        in_specs=[smem, smem, smem, whole(tgeo), whole(before), whole(after), whole(inc), whole(coef),
                  pl.BlockSpec((chunk_rows, rows), lambda c: (c, 0))] + [whole(p) for p in pieces],
        out_specs=(
            pl.BlockSpec((chunk_rows, rows), lambda c: (c, 0)),
            pl.BlockSpec((channels, rows), lambda c: (0, 0)),
        ),
        scratch_shapes=[
            pltpu.VMEM((FEATURES, rows), BF),
            pltpu.VMEM((patches, FEATURES), BF),
            pltpu.VMEM((2, channels, 2 * patches), BF),
            pltpu.VMEM((2, channels, rows), F32),
        ],
        compiler_params=pltpu.CompilerParams(dimension_semantics=("arbitrary",)),
        name="build_sweep",
    )(*plan, where, tgeo, before, after, inc, coef, k0, *pieces)


def sweep_kernel(
    block, pieces, scale, where_ref, before_ref, after_ref, inc_ref, prev_ref, coef_ref, k0_ref, k1_ref, *rest
):
    piece_refs = rest[:pieces]
    out_ref, left_ref, acc_ref = rest[pieces:]
    chunk = pl.program_id(0)

    @pl.when(chunk == 0)
    def _():
        load_sources(where_ref, piece_refs, before_ref, after_ref, left_ref, scale, block)

    accumulate(acc_ref, left_ref, 0, chunk, k0_ref)
    accumulate(acc_ref, left_ref, 1, chunk, k1_ref)

    @pl.when(chunk == pl.num_programs(0) - 1)
    def _():
        finish(acc_ref, inc_ref, prev_ref, coef_ref, out_ref)


def call_sweep(block, per_chunk, scale, where, before, after, inc, prev, coef, k0, k1, pieces):
    patches, rows = before.shape[1], inc.shape[1]
    chunks = patches // (block * per_chunk)
    chunk_rows = 2 * block * per_chunk
    whole = lambda x: pl.BlockSpec(x.shape, lambda c: (0,) * x.ndim)
    smem = pl.BlockSpec(memory_space=pltpu.SMEM)
    channels = inc.shape[0]
    table = pl.BlockSpec((chunk_rows, rows), lambda c: (c, 0))
    return pl.pallas_call(
        functools.partial(sweep_kernel, block, len(pieces), scale),
        grid=(chunks,),
        out_shape=jax.ShapeDtypeStruct((channels, rows), BF),
        in_specs=[smem, whole(before), whole(after), whole(inc), whole(prev), whole(coef), table, table]
        + [whole(p) for p in pieces],
        out_specs=pl.BlockSpec((channels, rows), lambda c: (0, 0)),
        scratch_shapes=[
            pltpu.VMEM((2, channels, 2 * patches), BF),
            pltpu.VMEM((2, channels, rows), F32),
        ],
        compiler_params=pltpu.CompilerParams(dimension_semantics=("arbitrary",)),
        name="sweep",
    )(where, before, after, inc, prev, coef, k0, k1, *pieces)


def shift(value, step):
    count = lax.axis_size("seg")
    return lax.ppermute(value, "seg", [(i, i + step) for i in range(count) if 0 <= i + step < count])


def gather_patches(value):
    count = lax.axis_size("patch")
    me = lax.axis_index("patch")
    pieces, where = [value], [me]
    if count <= 4:
        for k in range(1, count):
            pieces.append(lax.ppermute(value, "patch", [(i, i ^ k) for i in range(count)]))
            where.append(me ^ k)
        return pieces, jnp.stack(where).astype(jnp.int32)
    return [lax.all_gather(value, "patch", axis=1, tiled=True)], jnp.zeros((1,), jnp.int32)


def on_device(incident, wall_axial, wall_angle, wall_area, visibility, end_reflection):
    channels = incident.shape[1]
    rows = incident.shape[2]
    patches = wall_axial.shape[1]
    block = patches // visibility.shape[3]
    half = channels // 2
    per_chunk = min(8, patches // block)
    seg_index = lax.axis_index("seg")
    seg_count = lax.axis_size("seg")
    patch_index = lax.axis_index("patch")
    scale = KAPPA / math.sqrt(patches)
    inc = incident[0]
    angle = wall_angle[0]
    geo = jnp.stack([wall_axial[0], jnp.cos(angle), jnp.sin(angle), wall_area[0]])
    before, after = shift(geo, 1), shift(geo, -1)
    tgeo = lax.dynamic_slice_in_dim(geo, patch_index * rows, rows, 1)
    ends = jnp.stack([seg_index == 0, seg_index == seg_count - 1])
    coef = jnp.where(ends[:, None], end_reflection, 0.0)[:, :, None]
    plan = make_plan(visibility, per_chunk)

    def exchange(state):
        moved = jnp.concatenate([shift(state[:half], 1), shift(state[half:], -1)], 0)
        return gather_patches(moved)

    k0 = call_build(0, block, per_chunk, plan, tgeo, before)
    pieces, where = exchange(inc)
    k1, state = call_build_sweep(
        block, per_chunk, scale, plan, where, tgeo, before, after, inc, coef, k0, pieces
    )
    for sweep in range(1, ITERS):
        pieces, where = exchange(state)
        state = call_sweep(block, per_chunk, scale, where, before, after, inc, state, coef, k0, k1, pieces)
    return state[None]


def solution(mesh):
    return jax.shard_map(
        on_device,
        mesh=mesh,
        in_specs=(
            P("seg", None, "patch"),
            P("seg", None),
            P("seg", None),
            P("seg", None),
            P("seg", None, "patch", None),
            P(),
        ),
        out_specs=P("seg", None, "patch"),
        check_vma=False,
    )
```

time: 445 us -> 129 us (0.29); the launches traced: 440 us -> 129 us
  other arithmetic: 293 us -> 2.25 us
  Pallas kernels: 0 us -> 86.7 us
  local copies, waits for them, and re-layouts: 47.8 us -> 6.3 us
  blocking collectives: 29.1 us -> 0 us
  matrix products: 27.4 us -> 0 us
  loops' own time: 23.6 us -> 0 us
  waiting for transfers between devices: 0.03 us -> 9.84 us
    dynamic_update_slice x32 -> x0, other arithmetic: 289 us -> none  [on_device(): lax.map(build_block, jnp.arange(target_rows // gen_rows, dtype=jnp.int32))]
    pallas_call x0 -> x4, Pallas kernels: none -> 86.7 us  [the longest x1 34.6 us: call_build_sweep(): pl.pallas_call(functools.partial(build_sweep_kernel, block, per_chunk, le...]
    all_gather x4 -> x0, blocking collectives: 29.1 us -> none  [the longest x2 14.8 us: on_device(): lax.all_gather(after_cur, 'patch', axis=1, tiled=True)]
    dot_general x8 -> x0, matrix products: 27.4 us -> none  [the longest x4 17.1 us: couple(): lax.dot_general(sources, kernel_im, contract, preferred_element_type=jnp....]
    another operation x1 -> x0, loops' own time: 23.6 us -> none  [on_device(): lax.map(build_block, jnp.arange(target_rows // gen_rows, dtype=jnp.int32))]
    dynamic_slice x65 -> x1, local copies, waits for them, and re-layouts: 23.8 us -> 0.6 us  [on_device(): tgeo = lax.dynamic_slice_in_dim(geo, patch_index * rows, rows, 1)]
    broadcast_in_dim x65 -> x1, local copies, waits for them, and re-layouts: 12.9 us -> 0.71 us  [on_device(): coef = jnp.where(ends[:, None], end_reflection, 0.0)[:, :, None]]
    ppermute x6 -> x12, waiting for transfers between devices: 0.03 us -> 9.84 us  [the longest x6 5.72 us: gather_patches(): lax.ppermute(value, 'patch', [(i, i ^ k) for i in range(count)])]
  transfers between devices with their start and end apart: 6 -> 12, of which waited for: 0 -> 4; matrix products, arithmetic and copies ran while one was open for 81% -> 3% of each run, Pallas kernels for 0% -> 29%
where the time goes in v1:
time: 129 us
  Pallas kernels  86.7 us (67%)
  starting transfers between devices  23.5 us (18%)
  waiting for transfers between devices  9.84 us (8%)
  local copies, waits for them, and re-layouts  6.3 us (5%)
  other arithmetic  2.25 us (2%)
    pallas_call x1, Pallas kernels, call_build_sweep(): pl.pallas_call(functools.partial(build_sweep_kernel, block, per_chunk, le...  34.6 us
    pallas_call x1, Pallas kernels, call_build(): pl.pallas_call(functools.partial(build_kernel, direction, block, per_chun...  25.2 us
    ppermute x6, starting transfers between devices, shift(): lax.ppermute(value, 'seg', [(i, i + step) for i in range(count) if 0 <= i...  17.8 us
    pallas_call x1, Pallas kernels, call_sweep(): pl.pallas_call(functools.partial(sweep_kernel, block, len(pieces), scale)...  14.3 us
    pallas_call x1, Pallas kernels, make_plan(): pl.pallas_call(functools.partial(plan_kernel, per_chunk), out_shape=(jax....  12.6 us
    ppermute x6, waiting for transfers between devices, gather_patches(): lax.ppermute(value, 'patch', [(i, i ^ k) for i in range(count)])  5.72 us
    ppermute x6, starting transfers between devices, gather_patches(): lax.ppermute(value, 'patch', [(i, i ^ k) for i in range(count)])  5.68 us
    ppermute x6, waiting for transfers between devices, shift(): lax.ppermute(value, 'seg', [(i, i + step) for i in range(count) if 0 <= i...  4.12 us
  transfers between devices with their start and end apart: 12, of which 4 were waited for; matrix products, arithmetic and copies ran while one was open for 3% of the time, Pallas kernels for 29%

profile of v1, /device:TPU:17, one launch (start us, length us, event | category | flops | bytes accessed | tf_op | source)
XLA Modules:
  0.0 128.8 jit_solution(6589320054365323465)
XLA Ops:
  0.0 1.2 fusion.1
  1.2 0.8 pad_maximum_fusion
  2.0 2.6 %collective-permute-start.1 = (f32[4,4096]{1,0:T(4,128)S(1)}, f32[4,4096]{1,0:T(4,128)S(1)}, u32[]{:S(2)}, u32[]{:S(2)}) collective-permute-start(f32[4,4096]{1,0:T(4,128)S(1)} %pad_maximum_fusion), channel_id=1, source_target_pairs={{4,0},{8,4},{12,8},{16,12},{20,16},{24,20},{28,24},{5,1},{9,5},{13... | collective-permute-start | bytes 196616 | tf_op jit(solution)/shard_map/ppermute | solution.py:350
  4.6 3.1 %collective-permute-start = (f32[4,4096]{1,0:T(4,128)S(1)}, f32[4,4096]{1,0:T(4,128)S(1)}, u32[]{:S(2)}, u32[]{:S(2)}) collective-permute-start(f32[4,4096]{1,0:T(4,128)S(1)} %pad_maximum_fusion), channel_id=1, source_target_pairs={{0,4},{4,8},{8,12},{12,16},{16,20},{20,24},{24,28},{1,5},{5,9},{9,... | collective-permute-start | bytes 196616 | tf_op jit(solution)/shard_map/ppermute | solution.py:350
  7.7 0.9 slice_bitcast_fusion
  8.6 1.9 %collective-permute-start.3 = (bf16[32,1024]{1,0:T(8,128)(2,1)S(1)}, bf16[32,1024]{1,0:T(8,128)(2,1)S(1)}, u32[]{:S(2)}, u32[]{:S(2)}) collective-permute-start(bf16[32,1024]{1,0:T(8,128)(2,1)S(1)} %get-tuple-element.15), channel_id=1, source_target_pairs={{4,0},{8,4},{12,8},{16,12},{20,16},{24,20},{28,24},{5,1},{9,5},{13... | collective-permute-start | bytes 196616 | tf_op jit(solution)/shard_map/ppermute | solution.py:350
  10.5 3.6 %collective-permute-start.2 = (bf16[32,1024]{1,0:T(8,128)(2,1)S(1)}, bf16[32,1024]{1,0:T(8,128)(2,1)S(1)}, u32[]{:S(2)}, u32[]{:S(2)}) collective-permute-start(bf16[32,1024]{1,0:T(8,128)(2,1)S(1)} %get-tuple-element.16), channel_id=1, source_target_pairs={{0,4},{4,8},{8,12},{12,16},{16,20},{20,24},{24,28},{1,5},{5,9},{9,... | collective-permute-start | bytes 196616 | tf_op jit(solution)/shard_map/ppermute | solution.py:350
  14.2 0.1 pad_add_fusion
  14.2 0.7 select_bitcast_fusion
  15.0 0.5 collective-permute-done.2
  15.5 0.0 collective-permute-done.3
  15.5 0.0 copy-start.1
  15.5 2.2 %collective-permute-start.6 = (bf16[64,1024]{1,0:T(8,128)(2,1)S(1)}, bf16[64,1024]{1,0:T(8,128)(2,1)S(1)}, u32[]{:S(2)}, u32[]{:S(2)}) collective-permute-start(bf16[64,1024]{1,0:T(8,128)(2,1)S(1)} %constant_dynamic-update-slice_fusion.rest_0_), channel_id=1, source_target_pairs={{0,3},{1,2},{2,1},{3,0},{4,7},{5,6},{6,5},{7,4},{8,11},{9,10},{10,... | collective-permute-start | bytes 393224 | tf_op jit(solution)/shard_map/ppermute | solution.py:359
  17.7 0.2 collective-permute-start.5
  18.0 0.3 collective-permute-start.4
  18.2 0.6 constant_dynamic-slice_fusion.tgeo_ref
  18.8 12.6 %plan.1 = (s32[8,64]{1,0:T(8,128)}, s32[8]{0:T(128)}) custom-call(s32[1,2,8,32]{3,2,1,0:T(8,128)} %vis_ref.1), custom_call_target="tpu_custom_call" | custom-call | tf_op jit(solution)/shard_map/plan/pallas_call | solution.py:96
  31.4 0.7 copy.7.coef_ref
  32.2 0.6 pad_add_fusion.1.where_ref
  32.8 0.0 collective-permute-done.sgeo_ref.before_ref
  32.8 0.6 copy-done
  33.4 25.2 %build0.1.k0_ref = bf16[8192,1024]{1,0:T(8,128)(2,1)} custom-call(s32[8,64]{1,0:T(8,128)} %get-tuple-element.9.list_ref, s32[8]{0:T(128)} %get-tuple-element.10.count_ref, f32[4,1024]{1,0:T(4,128)} %constant_dynamic-slice_fusion.tgeo_ref, f32[4,4096]{1,0:T(4,128)} %copy-done), custom_call_target="tpu_custom_call" | custom-call | tf_op jit(solution)/shard_map/build0/pallas_call | solution.py:179
  58.6 0.0 collective-permute-done.1.after_ref
  58.6 0.0 collective-permute-done.6.rest_3_
  58.6 0.0 copy-start.4
  58.6 0.0 collective-permute-done.5.rest_2_
  58.6 0.0 collective-permute-done.4.rest_1_
  58.6 0.0 copy-start.6
  58.6 0.0 copy-done.1
  58.6 0.6 copy-done.3
  59.2 0.1 copy-done.4
  59.3 0.0 copy-done.5
  59.3 0.0 copy-done.6
  59.3 34.6 %build_sweep.1 = (bf16[8192,1024]{1,0:T(8,128)(2,1)}, bf16[64,1024]{1,0:T(8,128)(2,1)}) custom-call(s32[8,64]{1,0:T(8,128)} %get-tuple-element.9.list_ref, s32[8]{0:T(128)} %get-tuple-element.10.count_ref, s32[4]{0:T(128)} %pad_add_fusion.1.where_ref, f32[4,1024]{1,0:T(4,128)} %constant_dynamic-slice_fusion.tgeo_ref, f32[4,4096]{1,0:T(4,128)} %copy-done, ...), custom_call_target="tpu_custom_call" | custom-call | tf_op jit(solution)/shard_map/build_sweep/pallas_call | solution.py:281
  94.0 0.9 fusion
  94.8 4.7 %collective-permute-start.7 = (bf16[32,1024]{1,0:T(8,128)(2,1)S(1)}, bf16[32,1024]{1,0:T(8,128)(2,1)S(1)}, u32[]{:S(2)}, u32[]{:S(2)}) collective-permute-start(bf16[32,1024]{1,0:T(8,128)(2,1)S(1)} %get-tuple-element.14), channel_id=1, source_target_pairs={{0,4},{4,8},{8,12},{12,16},{16,20},{20,24},{24,28},{1,5},{5,9},{9,... | collective-permute-start | bytes 196616 | tf_op jit(solution)/shard_map/ppermute | solution.py:350
  99.5 1.9 %collective-permute-start.8 = (bf16[32,1024]{1,0:T(8,128)(2,1)S(1)}, bf16[32,1024]{1,0:T(8,128)(2,1)S(1)}, u32[]{:S(2)}, u32[]{:S(2)}) collective-permute-start(bf16[32,1024]{1,0:T(8,128)(2,1)S(1)} %get-tuple-element.13), channel_id=1, source_target_pairs={{4,0},{8,4},{12,8},{16,12},{20,16},{24,20},{28,24},{5,1},{9,5},{13... | collective-permute-start | bytes 196616 | tf_op jit(solution)/shard_map/ppermute | solution.py:350
  101.4 0.0 collective-permute-done.7
  101.5 3.6 %collective-permute-done.8 = bf16[32,1024]{1,0:T(8,128)(2,1)S(1)} collective-permute-done((bf16[32,1024]{1,0:T(8,128)(2,1)S(1)}, bf16[32,1024]{1,0:T(8,128)(2,1)S(1)}, u32[]{:S(2)}, u32[]{:S(2)}) %collective-permute-start.8) | collective-permute-done | bytes 65568 | tf_op jit(solution)/shard_map/ppermute | solution.py:350
  105.1 2.6 %collective-permute-start.11 = (bf16[64,1024]{1,0:T(8,128)(2,1)S(1)}, bf16[64,1024]{1,0:T(8,128)(2,1)S(1)}, u32[]{:S(2)}, u32[]{:S(2)}) collective-permute-start(bf16[64,1024]{1,0:T(8,128)(2,1)S(1)} %constant_dynamic-update-slice_fusion.2.rest_0_), channel_id=1, source_target_pairs={{0,3},{1,2},{2,1},{3,0},{4,7},{5,6},{6,5},{7,4},{8,11},{9,10},{10,... | collective-permute-start | bytes 393224 | tf_op jit(solution)/shard_map/ppermute | solution.py:359
  107.7 0.0 collective-permute-start.10
  107.7 0.3 collective-permute-start.9
  108.1 3.4 %collective-permute-done.11.rest_3_ = bf16[64,1024]{1,0:T(8,128)(2,1)S(1)} collective-permute-done((bf16[64,1024]{1,0:T(8,128)(2,1)S(1)}, bf16[64,1024]{1,0:T(8,128)(2,1)S(1)}, u32[]{:S(2)}, u32[]{:S(2)}) %collective-permute-start.11) | collective-permute-done | bytes 131104 | tf_op jit(solution)/shard_map/ppermute | solution.py:359
  111.5 2.3 %collective-permute-done.10.rest_2_ = bf16[64,1024]{1,0:T(8,128)(2,1)S(1)} collective-permute-done((bf16[64,1024]{1,0:T(8,128)(2,1)S(1)}, bf16[64,1024]{1,0:T(8,128)(2,1)S(1)}, u32[]{:S(2)}, u32[]{:S(2)}) %collective-permute-start.10) | collective-permute-done | bytes 131104 | tf_op jit(solution)/shard_map/ppermute | solution.py:359
  113.8 0.0 collective-permute-done.9.rest_1_
  113.8 0.6 copy-done.8
  114.4 0.0 copy-done.9
  114.5 14.3 %sweep.1 = bf16[64,1024]{1,0:T(8,128)(2,1)} custom-call(s32[4]{0:T(128)} %pad_add_fusion.1.where_ref, f32[4,4096]{1,0:T(4,128)} %copy-done, f32[4,4096]{1,0:T(4,128)} %copy-done.3, bf16[64,1024]{1,0:T(8,128)(2,1)} %bitcast.15, bf16[64,1024]{1,0:T(8,128)(2,1)} %get-tuple-element.11.prev_ref, f32[2,32,1]{2,1,0:T(8,128)} %copy.7.coef_ref, ...), custom_call_target="tpu_custom_call" | custom-call | tf_op jit(solution)/shard_map/sweep/pallas_call | solution.py:332
  (13 shorter events, 0.0 us)
Async XLA Ops:
  2.0 56.6 %collective-permute-start.1 = (f32[4,4096]{1,0:T(4,128)S(1)}, f32[4,4096]{1,0:T(4,128)S(1)}, u32[]{:S(2)}, u32[]{:S(2)}) collective-permute-start(f32[4,4096]{1,0:T(4,128)S(1)} %pad_maximum_fusion), channel_id=1, source_target_pairs={{4,0},{8,4},{12,8},{16,12},{20,16},{24,20},{28,24},{5,1},{9,5},{13... | collective-permute-start | bytes 196616 | tf_op jit(solution)/shard_map/ppermute | solution.py:350
  4.6 28.2 %collective-permute-start = (f32[4,4096]{1,0:T(4,128)S(1)}, f32[4,4096]{1,0:T(4,128)S(1)}, u32[]{:S(2)}, u32[]{:S(2)}) collective-permute-start(f32[4,4096]{1,0:T(4,128)S(1)} %pad_maximum_fusion), channel_id=1, source_target_pairs={{0,4},{4,8},{8,12},{12,16},{16,20},{20,24},{24,28},{1,5},{5,9},{9,... | collective-permute-start | bytes 196616 | tf_op jit(solution)/shard_map/ppermute | solution.py:350
  8.6 6.9 %collective-permute-start.3 = (bf16[32,1024]{1,0:T(8,128)(2,1)S(1)}, bf16[32,1024]{1,0:T(8,128)(2,1)S(1)}, u32[]{:S(2)}, u32[]{:S(2)}) collective-permute-start(bf16[32,1024]{1,0:T(8,128)(2,1)S(1)} %get-tuple-element.15), channel_id=1, source_target_pairs={{4,0},{8,4},{12,8},{16,12},{20,16},{24,20},{28,24},{5,1},{9,5},{13... | collective-permute-start | bytes 196616 | tf_op jit(solution)/shard_map/ppermute | solution.py:350
  10.5 5.0 %collective-permute-start.2 = (bf16[32,1024]{1,0:T(8,128)(2,1)S(1)}, bf16[32,1024]{1,0:T(8,128)(2,1)S(1)}, u32[]{:S(2)}, u32[]{:S(2)}) collective-permute-start(bf16[32,1024]{1,0:T(8,128)(2,1)S(1)} %get-tuple-element.16), channel_id=1, source_target_pairs={{0,4},{4,8},{8,12},{12,16},{16,20},{20,24},{24,28},{1,5},{5,9},{9,... | collective-permute-start | bytes 196616 | tf_op jit(solution)/shard_map/ppermute | solution.py:350
  15.5 43.1 %copy-start.1 = (bf16[64,1024]{1,0:T(8,128)(2,1)}, bf16[64,1024]{1,0:T(8,128)(2,1)S(1)}, u32[]{:S(2)}) copy-start(bf16[64,1024]{1,0:T(8,128)(2,1)S(1)} %constant_dynamic-update-slice_fusion.rest_0_) | copy-start | bytes 393220
  15.5 43.1 %collective-permute-start.6 = (bf16[64,1024]{1,0:T(8,128)(2,1)S(1)}, bf16[64,1024]{1,0:T(8,128)(2,1)S(1)}, u32[]{:S(2)}, u32[]{:S(2)}) collective-permute-start(bf16[64,1024]{1,0:T(8,128)(2,1)S(1)} %constant_dynamic-update-slice_fusion.rest_0_), channel_id=1, source_target_pairs={{0,3},{1,2},{2,1},{3,0},{4,7},{5,6},{6,5},{7,4},{8,11},{9,10},{10,... | collective-permute-start | bytes 393224 | tf_op jit(solution)/shard_map/ppermute | solution.py:359
  17.7 40.8 %collective-permute-start.5 = (bf16[64,1024]{1,0:T(8,128)(2,1)S(1)}, bf16[64,1024]{1,0:T(8,128)(2,1)S(1)}, u32[]{:S(2)}, u32[]{:S(2)}) collective-permute-start(bf16[64,1024]{1,0:T(8,128)(2,1)S(1)} %constant_dynamic-update-slice_fusion.rest_0_), channel_id=1, source_target_pairs={{0,2},{1,3},{2,0},{3,1},{4,6},{5,7},{6,4},{7,5},{8,10},{9,11},{10,... | collective-permute-start | bytes 393224 | tf_op jit(solution)/shard_map/ppermute | solution.py:359
  18.0 40.6 %collective-permute-start.4 = (bf16[64,1024]{1,0:T(8,128)(2,1)S(1)}, bf16[64,1024]{1,0:T(8,128)(2,1)S(1)}, u32[]{:S(2)}, u32[]{:S(2)}) collective-permute-start(bf16[64,1024]{1,0:T(8,128)(2,1)S(1)} %constant_dynamic-update-slice_fusion.rest_0_), channel_id=1, source_target_pairs={{0,1},{1,0},{2,3},{3,2},{4,5},{5,4},{6,7},{7,6},{8,9},{9,8},{10,11... | collective-permute-start | bytes 393224 | tf_op jit(solution)/shard_map/ppermute | solution.py:359
  32.8 0.6 copy-start
  58.6 0.6 copy-start.3
  58.6 0.7 copy-start.4
  58.6 0.7 copy-start.5
  58.6 0.7 copy-start.6
  94.8 6.6 %collective-permute-start.7 = (bf16[32,1024]{1,0:T(8,128)(2,1)S(1)}, bf16[32,1024]{1,0:T(8,128)(2,1)S(1)}, u32[]{:S(2)}, u32[]{:S(2)}) collective-permute-start(bf16[32,1024]{1,0:T(8,128)(2,1)S(1)} %get-tuple-element.14), channel_id=1, source_target_pairs={{0,4},{4,8},{8,12},{12,16},{16,20},{20,24},{24,28},{1,5},{5,9},{9,... | collective-permute-start | bytes 196616 | tf_op jit(solution)/shard_map/ppermute | solution.py:350
  99.5 5.6 %collective-permute-start.8 = (bf16[32,1024]{1,0:T(8,128)(2,1)S(1)}, bf16[32,1024]{1,0:T(8,128)(2,1)S(1)}, u32[]{:S(2)}, u32[]{:S(2)}) collective-permute-start(bf16[32,1024]{1,0:T(8,128)(2,1)S(1)} %get-tuple-element.13), channel_id=1, source_target_pairs={{4,0},{8,4},{12,8},{16,12},{20,16},{24,20},{28,24},{5,1},{9,5},{13... | collective-permute-start | bytes 196616 | tf_op jit(solution)/shard_map/ppermute | solution.py:350
  105.1 8.7 %copy-start.2 = (bf16[64,1024]{1,0:T(8,128)(2,1)}, bf16[64,1024]{1,0:T(8,128)(2,1)S(1)}, u32[]{:S(2)}) copy-start(bf16[64,1024]{1,0:T(8,128)(2,1)S(1)} %constant_dynamic-update-slice_fusion.2.rest_0_) | copy-start | bytes 393220
  105.1 6.4 %collective-permute-start.11 = (bf16[64,1024]{1,0:T(8,128)(2,1)S(1)}, bf16[64,1024]{1,0:T(8,128)(2,1)S(1)}, u32[]{:S(2)}, u32[]{:S(2)}) collective-permute-start(bf16[64,1024]{1,0:T(8,128)(2,1)S(1)} %constant_dynamic-update-slice_fusion.2.rest_0_), channel_id=1, source_target_pairs={{0,3},{1,2},{2,1},{3,0},{4,7},{5,6},{6,5},{7,4},{8,11},{9,10},{10,... | collective-permute-start | bytes 393224 | tf_op jit(solution)/shard_map/ppermute | solution.py:359
  107.7 6.1 %collective-permute-start.10 = (bf16[64,1024]{1,0:T(8,128)(2,1)S(1)}, bf16[64,1024]{1,0:T(8,128)(2,1)S(1)}, u32[]{:S(2)}, u32[]{:S(2)}) collective-permute-start(bf16[64,1024]{1,0:T(8,128)(2,1)S(1)} %constant_dynamic-update-slice_fusion.2.rest_0_), channel_id=1, source_target_pairs={{0,2},{1,3},{2,0},{3,1},{4,6},{5,7},{6,4},{7,5},{8,10},{9,11},{10,... | collective-permute-start | bytes 393224 | tf_op jit(solution)/shard_map/ppermute | solution.py:359
  107.7 6.1 %collective-permute-start.9 = (bf16[64,1024]{1,0:T(8,128)(2,1)S(1)}, bf16[64,1024]{1,0:T(8,128)(2,1)S(1)}, u32[]{:S(2)}, u32[]{:S(2)}) collective-permute-start(bf16[64,1024]{1,0:T(8,128)(2,1)S(1)} %constant_dynamic-update-slice_fusion.2.rest_0_), channel_id=1, source_target_pairs={{0,1},{1,0},{2,3},{3,2},{4,5},{5,4},{6,7},{7,6},{8,9},{9,8},{10,11... | collective-permute-start | bytes 393224 | tf_op jit(solution)/shard_map/ppermute | solution.py:359
  111.5 2.3 %copy-start.7 = (bf16[64,1024]{1,0:T(8,128)(2,1)}, bf16[64,1024]{1,0:T(8,128)(2,1)S(1)}, u32[]{:S(2)}) copy-start(bf16[64,1024]{1,0:T(8,128)(2,1)S(1)} %collective-permute-done.11.rest_3_) | copy-start | bytes 393220
  113.8 0.7 copy-start.8
  113.8 0.7 copy-start.9

commit v2 on v1

v2 whole, which is shorter than its diff:
```python
import functools
import math

import jax
import jax.numpy as jnp
from jax import lax
from jax.experimental import pallas as pl
from jax.experimental.pallas import tpu as pltpu
from jax.sharding import PartitionSpec as P

ITERS = 2

WAVENUMBER = 40.0
RADIUS = 0.5
SOFTENING = 0.25

KAPPA = WAVENUMBER / (2.0 * math.pi)
HALF_CHORD = 2.0 * RADIUS * RADIUS * KAPPA * KAPPA
SINE = tuple(
    value * (1.0 - 5e-7)
    for value in (4.442867903112522, -7.307443423342558, 3.5947880930735288, -0.7843740618048793)
)
SINE_HALF = (0.999999976589841, -0.16666647634617332, 0.00833289982302485, -0.00019800897745117133,
             2.5904884686762915e-06)
COSINE_HALF = (0.9999999997806504, -0.4999999935847076, 0.04166663625803946, -0.0013888361399933481,
               2.476016133696864e-05, -2.605149496508554e-07)

FEATURES = 32
PAIR = 8
BF = jnp.bfloat16
F32 = jnp.float32


def leading(x):
    wide = x * 65537.0
    return wide - (wide - x)


def split3(x):
    high = leading(x)
    rest = x - high
    mid = leading(rest)
    return high, mid, rest - mid


def near_side(geo, direction):
    return (geo[0:1] if direction == 0 else 1.0 - geo[0:1]) * KAPPA


def far_side(geo, direction):
    return (1.0 - geo[0:1] if direction == 0 else geo[0:1]) * KAPPA


def pad_rows(rows):
    width = rows[0].shape[1]
    rows = rows + [jnp.zeros((FEATURES - len(rows), width), F32)]
    return jnp.concatenate(rows, 0)


def target_features(geo, direction):
    u = near_side(geo, direction)
    one = jnp.ones_like(u)
    rows = list(split3(u * u + HALF_CHORD)) + [one, one, one]
    for value in (2.0 * u, -HALF_CHORD * geo[1:2], -HALF_CHORD * geo[2:3]):
        h, m, l = split3(value)
        rows += [h, h, m, m, h, l]
    return pad_rows(rows)


def source_features(geo, direction):
    v = far_side(geo, direction)
    one = jnp.ones_like(v)
    rows = [one, one, one] + list(split3(v * v))
    for value in (v, geo[1:2], geo[2:3]):
        h, m, l = split3(value)
        rows += [h, m, h, m, l, h]
    return pad_rows(rows)


def horner(coefs, x):
    total = coefs[-1]
    for coef in coefs[-2::-1]:
        total = total * x + coef
    return total


def exact_dot(a, b):
    return jnp.dot(a.astype(BF), b.astype(BF), preferred_element_type=F32)


def make_lists(lit, per_chunk):
    targets, sources = lit.shape
    chunks = sources // per_chunk
    size = per_chunk * targets
    i0 = lax.broadcasted_iota(jnp.int32, (sources, sources), 0)
    i1 = lax.broadcasted_iota(jnp.int32, (sources, sources), 1)
    same = i0 // per_chunk == i1 // per_chunk
    above = lax.broadcasted_iota(jnp.int32, (targets, targets), 0) > lax.broadcasted_iota(
        jnp.int32, (targets, targets), 1
    )
    sums = exact_dot(lit, jnp.where(same, 1.0, 0.0))
    rank = exact_dot(lit, jnp.where(same & (i0 < i1), 1.0, 0.0)) + exact_dot(
        jnp.where(above, 1.0, 0.0), sums
    )
    src = lax.broadcasted_iota(jnp.int32, lit.shape, 1) % per_chunk
    tgt = lax.broadcasted_iota(jnp.int32, lit.shape, 0)
    order = (tgt * per_chunk + src).astype(F32)
    place = jnp.where(lit > 0.5, rank, size - 1 - (order - rank))
    code = (src * targets + tgt).astype(F32)
    slot = lax.broadcasted_iota(jnp.int32, (size, sources), 0).astype(F32)
    found = jnp.zeros((size, sources), F32)
    for t in range(targets):
        found += jnp.where(slot == place[t : t + 1], code[t : t + 1], 0.0)
    c0 = lax.broadcasted_iota(jnp.int32, (sources, chunks), 0)
    c1 = lax.broadcasted_iota(jnp.int32, (sources, chunks), 1)
    pick = jnp.where(c0 // per_chunk == c1, 1.0, 0.0)
    codes = exact_dot(found, pick)
    counts = jnp.sum(exact_dot(lit, pick), axis=0, keepdims=True)
    return codes.astype(jnp.int32), counts.astype(jnp.int32)


def prep_kernel(per_chunk, axial_ref, angle_ref, area_ref, inc_ref, vis_ref, up_ref, down_ref, list_ref):
    rows = inc_ref.shape[1]
    channels = inc_ref.shape[0] // 2
    half = angle_ref[...] * 0.5
    square = half * half
    sine = horner(SINE_HALF, square) * half
    cosine = horner(COSINE_HALF, square)
    geo = [axial_ref[...], 1.0 - 2.0 * sine * sine, 2.0 * sine * cosine, area_ref[...]]
    for j in range(axial_ref.shape[1] // rows):
        part = jnp.concatenate([g[:, j * rows : (j + 1) * rows] for g in geo], 0)
        up_ref[channels + 4 * j : channels + 4 * j + 4] = part
        down_ref[channels + 4 * j : channels + 4 * j + 4] = part
    up_ref[:channels] = inc_ref[:channels].astype(F32)
    down_ref[:channels] = inc_ref[channels:].astype(F32)
    for d in range(2):
        codes, counts = make_lists(vis_ref[0, d].astype(F32), per_chunk)
        list_ref[d, : codes.shape[0]] = codes
        list_ref[d, codes.shape[0] :] = jnp.broadcast_to(counts, (8, counts.shape[1]))


def call_prep(per_chunk, axial, angle, area, inc, visibility):
    targets, sources = visibility.shape[2], visibility.shape[3]
    channels = inc.shape[0] // 2
    rows, patches = inc.shape[1], axial.shape[1]
    pack = jax.ShapeDtypeStruct((channels + 4 * (patches // rows), rows), F32)
    vmem = pl.BlockSpec(memory_space=pltpu.VMEM)
    return pl.pallas_call(
        functools.partial(prep_kernel, per_chunk),
        out_shape=(
            pack, pack,
            jax.ShapeDtypeStruct((2, per_chunk * targets + 8, sources // per_chunk), jnp.int32),
        ),
        in_specs=[vmem] * 5,
        out_specs=[vmem] * 3,
        name="prep",
    )(axial, angle, area, inc, visibility)


def table_block(q):
    q = jnp.maximum(q, 1e-12)
    turns = q * lax.rsqrt(q)
    f = turns - jnp.round(turns)
    mag = lax.rsqrt(q + SOFTENING * KAPPA * KAPPA)
    s = horner(SINE, f * f) * f
    rest = 2.0 - s * s
    both = mag * rest
    real = both - mag
    imag = (s * both) * lax.rsqrt(rest)
    return real.astype(BF), imag.astype(BF)


def build_chunk(direction, chunk, block, targets, list_ref, tf_ref, sf_ref, base, k_ref, even_ref, odd_ref):
    size = list_ref.shape[1] - 8
    count = list_ref[direction, size, chunk]

    def block_of(n):
        code = list_ref[direction, jnp.maximum(jnp.minimum(n, count - 1), 0), chunk]
        return lax.div(code, jnp.int32(targets)), lax.rem(code, jnp.int32(targets))

    def distances(group, q_ref):
        for u in range(PAIR):
            src, tgt = block_of(group * PAIR + u)
            cols = pl.ds(pl.multiple_of(tgt * block, block), block)
            feats = sf_ref[pl.ds(pl.multiple_of(base + src * block, block), block), :]
            q_ref[u * block : (u + 1) * block] = jnp.dot(feats, tf_ref[:, cols], preferred_element_type=F32)

    def entries(group, q_ref):
        for u in range(PAIR):
            src, tgt = block_of(group * PAIR + u)
            top = pl.multiple_of(src * (2 * block), 2 * block)
            part = 32
            for h in range(0, block, part):
                real, imag = table_block(q_ref[u * block + h : u * block + h + part])
                k_ref[tgt, pl.ds(pl.multiple_of(top + h, part), part), :] = real
                k_ref[tgt, pl.ds(pl.multiple_of(top + block + h, part), part), :] = imag

    def body(step, carry):
        distances(step, even_ref)
        entries(step, even_ref)
        return carry

    lax.fori_loop(0, lax.div(count + PAIR - 1, jnp.int32(PAIR)), body, 0)

    def clear(n, carry):
        code = list_ref[direction, n, chunk]
        src, tgt = lax.div(code, jnp.int32(targets)), lax.rem(code, jnp.int32(targets))
        rows = pl.ds(pl.multiple_of(src * (2 * block), 2 * block), 2 * block)
        k_ref[tgt, rows, :] = jnp.zeros((2 * block, block), BF)
        return carry

    lax.fori_loop(count, size, clear, 0)


def quarters(pack_ref, channels):
    return [pack_ref[r : r + 4] for r in range(channels, pack_ref.shape[0], 4)]


def pick(parts, index):
    chosen = parts[0]
    for j in range(1, len(parts)):
        chosen = jnp.where(index == j, parts[j], chosen)
    return chosen


def build_features(direction, channels, own_ref, pack_ref, tf_ref, sf_ref):
    rows = own_ref.shape[1]
    own = pick(quarters(own_ref, channels), lax.axis_index("patch"))
    tf_ref[...] = target_features(own, direction).astype(BF)
    for j, geo in enumerate(quarters(pack_ref, channels)):
        sf_ref[j * rows : (j + 1) * rows] = source_features(geo, direction).T.astype(BF)


def build_kernel(direction, block, per_chunk, channels, list_ref, own_ref, pack_ref, k_ref, tf_ref, sf_ref, *q):
    chunk = pl.program_id(0)

    @pl.when(chunk == 0)
    def _():
        build_features(direction, channels, own_ref, pack_ref, tf_ref, sf_ref)

    build_chunk(
        direction, chunk, block, k_ref.shape[0], list_ref, tf_ref, sf_ref, chunk * (per_chunk * block), k_ref, *q
    )


def whole(x):
    return pl.BlockSpec(x.shape, lambda c: (0,) * x.ndim)


def table_spec(targets, chunk_rows, block):
    return pl.BlockSpec((targets, chunk_rows, block), lambda c: (0, c, 0))


def call_build(direction, block, per_chunk, channels, lists, own, pack, patches):
    rows = own.shape[1]
    targets = rows // block
    chunk_rows = 2 * block * per_chunk
    return pl.pallas_call(
        functools.partial(build_kernel, direction, block, per_chunk, channels),
        grid=(patches // (block * per_chunk),),
        out_shape=jax.ShapeDtypeStruct((targets, 2 * patches, block), BF),
        in_specs=[pl.BlockSpec(memory_space=pltpu.SMEM), whole(own), whole(pack)],
        out_specs=table_spec(targets, chunk_rows, block),
        scratch_shapes=[
            pltpu.VMEM((FEATURES, rows), BF),
            pltpu.VMEM((patches, FEATURES), BF),
            pltpu.VMEM((PAIR * block, block), F32),
            pltpu.VMEM((PAIR * block, block), F32),
        ],
        compiler_params=pltpu.CompilerParams(dimension_semantics=("arbitrary",)),
        name=f"build{direction}",
    )(lists, own, pack)


def load_piece(k, piece_ref, packs, left_ref, scale, block):
    channels = piece_ref.shape[0] // 2
    half = channels // 2
    width = piece_ref.shape[1]
    gathered = width != packs[0].shape[1]
    group = lax.axis_index("patch") ^ k
    for d, pack_ref in enumerate(packs):
        areas = [pack_ref[r + 3 : r + 4] for r in range(channels, pack_ref.shape[0], 4)]
        area = jnp.concatenate(areas, 1) if gathered else pick(areas, group)
        area = area * scale
        for n in range(width // block):
            cur = piece_ref[d * channels : (d + 1) * channels, n * block : (n + 1) * block].astype(F32)
            cur = cur * area[:, n * block : (n + 1) * block]
            high = leading(cur)
            low = (cur - high).astype(BF)
            high = high.astype(BF)
            a = jnp.concatenate([high, low], 0)
            b = jnp.concatenate([high[half:], -high[:half], low[half:], -low[:half]], 0)
            start = n * block if gathered else group * width + n * block
            top = pl.multiple_of(2 * start, 2 * block)
            left_ref[d, :, pl.ds(top, block)] = a
            left_ref[d, :, pl.ds(pl.multiple_of(top + block, block), block)] = b


def finish(acc_ref, inc_ref, prev_ref, ends_ref, out_ref):
    channels = inc_ref.shape[0] // 2
    half = channels // 2
    prev = prev_ref[...].astype(F32)
    seg = lax.axis_index("seg")
    diagonal = lax.broadcasted_iota(jnp.int32, (channels, channels), 0) == lax.broadcasted_iota(
        jnp.int32, (channels, channels), 1
    )
    for d, end in enumerate((0, lax.axis_size("seg") - 1)):
        total = acc_ref[d, :channels] + acc_ref[d, channels:]
        other = prev[(1 - d) * channels : (2 - d) * channels]
        flag = jnp.where(seg == end, 1.0, 0.0)
        coef = jnp.sum(jnp.where(diagonal, ends_ref[d : d + 1] * flag, 0.0), axis=1, keepdims=True)
        cre = coef[:half]
        cim = coef[half:]
        mirrored = jnp.concatenate(
            [cre * other[:half] - cim * other[half:], cre * other[half:] + cim * other[:half]], 0
        )
        rows = slice(d * channels, (d + 1) * channels)
        out_ref[rows] = (inc_ref[rows].astype(F32) + total + mirrored).astype(BF)


def accumulate(acc_ref, left_ref, chunk, k_refs):
    targets, rows, block = k_refs[1].shape
    cols = pl.ds(pl.multiple_of(chunk * rows, rows), rows)
    group = 2 if targets % 2 == 0 else 1

    def body(n, carry):
        lanes = pl.ds(pl.multiple_of(n * (group * block), group * block), group * block)
        for d, k_ref in k_refs.items():
            right = jnp.concatenate([k_ref[n * group + g] for g in range(group)], 1)
            part = jnp.dot(left_ref[d, :, cols], right, preferred_element_type=F32)
            acc_ref[d, :, lanes] = jnp.where(chunk == 0, part, acc_ref[d, :, lanes] + part)
        return carry

    lax.fori_loop(0, targets // group, body, 0)


def build_sweep_kernel(
    block, per_chunk, pieces, scale, list_ref, own_ref, before_ref, after_ref, inc_ref, ends_ref, k0_ref, *rest
):
    piece_refs = rest[:pieces]
    k_ref, out_ref, tf_ref, sf_ref, left_ref, acc_ref, even_ref, odd_ref = rest[pieces:]
    chunk = pl.program_id(0)
    channels = inc_ref.shape[0] // 2

    @pl.when(chunk == 0)
    def _():
        build_features(1, channels, own_ref, after_ref, tf_ref, sf_ref)
        for k, piece_ref in enumerate(piece_refs):
            load_piece(k, piece_ref, (before_ref, after_ref), left_ref, scale, block)

    build_chunk(
        1, chunk, block, k_ref.shape[0], list_ref, tf_ref, sf_ref, chunk * (per_chunk * block), k_ref,
        even_ref, odd_ref,
    )
    accumulate(acc_ref, left_ref, chunk, {0: k0_ref, 1: k_ref})

    @pl.when(chunk == pl.num_programs(0) - 1)
    def _():
        finish(acc_ref, inc_ref, inc_ref, ends_ref, out_ref)


def call_build_sweep(block, per_chunk, scale, patches, lists, own, before, after, inc, ends, k0, pieces):
    rows = inc.shape[1]
    chunk_rows = 2 * block * per_chunk
    targets = rows // block
    channels = inc.shape[0]
    spec = table_spec(targets, chunk_rows, block)
    return pl.pallas_call(
        functools.partial(build_sweep_kernel, block, per_chunk, len(pieces), scale),
        grid=(patches // (block * per_chunk),),
        out_shape=(jax.ShapeDtypeStruct(k0.shape, BF), jax.ShapeDtypeStruct(inc.shape, BF)),
        in_specs=[pl.BlockSpec(memory_space=pltpu.SMEM), whole(own), whole(before), whole(after), whole(inc),
                  whole(ends), spec] + [whole(p) for p in pieces],
        out_specs=(spec, whole(inc)),
        scratch_shapes=[
            pltpu.VMEM((FEATURES, rows), BF),
            pltpu.VMEM((patches, FEATURES), BF),
            pltpu.VMEM((2, channels, 2 * patches), BF),
            pltpu.VMEM((2, channels, rows), F32),
            pltpu.VMEM((PAIR * block, block), F32),
            pltpu.VMEM((PAIR * block, block), F32),
        ],
        compiler_params=pltpu.CompilerParams(dimension_semantics=("arbitrary",)),
        name="build_sweep",
    )(lists, own, before, after, inc, ends, k0, *pieces)


def sweep_kernel(block, pieces, scale, before_ref, after_ref, inc_ref, prev_ref, ends_ref, k0_ref, k1_ref, *rest):
    piece_refs = rest[:pieces]
    out_ref, left_ref, acc_ref = rest[pieces:]
    chunk = pl.program_id(0)

    @pl.when(chunk == 0)
    def _():
        for k, piece_ref in enumerate(piece_refs):
            load_piece(k, piece_ref, (before_ref, after_ref), left_ref, scale, block)

    accumulate(acc_ref, left_ref, chunk, {0: k0_ref, 1: k1_ref})

    @pl.when(chunk == pl.num_programs(0) - 1)
    def _():
        finish(acc_ref, inc_ref, prev_ref, ends_ref, out_ref)


def call_sweep(block, per_chunk, scale, patches, before, after, inc, prev, ends, k0, k1, pieces):
    rows = inc.shape[1]
    chunk_rows = 2 * block * per_chunk
    channels = inc.shape[0]
    spec = table_spec(rows // block, chunk_rows, block)
    return pl.pallas_call(
        functools.partial(sweep_kernel, block, len(pieces), scale),
        grid=(patches // (block * per_chunk),),
        out_shape=jax.ShapeDtypeStruct(inc.shape, BF),
        in_specs=[whole(before), whole(after), whole(inc), whole(prev), whole(ends), spec, spec]
        + [whole(p) for p in pieces],
        out_specs=whole(inc),
        scratch_shapes=[
            pltpu.VMEM((2, channels, 2 * patches), BF),
            pltpu.VMEM((2, channels, rows), F32),
        ],
        compiler_params=pltpu.CompilerParams(dimension_semantics=("arbitrary",)),
        name="sweep",
    )(before, after, inc, prev, ends, k0, k1, *pieces)


def shift(value, step):
    count = lax.axis_size("seg")
    return lax.ppermute(value, "seg", [(i, i + step) for i in range(count) if 0 <= i + step < count])


def gather_patches(value):
    count = lax.axis_size("patch")
    if count not in (1, 2, 4):
        return [lax.all_gather(value, "patch", axis=1, tiled=True)]
    return [value] + [
        lax.ppermute(value, "patch", [(i, i ^ k) for i in range(count)]) for k in range(1, count)
    ]


def on_device(incident, wall_axial, wall_angle, wall_area, visibility, end_reflection):
    channels = incident.shape[1]
    patches = wall_axial.shape[1]
    block = patches // visibility.shape[3]
    half = channels // 2
    per_chunk = min(8, patches // block)
    scale = KAPPA / math.sqrt(patches)
    inc = incident[0]
    up, down, lists = call_prep(per_chunk, wall_axial, wall_angle, wall_area, inc, visibility)
    before, after = shift(up, 1), shift(down, -1)
    moved = jnp.concatenate([before[:half], after[:half]], 0).astype(BF)
    pieces = gather_patches(moved)
    k0 = call_build(0, block, per_chunk, half, lists, up, before, patches)
    k1, state = call_build_sweep(
        block, per_chunk, scale, patches, lists, up, before, after, inc, end_reflection, k0, pieces
    )
    for sweep in range(1, ITERS):
        moved = jnp.concatenate([shift(state[:half], 1), shift(state[half:], -1)], 0)
        pieces = gather_patches(moved)
        state = call_sweep(
            block, per_chunk, scale, patches, before, after, inc, state, end_reflection, k0, k1, pieces
        )
    return state[None]


def solution(mesh):
    return jax.shard_map(
        on_device,
        mesh=mesh,
        in_specs=(
            P("seg", None, "patch"),
            P("seg", None),
            P("seg", None),
            P("seg", None),
            P("seg", None, "patch", None),
            P(),
        ),
        out_specs=P("seg", None, "patch"),
        check_vma=False,
    )
```

time: 129 us -> 101 us (0.78)
  Pallas kernels: 86.7 us -> 66.3 us
  starting transfers between devices: 23.5 us -> 19.1 us
  local copies, waits for them, and re-layouts: 6.3 us -> 2.89 us
  other arithmetic: 2.25 us -> 0.01 us
  waiting for transfers between devices: 9.84 us -> 12 us
    pallas_call x1, Pallas kernels: 12.6 us -> 2.18 us  [call_prep(): pl.pallas_call(functools.partial(prep_kernel, per_chunk), out_shape=(pack...]
    pallas_call x1, Pallas kernels: 34.6 us -> 29 us  [call_build_sweep(): pl.pallas_call(functools.partial(build_sweep_kernel, block, per_chunk, le...]
    pallas_call x1, Pallas kernels: 25.2 us -> 20.1 us  [call_build(): pl.pallas_call(functools.partial(build_kernel, direction, block, per_chun...]
    ppermute x6 -> x4, starting transfers between devices: 17.8 us -> 12.8 us  [shift(): lax.ppermute(value, 'seg', [(i, i + step) for i in range(count) if 0 <= i...]
    ppermute x6 -> x4, waiting for transfers between devices: 4.12 us -> 6.53 us  [shift(): lax.ppermute(value, 'seg', [(i, i + step) for i in range(count) if 0 <= i...]
    another operation x3 -> x0, other arithmetic: 1.5 us -> none  [the longest x1 0.8 us: on_device(): jnp.stack([wall_axial[0], jnp.cos(angle), jnp.sin(angle), wall_area[0]])]
  transfers between devices with their start and end apart: 12 -> 10, of which waited for: 4 -> 6; matrix products, arithmetic and copies ran while one was open for 3% -> 0% of each run, Pallas kernels for 29% -> 20%
where the time goes in v2:
time: 101 us; the launch traced here: 100 us
  Pallas kernels  66.3 us (66%)
  starting transfers between devices  19.1 us (19%)
  waiting for transfers between devices  12 us (12%)
  local copies, waits for them, and re-layouts  2.89 us (3%)
    pallas_call x1, Pallas kernels, call_build_sweep(): pl.pallas_call(functools.partial(build_sweep_kernel, block, per_chunk, le...  29 us
    pallas_call x1, Pallas kernels, call_build(): pl.pallas_call(functools.partial(build_kernel, direction, block, per_chun...  20.1 us
    pallas_call x1, Pallas kernels, call_sweep(): pl.pallas_call(functools.partial(sweep_kernel, block, len(pieces), scale)...  15 us
    ppermute x4, starting transfers between devices, shift(): lax.ppermute(value, 'seg', [(i, i + step) for i in range(count) if 0 <= i...  12.8 us
    ppermute x4, waiting for transfers between devices, shift(): lax.ppermute(value, 'seg', [(i, i + step) for i in range(count) if 0 <= i...  6.53 us
    ppermute x6, starting transfers between devices, gather_patches(): lax.ppermute(value, 'patch', [(i, i ^ k) for i in range(count)])  6.28 us
    ppermute x6, waiting for transfers between devices, gather_patches(): lax.ppermute(value, 'patch', [(i, i ^ k) for i in range(count)])  5.52 us
    pallas_call x1, Pallas kernels, call_prep(): pl.pallas_call(functools.partial(prep_kernel, per_chunk), out_shape=(pack...  2.18 us
  transfers between devices with their start and end apart: 10, of which 6 were waited for; matrix products, arithmetic and copies ran while one was open for 0% of the time, Pallas kernels for 20%

profile of v2, /device:TPU:17, one launch (start us, length us, event | category | flops | bytes accessed | tf_op | source)
XLA Modules:
  0.0 100.5 jit_solution(2529198393873556042)
XLA Ops:
  0.0 2.2 %prep.1 = (f32[48,1024]{1,0:T(8,128)}, f32[48,1024]{1,0:T(8,128)}, s32[2,72,4]{2,1,0:T(8,128)}) custom-call(f32[1,4096]{1,0:T(1,128)} %axial_ref.1, f32[1,4096]{1,0:T(1,128)} %angle_ref.1, f32[1,4096]{1,0:T(1,128)} %area_ref.1, bf16[64,1024]{1,0:T(8,128)(2,1)} %bitcast.2, s32[1,2,8,32]{3,2,1,0:T(8,128)} %vis_ref.1), custom_call_target="tpu_custom_call" | custom-call | tf_op jit(solution)/shard_map/prep/pallas_call | solution.py:148
  2.2 2.6 %collective-permute-start.1 = (f32[48,1024]{1,0:T(8,128)}, f32[48,1024]{1,0:T(8,128)S(1)}, u32[]{:S(2)}, u32[]{:S(2)}) collective-permute-start(f32[48,1024]{1,0:T(8,128)} %get-tuple-element.11), channel_id=1, source_target_pairs={{4,0},{8,4},{12,8},{16,12},{20,16},{24,20},{28,24},{5,1},{9,5},{13... | collective-permute-start | bytes 589832 | tf_op jit(solution)/shard_map/ppermute | solution.py:428
  4.8 3.1 %collective-permute-start = (f32[48,1024]{1,0:T(8,128)}, f32[48,1024]{1,0:T(8,128)S(1)}, u32[]{:S(2)}, u32[]{:S(2)}) collective-permute-start(f32[48,1024]{1,0:T(8,128)} %get-tuple-element.10.own_ref), channel_id=1, source_target_pairs={{0,4},{4,8},{8,12},{12,16},{16,20},{20,24},{24,28},{1,5},{5,9},{9,... | collective-permute-start | bytes 589832 | tf_op jit(solution)/shard_map/ppermute | solution.py:428
  7.9 1.9 %collective-permute-done.1.after_ref = f32[48,1024]{1,0:T(8,128)S(1)} collective-permute-done((f32[48,1024]{1,0:T(8,128)}, f32[48,1024]{1,0:T(8,128)S(1)}, u32[]{:S(2)}, u32[]{:S(2)}) %collective-permute-start.1) | collective-permute-done | bytes 196640 | tf_op jit(solution)/shard_map/ppermute | solution.py:428
  9.8 0.0 copy-start.1
  9.8 1.0 collective-permute-done.pack_ref.before_ref
  10.8 0.0 copy-start
  10.8 0.0 copy-start.2
  10.8 2.2 %collective-permute-start.4 = (bf16[64,1024]{1,0:T(8,128)(2,1)S(1)}, bf16[64,1024]{1,0:T(8,128)(2,1)S(1)}, u32[]{:S(2)}, u32[]{:S(2)}) collective-permute-start(bf16[64,1024]{1,0:T(8,128)(2,1)S(1)} %pad_maximum_fusion.rest_0_), channel_id=1, source_target_pairs={{0,3},{1,2},{2,1},{3,0},{4,7},{5,6},{6,5},{7,4},{8,11},{9,10},{10,... | collective-permute-start | bytes 393224 | tf_op jit(solution)/shard_map/ppermute | solution.py:436
  13.1 0.2 collective-permute-start.3
  13.3 0.3 collective-permute-start.2
  13.5 0.0 copy-done
  13.5 20.1 %build0.1.k0_ref = bf16[8,8192,128]{2,1,0:T(8,128)(2,1)} custom-call(s32[2,72,4]{2,1,0:T(8,128)} %get-tuple-element.12.list_ref, f32[48,1024]{1,0:T(8,128)} %get-tuple-element.10.own_ref, f32[48,1024]{1,0:T(8,128)} %copy-done), custom_call_target="tpu_custom_call" | custom-call | tf_op jit(solution)/shard_map/build0/pallas_call | solution.py:258
  33.7 0.0 collective-permute-done.4.rest_3_
  33.7 0.0 copy-start.4
  33.7 0.0 collective-permute-done.3.rest_2_
  33.7 0.0 copy-start.6
  33.7 0.0 collective-permute-done.2.rest_1_
  33.7 0.0 copy-done.1
  33.7 0.0 copy-done.2
  33.7 0.6 copy-done.4
  34.3 0.0 copy-done.6
  34.4 0.0 copy-start.8
  34.4 0.7 copy-done.8
  35.0 29.0 %build_sweep.1 = (bf16[8,8192,128]{2,1,0:T(8,128)(2,1)}, bf16[64,1024]{1,0:T(8,128)(2,1)}) custom-call(s32[2,72,4]{2,1,0:T(8,128)} %get-tuple-element.12.list_ref, f32[48,1024]{1,0:T(8,128)} %get-tuple-element.10.own_ref, f32[48,1024]{1,0:T(8,128)} %copy-done, f32[48,1024]{1,0:T(8,128)} %copy-done.1, bf16[64,1024]{1,0:T(8,128)(2,1)} %bitcast.3, ...), custom_call_target="tpu_custom_call" | custom-call | tf_op jit(solution)/shard_map/build_sweep/pallas_call | solution.py:368
  64.0 0.9 fusion
  64.9 5.2 %collective-permute-start.5 = (bf16[32,1024]{1,0:T(8,128)(2,1)S(1)}, bf16[32,1024]{1,0:T(8,128)(2,1)S(1)}, u32[]{:S(2)}, u32[]{:S(2)}) collective-permute-start(bf16[32,1024]{1,0:T(8,128)(2,1)S(1)} %get-tuple-element.16), channel_id=1, source_target_pairs={{0,4},{4,8},{8,12},{12,16},{16,20},{20,24},{24,28},{1,5},{5,9},{9,... | collective-permute-start | bytes 196616 | tf_op jit(solution)/shard_map/ppermute | solution.py:428
  70.1 1.9 %collective-permute-start.6 = (bf16[32,1024]{1,0:T(8,128)(2,1)S(1)}, bf16[32,1024]{1,0:T(8,128)(2,1)S(1)}, u32[]{:S(2)}, u32[]{:S(2)}) collective-permute-start(bf16[32,1024]{1,0:T(8,128)(2,1)S(1)} %get-tuple-element.15), channel_id=1, source_target_pairs={{4,0},{8,4},{12,8},{16,12},{20,16},{24,20},{28,24},{5,1},{9,5},{13... | collective-permute-start | bytes 196616 | tf_op jit(solution)/shard_map/ppermute | solution.py:428
  72.0 0.0 collective-permute-done.5
  72.0 3.6 %collective-permute-done.6 = bf16[32,1024]{1,0:T(8,128)(2,1)S(1)} collective-permute-done((bf16[32,1024]{1,0:T(8,128)(2,1)S(1)}, bf16[32,1024]{1,0:T(8,128)(2,1)S(1)}, u32[]{:S(2)}, u32[]{:S(2)}) %collective-permute-start.6) | collective-permute-done | bytes 65568 | tf_op jit(solution)/shard_map/ppermute | solution.py:428
  75.7 0.0 copy-start.3
  75.7 2.9 %collective-permute-start.9 = (bf16[64,1024]{1,0:T(8,128)(2,1)S(1)}, bf16[64,1024]{1,0:T(8,128)(2,1)S(1)}, u32[]{:S(2)}, u32[]{:S(2)}) collective-permute-start(bf16[64,1024]{1,0:T(8,128)(2,1)S(1)} %constant_dynamic-update-slice_fusion.rest_0_), channel_id=1, source_target_pairs={{0,3},{1,2},{2,1},{3,0},{4,7},{5,6},{6,5},{7,4},{8,11},{9,10},{10,... | collective-permute-start | bytes 393224 | tf_op jit(solution)/shard_map/ppermute | solution.py:436
  78.6 0.7 collective-permute-start.8
  79.2 0.0 collective-permute-start.7
  79.2 2.7 %collective-permute-done.9.rest_3_ = bf16[64,1024]{1,0:T(8,128)(2,1)S(1)} collective-permute-done((bf16[64,1024]{1,0:T(8,128)(2,1)S(1)}, bf16[64,1024]{1,0:T(8,128)(2,1)S(1)}, u32[]{:S(2)}, u32[]{:S(2)}) %collective-permute-start.9) | collective-permute-done | bytes 131104 | tf_op jit(solution)/shard_map/ppermute | solution.py:436
  81.9 0.0 copy-start.5
  81.9 2.4 %collective-permute-done.8.rest_2_ = bf16[64,1024]{1,0:T(8,128)(2,1)S(1)} collective-permute-done((bf16[64,1024]{1,0:T(8,128)(2,1)S(1)}, bf16[64,1024]{1,0:T(8,128)(2,1)S(1)}, u32[]{:S(2)}, u32[]{:S(2)}) %collective-permute-start.8) | collective-permute-done | bytes 131104 | tf_op jit(solution)/shard_map/ppermute | solution.py:436
  84.3 0.0 copy-start.7
  84.3 0.4 collective-permute-done.7.rest_1_
  84.7 0.0 copy-start.9
  84.8 0.0 copy-done.3
  84.8 0.0 copy-done.5
  84.8 0.2 copy-done.7
  85.0 0.4 copy-done.9
  85.4 15.0 %sweep.1 = bf16[64,1024]{1,0:T(8,128)(2,1)} custom-call(f32[48,1024]{1,0:T(8,128)} %copy-done, f32[48,1024]{1,0:T(8,128)} %copy-done.1, bf16[64,1024]{1,0:T(8,128)(2,1)} %bitcast.4, bf16[64,1024]{1,0:T(8,128)(2,1)} %get-tuple-element.13.prev_ref, f32[2,32]{1,0:T(2,128)} %ends_ref.3, bf16[8,8192,128]{2,1,0:T(8,128)(2,1)} %build0.1.k0_ref, ...), custom_call_target="tpu_custom_call" | custom-call | tf_op jit(solution)/shard_map/sweep/pallas_call | solution.py:410
  (5 shorter events, 0.0 us)
Async XLA Ops:
  2.2 7.6 %collective-permute-start.1 = (f32[48,1024]{1,0:T(8,128)}, f32[48,1024]{1,0:T(8,128)S(1)}, u32[]{:S(2)}, u32[]{:S(2)}) collective-permute-start(f32[48,1024]{1,0:T(8,128)} %get-tuple-element.11), channel_id=1, source_target_pairs={{4,0},{8,4},{12,8},{16,12},{20,16},{24,20},{28,24},{5,1},{9,5},{13... | collective-permute-start | bytes 589832 | tf_op jit(solution)/shard_map/ppermute | solution.py:428
  4.8 6.0 %collective-permute-start = (f32[48,1024]{1,0:T(8,128)}, f32[48,1024]{1,0:T(8,128)S(1)}, u32[]{:S(2)}, u32[]{:S(2)}) collective-permute-start(f32[48,1024]{1,0:T(8,128)} %get-tuple-element.10.own_ref), channel_id=1, source_target_pairs={{0,4},{4,8},{8,12},{12,16},{16,20},{20,24},{24,28},{1,5},{5,9},{9,... | collective-permute-start | bytes 589832 | tf_op jit(solution)/shard_map/ppermute | solution.py:428
  9.8 23.9 %copy-start.1 = (f32[48,1024]{1,0:T(8,128)}, f32[48,1024]{1,0:T(8,128)S(1)}, u32[]{:S(2)}) copy-start(f32[48,1024]{1,0:T(8,128)S(1)} %collective-permute-done.1.after_ref) | copy-start | bytes 589828
  10.8 2.8 %copy-start = (f32[48,1024]{1,0:T(8,128)}, f32[48,1024]{1,0:T(8,128)S(1)}, u32[]{:S(2)}) copy-start(f32[48,1024]{1,0:T(8,128)S(1)} %collective-permute-done.pack_ref.before_ref) | copy-start | bytes 589828
  10.8 22.9 %copy-start.2 = (bf16[64,1024]{1,0:T(8,128)(2,1)}, bf16[64,1024]{1,0:T(8,128)(2,1)S(1)}, u32[]{:S(2)}) copy-start(bf16[64,1024]{1,0:T(8,128)(2,1)S(1)} %pad_maximum_fusion.rest_0_) | copy-start | bytes 393220
  10.8 22.8 %collective-permute-start.4 = (bf16[64,1024]{1,0:T(8,128)(2,1)S(1)}, bf16[64,1024]{1,0:T(8,128)(2,1)S(1)}, u32[]{:S(2)}, u32[]{:S(2)}) collective-permute-start(bf16[64,1024]{1,0:T(8,128)(2,1)S(1)} %pad_maximum_fusion.rest_0_), channel_id=1, source_target_pairs={{0,3},{1,2},{2,1},{3,0},{4,7},{5,6},{6,5},{7,4},{8,11},{9,10},{10,... | collective-permute-start | bytes 393224 | tf_op jit(solution)/shard_map/ppermute | solution.py:436
  13.1 20.6 %collective-permute-start.3 = (bf16[64,1024]{1,0:T(8,128)(2,1)S(1)}, bf16[64,1024]{1,0:T(8,128)(2,1)S(1)}, u32[]{:S(2)}, u32[]{:S(2)}) collective-permute-start(bf16[64,1024]{1,0:T(8,128)(2,1)S(1)} %pad_maximum_fusion.rest_0_), channel_id=1, source_target_pairs={{0,2},{1,3},{2,0},{3,1},{4,6},{5,7},{6,4},{7,5},{8,10},{9,11},{10,... | collective-permute-start | bytes 393224 | tf_op jit(solution)/shard_map/ppermute | solution.py:436
  13.3 20.4 %collective-permute-start.2 = (bf16[64,1024]{1,0:T(8,128)(2,1)S(1)}, bf16[64,1024]{1,0:T(8,128)(2,1)S(1)}, u32[]{:S(2)}, u32[]{:S(2)}) collective-permute-start(bf16[64,1024]{1,0:T(8,128)(2,1)S(1)} %pad_maximum_fusion.rest_0_), channel_id=1, source_target_pairs={{0,1},{1,0},{2,3},{3,2},{4,5},{5,4},{6,7},{7,6},{8,9},{9,8},{10,11... | collective-permute-start | bytes 393224 | tf_op jit(solution)/shard_map/ppermute | solution.py:436
  33.7 0.7 copy-start.4
  33.7 0.7 copy-start.6
  34.4 0.7 copy-start.8
  64.9 7.1 %collective-permute-start.5 = (bf16[32,1024]{1,0:T(8,128)(2,1)S(1)}, bf16[32,1024]{1,0:T(8,128)(2,1)S(1)}, u32[]{:S(2)}, u32[]{:S(2)}) collective-permute-start(bf16[32,1024]{1,0:T(8,128)(2,1)S(1)} %get-tuple-element.16), channel_id=1, source_target_pairs={{0,4},{4,8},{8,12},{12,16},{16,20},{20,24},{24,28},{1,5},{5,9},{9,... | collective-permute-start | bytes 196616 | tf_op jit(solution)/shard_map/ppermute | solution.py:428
  70.1 5.6 %collective-permute-start.6 = (bf16[32,1024]{1,0:T(8,128)(2,1)S(1)}, bf16[32,1024]{1,0:T(8,128)(2,1)S(1)}, u32[]{:S(2)}, u32[]{:S(2)}) collective-permute-start(bf16[32,1024]{1,0:T(8,128)(2,1)S(1)} %get-tuple-element.15), channel_id=1, source_target_pairs={{4,0},{8,4},{12,8},{16,12},{20,16},{24,20},{28,24},{5,1},{9,5},{13... | collective-permute-start | bytes 196616 | tf_op jit(solution)/shard_map/ppermute | solution.py:428
  75.7 9.1 %copy-start.3 = (bf16[64,1024]{1,0:T(8,128)(2,1)}, bf16[64,1024]{1,0:T(8,128)(2,1)S(1)}, u32[]{:S(2)}) copy-start(bf16[64,1024]{1,0:T(8,128)(2,1)S(1)} %constant_dynamic-update-slice_fusion.rest_0_) | copy-start | bytes 393220
  75.7 6.3 %collective-permute-start.9 = (bf16[64,1024]{1,0:T(8,128)(2,1)S(1)}, bf16[64,1024]{1,0:T(8,128)(2,1)S(1)}, u32[]{:S(2)}, u32[]{:S(2)}) collective-permute-start(bf16[64,1024]{1,0:T(8,128)(2,1)S(1)} %constant_dynamic-update-slice_fusion.rest_0_), channel_id=1, source_target_pairs={{0,3},{1,2},{2,1},{3,0},{4,7},{5,6},{6,5},{7,4},{8,11},{9,10},{10,... | collective-permute-start | bytes 393224 | tf_op jit(solution)/shard_map/ppermute | solution.py:436
  78.6 5.8 %collective-permute-start.8 = (bf16[64,1024]{1,0:T(8,128)(2,1)S(1)}, bf16[64,1024]{1,0:T(8,128)(2,1)S(1)}, u32[]{:S(2)}, u32[]{:S(2)}) collective-permute-start(bf16[64,1024]{1,0:T(8,128)(2,1)S(1)} %constant_dynamic-update-slice_fusion.rest_0_), channel_id=1, source_target_pairs={{0,2},{1,3},{2,0},{3,1},{4,6},{5,7},{6,4},{7,5},{8,10},{9,11},{10,... | collective-permute-start | bytes 393224 | tf_op jit(solution)/shard_map/ppermute | solution.py:436
  79.2 5.5 %collective-permute-start.7 = (bf16[64,1024]{1,0:T(8,128)(2,1)S(1)}, bf16[64,1024]{1,0:T(8,128)(2,1)S(1)}, u32[]{:S(2)}, u32[]{:S(2)}) collective-permute-start(bf16[64,1024]{1,0:T(8,128)(2,1)S(1)} %constant_dynamic-update-slice_fusion.rest_0_), channel_id=1, source_target_pairs={{0,1},{1,0},{2,3},{3,2},{4,5},{5,4},{6,7},{7,6},{8,9},{9,8},{10,11... | collective-permute-start | bytes 393224 | tf_op jit(solution)/shard_map/ppermute | solution.py:436
  81.9 2.8 %copy-start.5 = (bf16[64,1024]{1,0:T(8,128)(2,1)}, bf16[64,1024]{1,0:T(8,128)(2,1)S(1)}, u32[]{:S(2)}) copy-start(bf16[64,1024]{1,0:T(8,128)(2,1)S(1)} %collective-permute-done.9.rest_3_) | copy-start | bytes 393220
  84.3 0.6 copy-start.7
  84.7 0.7 copy-start.9

commit v3 on v2

--- a/solution.py
+++ b/solution.py
@@ -26,6 +26,7 @@
                2.476016133696864e-05, -2.605149496508554e-07)
 
 FEATURES = 32
+ROOMY = 50 * 2**20
 PAIR = 8
 BF = jnp.bfloat16
 F32 = jnp.float32
@@ -267,12 +268,12 @@
             pltpu.VMEM((PAIR * block, block), F32),
             pltpu.VMEM((PAIR * block, block), F32),
         ],
-        compiler_params=pltpu.CompilerParams(dimension_semantics=("arbitrary",)),
+        compiler_params=pltpu.CompilerParams(dimension_semantics=("arbitrary",), vmem_limit_bytes=ROOMY),
         name=f"build{direction}",
     )(lists, own, pack)
 
 
-def load_piece(k, piece_ref, packs, left_ref, scale, block):
+def load_piece(k, piece_ref, packs, left_ref, scale, block, local=False):
     channels = piece_ref.shape[0] // 2
     half = channels // 2
     width = piece_ref.shape[1]
@@ -290,23 +291,22 @@
             high = high.astype(BF)
             a = jnp.concatenate([high, low], 0)
             b = jnp.concatenate([high[half:], -high[:half], low[half:], -low[:half]], 0)
-            start = n * block if gathered else group * width + n * block
+            start = n * block if gathered or local else group * width + n * block
             top = pl.multiple_of(2 * start, 2 * block)
             left_ref[d, :, pl.ds(top, block)] = a
             left_ref[d, :, pl.ds(pl.multiple_of(top + block, block), block)] = b
 
 
-def finish(acc_ref, inc_ref, prev_ref, ends_ref, out_ref):
+def finish(acc_ref, inc_ref, prev, ends_ref, store):
     channels = inc_ref.shape[0] // 2
     half = channels // 2
-    prev = prev_ref[...].astype(F32)
     seg = lax.axis_index("seg")
     diagonal = lax.broadcasted_iota(jnp.int32, (channels, channels), 0) == lax.broadcasted_iota(
         jnp.int32, (channels, channels), 1
     )
     for d, end in enumerate((0, lax.axis_size("seg") - 1)):
         total = acc_ref[d, :channels] + acc_ref[d, channels:]
-        other = prev[(1 - d) * channels : (2 - d) * channels]
+        other = prev[1 - d].astype(F32)
         flag = jnp.where(seg == end, 1.0, 0.0)
         coef = jnp.sum(jnp.where(diagonal, ends_ref[d : d + 1] * flag, 0.0), axis=1, keepdims=True)
         cre = coef[:half]
@@ -315,7 +315,7 @@
             [cre * other[:half] - cim * other[half:], cre * other[half:] + cim * other[:half]], 0
         )
         rows = slice(d * channels, (d + 1) * channels)
-        out_ref[rows] = (inc_ref[rows].astype(F32) + total + mirrored).astype(BF)
+        store(d, (inc_ref[rows].astype(F32) + total + mirrored).astype(BF))
 
 
 def accumulate(acc_ref, left_ref, chunk, k_refs):
@@ -338,7 +338,7 @@
     block, per_chunk, pieces, scale, list_ref, own_ref, before_ref, after_ref, inc_ref, ends_ref, k0_ref, *rest
 ):
     piece_refs = rest[:pieces]
-    k_ref, out_ref, tf_ref, sf_ref, left_ref, acc_ref, even_ref, odd_ref = rest[pieces:]
+    k_ref, fore_ref, back_ref, tf_ref, sf_ref, left_ref, acc_ref, even_ref, odd_ref = rest[pieces:]
     chunk = pl.program_id(0)
     channels = inc_ref.shape[0] // 2
 
@@ -356,7 +356,10 @@
 
     @pl.when(chunk == pl.num_programs(0) - 1)
     def _():
-        finish(acc_ref, inc_ref, inc_ref, ends_ref, out_ref)
+        def store(d, value):
+            (fore_ref, back_ref)[d][...] = value
+
+        finish(acc_ref, inc_ref, (inc_ref[:channels], inc_ref[channels:]), ends_ref, store)
 
 
 def call_build_sweep(block, per_chunk, scale, patches, lists, own, before, after, inc, ends, k0, pieces):
@@ -364,14 +367,15 @@
     chunk_rows = 2 * block * per_chunk
     targets = rows // block
     channels = inc.shape[0]
+    part = jax.ShapeDtypeStruct((channels // 2, rows), BF)
     spec = table_spec(targets, chunk_rows, block)
     return pl.pallas_call(
         functools.partial(build_sweep_kernel, block, per_chunk, len(pieces), scale),
         grid=(patches // (block * per_chunk),),
-        out_shape=(jax.ShapeDtypeStruct(k0.shape, BF), jax.ShapeDtypeStruct(inc.shape, BF)),
+        out_shape=(jax.ShapeDtypeStruct(k0.shape, BF), part, part),
         in_specs=[pl.BlockSpec(memory_space=pltpu.SMEM), whole(own), whole(before), whole(after), whole(inc),
                   whole(ends), spec] + [whole(p) for p in pieces],
-        out_specs=(spec, whole(inc)),
+        out_specs=(spec, whole(part), whole(part)),
         scratch_shapes=[
             pltpu.VMEM((FEATURES, rows), BF),
             pltpu.VMEM((patches, FEATURES), BF),
@@ -380,47 +384,102 @@
             pltpu.VMEM((PAIR * block, block), F32),
             pltpu.VMEM((PAIR * block, block), F32),
         ],
-        compiler_params=pltpu.CompilerParams(dimension_semantics=("arbitrary",)),
+        compiler_params=pltpu.CompilerParams(dimension_semantics=("arbitrary",), vmem_limit_bytes=ROOMY),
         name="build_sweep",
     )(lists, own, before, after, inc, ends, k0, *pieces)
 
 
-def sweep_kernel(block, pieces, scale, before_ref, after_ref, inc_ref, prev_ref, ends_ref, k0_ref, k1_ref, *rest):
-    piece_refs = rest[:pieces]
-    out_ref, left_ref, acc_ref = rest[pieces:]
-    chunk = pl.program_id(0)
-
-    @pl.when(chunk == 0)
-    def _():
-        for k, piece_ref in enumerate(piece_refs):
-            load_piece(k, piece_ref, (before_ref, after_ref), left_ref, scale, block)
-
-    accumulate(acc_ref, left_ref, chunk, {0: k0_ref, 1: k1_ref})
-
-    @pl.when(chunk == pl.num_programs(0) - 1)
-    def _():
-        finish(acc_ref, inc_ref, prev_ref, ends_ref, out_ref)
-
-
-def call_sweep(block, per_chunk, scale, patches, before, after, inc, prev, ends, k0, k1, pieces):
-    rows = inc.shape[1]
-    chunk_rows = 2 * block * per_chunk
-    channels = inc.shape[0]
-    spec = table_spec(rows // block, chunk_rows, block)
+def sweep_kernel(groups, block, scale, first, last, *refs):
+    before_ref, after_ref, inc_ref, fore_ref, back_ref, ends_ref, k0_ref, k1_ref = refs[:8]
+    count = len(groups)
+    piece_refs = refs[8 : 8 + count]
+    refs = refs[8 + count :]
+    if not first:
+        base_ref, refs = refs[0], refs[1:]
+    out_ref, refs = refs[0], refs[1:]
+    acc_ref = refs[0] if last else out_ref
+    left_ref, buf_ref, sem_ref = refs[-3:]
+    targets = k0_ref.shape[0]
+    rows = buf_ref.shape[3]
+    copies = {}
+    for g, k in enumerate(groups):
+        start = pl.multiple_of((lax.axis_index("patch") ^ k) * rows, block) if rows < k0_ref.shape[1] else 0
+        for d, k_ref in enumerate((k0_ref, k1_ref)):
+            copies[g, d] = pltpu.make_async_copy(
+                k_ref.at[:, pl.ds(start, rows), :], buf_ref.at[g, d], sem_ref.at[g, d]
+            )
+            copies[g, d].start()
+    for g, (k, piece_ref) in enumerate(zip(groups, piece_refs)):
+        load_piece(k, piece_ref, (before_ref, after_ref), left_ref.at[g], scale, block, local=True)
+    if not first:
+        acc_ref[...] = base_ref[...]
+    unit = 2 if targets % 2 == 0 else 1
+    for g in range(count):
+        for d in range(2):
+            copies[g, d].wait()
+
+            def body(n, carry, g=g, d=d):
+                right = jnp.concatenate([buf_ref[g, d, n * unit + u] for u in range(unit)], 1)
+                lanes = pl.ds(pl.multiple_of(n * (unit * block), unit * block), unit * block)
+                part = jnp.dot(left_ref[g, d], right, preferred_element_type=F32)
+                acc_ref[d, :, lanes] = part if first and g == 0 else acc_ref[d, :, lanes] + part
+                return carry
+
+            lax.fori_loop(0, targets // unit, body, 0)
+    if last:
+        half = out_ref.shape[0] // 2
+
+        def store(d, value):
+            out_ref[d * half : (d + 1) * half] = value
+
+        finish(acc_ref, inc_ref, (fore_ref[...], back_ref[...]), ends_ref, store)
+
+
+def call_sweep(groups, block, scale, before, after, inc, fore, back, ends, k0, k1, pieces, base, last):
+    channels, rows = inc.shape
+    targets = k0.shape[0]
+    depth = 2 * pieces[0].shape[1]
+    vmem = pl.BlockSpec(memory_space=pltpu.VMEM)
+    table = pl.BlockSpec(memory_space=pl.ANY)
+    extra = [] if base is None else [base]
+    sums = jax.ShapeDtypeStruct((2, channels, rows), F32)
     return pl.pallas_call(
-        functools.partial(sweep_kernel, block, len(pieces), scale),
-        grid=(patches // (block * per_chunk),),
-        out_shape=jax.ShapeDtypeStruct(inc.shape, BF),
-        in_specs=[whole(before), whole(after), whole(inc), whole(prev), whole(ends), spec, spec]
-        + [whole(p) for p in pieces],
-        out_specs=whole(inc),
-        scratch_shapes=[
-            pltpu.VMEM((2, channels, 2 * patches), BF),
-            pltpu.VMEM((2, channels, rows), F32),
+        functools.partial(sweep_kernel, groups, block, scale, base is None, last),
+        out_shape=jax.ShapeDtypeStruct(inc.shape, BF) if last else sums,
+        in_specs=[vmem] * 6 + [table] * 2 + [vmem] * (len(pieces) + len(extra)),
+        out_specs=vmem,
+        scratch_shapes=([pltpu.VMEM(sums.shape, F32)] if last else [])
+        + [
+            pltpu.VMEM((len(groups), 2, channels, depth), BF),
+            pltpu.VMEM((len(groups), 2, targets, depth, block), BF),
+            pltpu.SemaphoreType.DMA((len(groups), 2)),
         ],
-        compiler_params=pltpu.CompilerParams(dimension_semantics=("arbitrary",)),
-        name="sweep",
-    )(before, after, inc, prev, ends, k0, k1, *pieces)
+        cost_estimate=pl.CostEstimate(
+            flops=4 * len(groups) * channels * rows * depth,
+            bytes_accessed=4 * len(groups) * rows * depth,
+            transcendentals=0,
+        ),
+        compiler_params=pltpu.CompilerParams(vmem_limit_bytes=ROOMY),
+        name="sweep" if last else "own_sweep",
+    )(before, after, inc, fore, back, ends, k0, k1, *pieces, *extra)
+
+
+def join_kernel(top_ref, bottom_ref, out_ref):
+    half = out_ref.shape[0] // 2
+    out_ref[:half] = top_ref[:half].astype(BF)
+    out_ref[half:] = bottom_ref[:half].astype(BF)
+
+
+def join(top, bottom, channels):
+    vmem = pl.BlockSpec(memory_space=pltpu.VMEM)
+    return pl.pallas_call(
+        join_kernel,
+        out_shape=jax.ShapeDtypeStruct((channels, top.shape[1]), BF),
+        in_specs=[vmem] * 2,
+        out_specs=vmem,
+        compiler_params=pltpu.CompilerParams(vmem_limit_bytes=4 * 2**20),
+        name="join",
+    )(top, bottom)
 
 
 def shift(value, step):
@@ -447,18 +506,22 @@
     inc = incident[0]
     up, down, lists = call_prep(per_chunk, wall_axial, wall_angle, wall_area, inc, visibility)
     before, after = shift(up, 1), shift(down, -1)
-    moved = jnp.concatenate([before[:half], after[:half]], 0).astype(BF)
-    pieces = gather_patches(moved)
+    pieces = gather_patches(join(before, after, channels))
     k0 = call_build(0, block, per_chunk, half, lists, up, before, patches)
-    k1, state = call_build_sweep(
+    k1, fore, back = call_build_sweep(
         block, per_chunk, scale, patches, lists, up, before, after, inc, end_reflection, k0, pieces
     )
     for sweep in range(1, ITERS):
-        moved = jnp.concatenate([shift(state[:half], 1), shift(state[half:], -1)], 0)
-        pieces = gather_patches(moved)
-        state = call_sweep(
-            block, per_chunk, scale, patches, before, after, inc, state, end_reflection, k0, k1, pieces
-        )
+        pieces = gather_patches(join(shift(fore, 1), shift(back, -1), channels))
+        groups = tuple(range(len(pieces)))
+        common = (block, scale, before, after, inc, fore, back, end_reflection, k0, k1)
+        base = None
+        if len(groups) > 1:
+            base = call_sweep(groups[:1], *common, pieces[:1], None, False)
+            groups, pieces = groups[1:], pieces[1:]
+        state = call_sweep(groups, *common, pieces, base, True)
+        if sweep + 1 < ITERS:
+            fore, back = state[:half], state[half:]
     return state[None]
 
 

time: 101 us -> 94.8 us (0.939)
  waiting for transfers between devices: 12 us -> 7.56 us
  local copies, waits for them, and re-layouts: 2.89 us -> 1.82 us
    ppermute x6, waiting for transfers between devices: 5.52 us -> 1.29 us  [gather_patches(): lax.ppermute(value, 'patch', [(i, i ^ k) for i in range(count)])]
    pallas_call x1 -> x4, Pallas kernels: 15 us -> 15.1 us  [the longest x2 15.1 us: call_sweep(): pl.pallas_call(functools.partial(sweep_kernel, groups, block, scale, base...]
  transfers between devices with their start and end apart: 10 -> 10, of which waited for: 6 -> 4; matrix products, arithmetic and copies ran while one was open for 0% -> 0% of each run, Pallas kernels for 20% -> 26%
where the time goes in v3:
time: 94.8 us; the launch traced here: 94.7 us
  Pallas kernels  65.4 us (69%)
  starting transfers between devices  19.8 us (21%)
  waiting for transfers between devices  7.56 us (8%)
  local copies, waits for them, and re-layouts  1.82 us (2%)
    pallas_call x1, Pallas kernels, call_build_sweep(): pl.pallas_call(functools.partial(build_sweep_kernel, block, per_chunk, le...  28.6 us
    pallas_call x1, Pallas kernels, call_build(): pl.pallas_call(functools.partial(build_kernel, direction, block, per_chun...  19.5 us
    pallas_call x2, Pallas kernels, call_sweep(): pl.pallas_call(functools.partial(sweep_kernel, groups, block, scale, base...  15.1 us
    ppermute x4, starting transfers between devices, shift(): lax.ppermute(value, 'seg', [(i, i + step) for i in range(count) if 0 <= i...  13.6 us
    ppermute x4, waiting for transfers between devices, shift(): lax.ppermute(value, 'seg', [(i, i + step) for i in range(count) if 0 <= i...  6.27 us
    ppermute x6, starting transfers between devices, gather_patches(): lax.ppermute(value, 'patch', [(i, i ^ k) for i in range(count)])  6.25 us
    pallas_call x1, Pallas kernels, call_prep(): pl.pallas_call(functools.partial(prep_kernel, per_chunk), out_shape=(pack...  2.23 us
  transfers between devices with their start and end apart: 10, of which 4 were waited for; matrix products, arithmetic and copies ran while one was open for 0% of the time, Pallas kernels for 26%

profile of v3, /device:TPU:17, one launch (start us, length us, event | category | flops | bytes accessed | tf_op | source)
XLA Modules:
  0.0 94.7 jit_solution(8009278246749705976)
XLA Ops:
  0.0 0.0 copy-start
  0.0 0.0 copy-start.3
  0.0 2.2 %prep.1 = (f32[48,1024]{1,0:T(8,128)}, f32[48,1024]{1,0:T(8,128)}, s32[2,72,4]{2,1,0:T(8,128)}) custom-call(f32[1,4096]{1,0:T(1,128)} %axial_ref.1, f32[1,4096]{1,0:T(1,128)} %angle_ref.1, f32[1,4096]{1,0:T(1,128)} %area_ref.1, bf16[64,1024]{1,0:T(8,128)(2,1)} %bitcast.2, s32[1,2,8,32]{3,2,1,0:T(8,128)} %vis_ref.1), custom_call_target="tpu_custom_call" | custom-call | tf_op jit(solution)/shard_map/prep/pallas_call | solution.py:149
  2.2 2.6 %collective-permute-start.1 = (f32[48,1024]{1,0:T(8,128)}, f32[48,1024]{1,0:T(8,128)S(1)}, u32[]{:S(2)}, u32[]{:S(2)}) collective-permute-start(f32[48,1024]{1,0:T(8,128)} %get-tuple-element.12), channel_id=1, source_target_pairs={{4,0},{8,4},{12,8},{16,12},{20,16},{24,20},{28,24},{5,1},{9,5},{13... | collective-permute-start | bytes 589832 | tf_op jit(solution)/shard_map/ppermute | solution.py:487
  4.8 3.1 %collective-permute-start = (f32[48,1024]{1,0:T(8,128)}, f32[48,1024]{1,0:T(8,128)S(1)}, u32[]{:S(2)}, u32[]{:S(2)}) collective-permute-start(f32[48,1024]{1,0:T(8,128)} %get-tuple-element.11.own_ref), channel_id=1, source_target_pairs={{0,4},{4,8},{8,12},{12,16},{16,20},{20,24},{24,28},{1,5},{5,9},{9,... | collective-permute-start | bytes 589832 | tf_op jit(solution)/shard_map/ppermute | solution.py:487
  7.9 1.9 %collective-permute-done.1.bottom_ref.after_ref.refs_1_ = f32[48,1024]{1,0:T(8,128)S(1)} collective-permute-done((f32[48,1024]{1,0:T(8,128)}, f32[48,1024]{1,0:T(8,128)S(1)}, u32[]{:S(2)}, u32[]{:S(2)}) %collective-permute-start.1) | collective-permute-done | bytes 196640 | tf_op jit(solution)/shard_map/ppermute | solution.py:487
  9.8 1.0 %collective-permute-done.pack_ref.top_ref.before_ref.refs_0_ = f32[48,1024]{1,0:T(8,128)S(1)} collective-permute-done((f32[48,1024]{1,0:T(8,128)}, f32[48,1024]{1,0:T(8,128)S(1)}, u32[]{:S(2)}, u32[]{:S(2)}) %collective-permute-start) | collective-permute-done | bytes 196640 | tf_op jit(solution)/shard_map/ppermute | solution.py:487
  10.8 2.2 %collective-permute-start.4 = (bf16[64,1024]{1,0:T(8,128)(2,1)S(1)}, bf16[64,1024]{1,0:T(8,128)(2,1)S(1)}, u32[]{:S(2)}, u32[]{:S(2)}) collective-permute-start(bf16[64,1024]{1,0:T(8,128)(2,1)S(1)} %join.2.rest_0_), channel_id=1, source_target_pairs={{0,3},{1,2},{2,1},{3,0},{4,7},{5,6},{6,5},{7,4},{8,11},{9,10},{10,... | collective-permute-start | bytes 393224 | tf_op jit(solution)/shard_map/ppermute | solution.py:495
  13.1 0.2 collective-permute-start.3
  13.3 0.3 collective-permute-start.2
  13.6 0.0 copy-start.1
  13.6 0.9 copy-done.1
  14.5 0.0 copy-start.2
  14.5 0.9 copy-done.2
  15.4 19.5 %build0.1.k0_ref.refs_6_ = bf16[8,8192,128]{2,1,0:T(8,128)(2,1)} custom-call(s32[2,72,4]{2,1,0:T(8,128)S(1)} %copy-done.2, f32[48,1024]{1,0:T(8,128)S(1)} %copy-done.1, f32[48,1024]{1,0:T(8,128)S(1)} %collective-permute-done.pack_ref.top_ref.before_ref.refs_0_), custom_call_target="tpu_custom_call" | custom-call | tf_op jit(solution)/shard_map/build0/pallas_call | solution.py:259
  34.9 0.0 collective-permute-done.4.rest_3_
  34.9 0.0 collective-permute-done.3.rest_2_
  34.9 0.0 collective-permute-done.2.rest_1_
  34.9 0.0 copy-done
  34.9 0.0 copy-done.3
  34.9 28.6 %build_sweep.1 = (bf16[8,8192,128]{2,1,0:T(8,128)(2,1)}, bf16[32,1024]{1,0:T(8,128)(2,1)S(1)}, bf16[32,1024]{1,0:T(8,128)(2,1)S(1)}) custom-call(s32[2,72,4]{2,1,0:T(8,128)S(1)} %copy-done.2, f32[48,1024]{1,0:T(8,128)S(1)} %copy-done.1, f32[48,1024]{1,0:T(8,128)S(1)} %collective-permute-done.pack_ref.top_ref.before_ref.refs_0_, ...), custom_call_target="tpu_custom_call" | custom-call | tf_op jit(solution)/shard_map/build_sweep/pallas_call | solution.py:372
  63.5 5.7 %collective-permute-start.5 = (bf16[32,1024]{1,0:T(8,128)(2,1)S(1)}, bf16[32,1024]{1,0:T(8,128)(2,1)S(1)}, u32[]{:S(2)}, u32[]{:S(2)}) collective-permute-start(bf16[32,1024]{1,0:T(8,128)(2,1)S(1)} %get-tuple-element.14.refs_3_), channel_id=1, source_target_pairs={{0,4},{4,8},{8,12},{12,16},{16,20},{20,24},{24,28},{1,5},{5,9},{9,... | collective-permute-start | bytes 196616 | tf_op jit(solution)/shard_map/ppermute | solution.py:487
  69.2 2.2 %collective-permute-start.6 = (bf16[32,1024]{1,0:T(8,128)(2,1)S(1)}, bf16[32,1024]{1,0:T(8,128)(2,1)S(1)}, u32[]{:S(2)}, u32[]{:S(2)}) collective-permute-start(bf16[32,1024]{1,0:T(8,128)(2,1)S(1)} %get-tuple-element.15.refs_4_), channel_id=1, source_target_pairs={{4,0},{8,4},{12,8},{16,12},{20,16},{24,20},{28,24},{5,1},{9,5},{13... | collective-permute-start | bytes 196616 | tf_op jit(solution)/shard_map/ppermute | solution.py:487
  71.4 0.0 collective-permute-done.5.top_ref
  71.4 3.4 %collective-permute-done.6.bottom_ref = bf16[32,1024]{1,0:T(8,128)(2,1)S(1)} collective-permute-done((bf16[32,1024]{1,0:T(8,128)(2,1)S(1)}, bf16[32,1024]{1,0:T(8,128)(2,1)S(1)}, u32[]{:S(2)}, u32[]{:S(2)}) %collective-permute-start.6) | collective-permute-done | bytes 65568 | tf_op jit(solution)/shard_map/ppermute | solution.py:487
  74.8 3.2 %collective-permute-start.9 = (bf16[64,1024]{1,0:T(8,128)(2,1)S(1)}, bf16[64,1024]{1,0:T(8,128)(2,1)S(1)}, u32[]{:S(2)}, u32[]{:S(2)}) collective-permute-start(bf16[64,1024]{1,0:T(8,128)(2,1)S(1)} %join.3.refs_8_), channel_id=1, source_target_pairs={{0,3},{1,2},{2,1},{3,0},{4,7},{5,6},{6,5},{7,4},{8,11},{9,10},{10,... | collective-permute-start | bytes 393224 | tf_op jit(solution)/shard_map/ppermute | solution.py:495
  78.0 0.0 collective-permute-start.8
  78.0 0.4 collective-permute-start.7
  78.3 4.7 %own_sweep.1.refs_11_ = f32[2,64,1024]{2,1,0:T(8,128)S(1)} custom-call(f32[48,1024]{1,0:T(8,128)S(1)} %collective-permute-done.pack_ref.top_ref.before_ref.refs_0_, f32[48,1024]{1,0:T(8,128)S(1)} %collective-permute-done.1.bottom_ref.after_ref.refs_1_, bf16[64,1024]{1,0:T(8,128)(2,1)S(1)} %bitcast.4, bf16[32,1024]{1,0:T(8,128)(2,1)S(1)} %get-tuple-element.14.refs_3_, ...), custom_call_target="tpu_custom_call" | custom-call | flops 536870912 | bytes 8388608 | tf_op jit(solution)/shard_map/own_sweep/pallas_call | solution.py:446
  83.0 0.0 collective-permute-done.9.refs_10_
  83.0 1.3 %collective-permute-done.8.refs_9_ = bf16[64,1024]{1,0:T(8,128)(2,1)S(1)} collective-permute-done((bf16[64,1024]{1,0:T(8,128)(2,1)S(1)}, bf16[64,1024]{1,0:T(8,128)(2,1)S(1)}, u32[]{:S(2)}, u32[]{:S(2)}) %collective-permute-start.8) | collective-permute-done | bytes 131104 | tf_op jit(solution)/shard_map/ppermute | solution.py:495
  84.3 0.0 collective-permute-done.7.refs_8_
  84.3 10.4 %sweep.1 = bf16[64,1024]{1,0:T(8,128)(2,1)} custom-call(f32[48,1024]{1,0:T(8,128)S(1)} %collective-permute-done.pack_ref.top_ref.before_ref.refs_0_, f32[48,1024]{1,0:T(8,128)S(1)} %collective-permute-done.1.bottom_ref.after_ref.refs_1_, bf16[64,1024]{1,0:T(8,128)(2,1)S(1)} %bitcast.5, bf16[32,1024]{1,0:T(8,128)(2,1)S(1)} %get-tuple-element.14.refs_3_, ...), custom_call_target="tpu_custom_call" | custom-call | flops 1610612736 | bytes 25165824 | tf_op jit(solution)/shard_map/sweep/pallas_call | solution.py:446
  (2 shorter events, 0.0 us)
Async XLA Ops:
  0.0 34.9 %copy-start = (bf16[1,64,1024]{2,1,0:T(8,128)(2,1)S(1)}, bf16[1,64,1024]{2,1,0:T(8,128)(2,1)}, u32[]{:S(2)}) copy-start(bf16[1,64,1024]{2,1,0:T(8,128)(2,1)} %param.6) | copy-start | bytes 393220
  0.0 34.9 %copy-start.3 = (f32[2,32]{1,0:T(2,128)S(1)}, f32[2,32]{1,0:T(2,128)}, u32[]{:S(2)}) copy-start(f32[2,32]{1,0:T(2,128)} %refs_5_.3) | copy-start | bytes 772
  2.2 7.6 %collective-permute-start.1 = (f32[48,1024]{1,0:T(8,128)}, f32[48,1024]{1,0:T(8,128)S(1)}, u32[]{:S(2)}, u32[]{:S(2)}) collective-permute-start(f32[48,1024]{1,0:T(8,128)} %get-tuple-element.12), channel_id=1, source_target_pairs={{4,0},{8,4},{12,8},{16,12},{20,16},{24,20},{28,24},{5,1},{9,5},{13... | collective-permute-start | bytes 589832 | tf_op jit(solution)/shard_map/ppermute | solution.py:487
  4.8 6.0 %collective-permute-start = (f32[48,1024]{1,0:T(8,128)}, f32[48,1024]{1,0:T(8,128)S(1)}, u32[]{:S(2)}, u32[]{:S(2)}) collective-permute-start(f32[48,1024]{1,0:T(8,128)} %get-tuple-element.11.own_ref), channel_id=1, source_target_pairs={{0,4},{4,8},{8,12},{12,16},{16,20},{20,24},{24,28},{1,5},{5,9},{9,... | collective-permute-start | bytes 589832 | tf_op jit(solution)/shard_map/ppermute | solution.py:487
  10.8 24.0 %collective-permute-start.4 = (bf16[64,1024]{1,0:T(8,128)(2,1)S(1)}, bf16[64,1024]{1,0:T(8,128)(2,1)S(1)}, u32[]{:S(2)}, u32[]{:S(2)}) collective-permute-start(bf16[64,1024]{1,0:T(8,128)(2,1)S(1)} %join.2.rest_0_), channel_id=1, source_target_pairs={{0,3},{1,2},{2,1},{3,0},{4,7},{5,6},{6,5},{7,4},{8,11},{9,10},{10,... | collective-permute-start | bytes 393224 | tf_op jit(solution)/shard_map/ppermute | solution.py:495
  13.1 21.8 %collective-permute-start.3 = (bf16[64,1024]{1,0:T(8,128)(2,1)S(1)}, bf16[64,1024]{1,0:T(8,128)(2,1)S(1)}, u32[]{:S(2)}, u32[]{:S(2)}) collective-permute-start(bf16[64,1024]{1,0:T(8,128)(2,1)S(1)} %join.2.rest_0_), channel_id=1, source_target_pairs={{0,2},{1,3},{2,0},{3,1},{4,6},{5,7},{6,4},{7,5},{8,10},{9,11},{10,... | collective-permute-start | bytes 393224 | tf_op jit(solution)/shard_map/ppermute | solution.py:495
  13.3 21.6 %collective-permute-start.2 = (bf16[64,1024]{1,0:T(8,128)(2,1)S(1)}, bf16[64,1024]{1,0:T(8,128)(2,1)S(1)}, u32[]{:S(2)}, u32[]{:S(2)}) collective-permute-start(bf16[64,1024]{1,0:T(8,128)(2,1)S(1)} %join.2.rest_0_), channel_id=1, source_target_pairs={{0,1},{1,0},{2,3},{3,2},{4,5},{5,4},{6,7},{7,6},{8,9},{9,8},{10,11... | collective-permute-start | bytes 393224 | tf_op jit(solution)/shard_map/ppermute | solution.py:495
  13.6 0.9 copy-start.1
  14.5 0.9 copy-start.2
  63.5 7.9 %collective-permute-start.5 = (bf16[32,1024]{1,0:T(8,128)(2,1)S(1)}, bf16[32,1024]{1,0:T(8,128)(2,1)S(1)}, u32[]{:S(2)}, u32[]{:S(2)}) collective-permute-start(bf16[32,1024]{1,0:T(8,128)(2,1)S(1)} %get-tuple-element.14.refs_3_), channel_id=1, source_target_pairs={{0,4},{4,8},{8,12},{12,16},{16,20},{20,24},{24,28},{1,5},{5,9},{9,... | collective-permute-start | bytes 196616 | tf_op jit(solution)/shard_map/ppermute | solution.py:487
  69.2 5.6 %collective-permute-start.6 = (bf16[32,1024]{1,0:T(8,128)(2,1)S(1)}, bf16[32,1024]{1,0:T(8,128)(2,1)S(1)}, u32[]{:S(2)}, u32[]{:S(2)}) collective-permute-start(bf16[32,1024]{1,0:T(8,128)(2,1)S(1)} %get-tuple-element.15.refs_4_), channel_id=1, source_target_pairs={{4,0},{8,4},{12,8},{16,12},{20,16},{24,20},{28,24},{5,1},{9,5},{13... | collective-permute-start | bytes 196616 | tf_op jit(solution)/shard_map/ppermute | solution.py:487
  74.8 8.3 %collective-permute-start.9 = (bf16[64,1024]{1,0:T(8,128)(2,1)S(1)}, bf16[64,1024]{1,0:T(8,128)(2,1)S(1)}, u32[]{:S(2)}, u32[]{:S(2)}) collective-permute-start(bf16[64,1024]{1,0:T(8,128)(2,1)S(1)} %join.3.refs_8_), channel_id=1, source_target_pairs={{0,3},{1,2},{2,1},{3,0},{4,7},{5,6},{6,5},{7,4},{8,11},{9,10},{10,... | collective-permute-start | bytes 393224 | tf_op jit(solution)/shard_map/ppermute | solution.py:495
  78.0 6.4 %collective-permute-start.8 = (bf16[64,1024]{1,0:T(8,128)(2,1)S(1)}, bf16[64,1024]{1,0:T(8,128)(2,1)S(1)}, u32[]{:S(2)}, u32[]{:S(2)}) collective-permute-start(bf16[64,1024]{1,0:T(8,128)(2,1)S(1)} %join.3.refs_8_), channel_id=1, source_target_pairs={{0,2},{1,3},{2,0},{3,1},{4,6},{5,7},{6,4},{7,5},{8,10},{9,11},{10,... | collective-permute-start | bytes 393224 | tf_op jit(solution)/shard_map/ppermute | solution.py:495
  78.0 6.4 %collective-permute-start.7 = (bf16[64,1024]{1,0:T(8,128)(2,1)S(1)}, bf16[64,1024]{1,0:T(8,128)(2,1)S(1)}, u32[]{:S(2)}, u32[]{:S(2)}) collective-permute-start(bf16[64,1024]{1,0:T(8,128)(2,1)S(1)} %join.3.refs_8_), channel_id=1, source_target_pairs={{0,1},{1,0},{2,3},{3,2},{4,5},{5,4},{6,7},{7,6},{8,9},{9,8},{10,11... | collective-permute-start | bytes 393224 | tf_op jit(solution)/shard_map/ppermute | solution.py:495

commit v4 on v3

--- a/solution.py
+++ b/solution.py
@@ -146,6 +146,9 @@
     rows, patches = inc.shape[1], axial.shape[1]
     pack = jax.ShapeDtypeStruct((channels + 4 * (patches // rows), rows), F32)
     vmem = pl.BlockSpec(memory_space=pltpu.VMEM)
+    axial, angle, area, inc, visibility = [
+        pltpu.with_memory_space_constraint(x, pltpu.HBM) for x in (axial, angle, area, inc, visibility)
+    ]
     return pl.pallas_call(
         functools.partial(prep_kernel, per_chunk),
         out_shape=(
@@ -154,6 +157,7 @@
         ),
         in_specs=[vmem] * 5,
         out_specs=[vmem] * 3,
+        compiler_params=pltpu.CompilerParams(vmem_limit_bytes=ROOMY),
         name="prep",
     )(axial, angle, area, inc, visibility)
 
@@ -171,7 +175,7 @@
     return real.astype(BF), imag.astype(BF)
 
 
-def build_chunk(direction, chunk, block, targets, list_ref, tf_ref, sf_ref, base, k_ref, even_ref, odd_ref):
+def build_chunk(direction, chunk, block, targets, list_ref, tf_ref, sf_ref, base, k_ref, q_ref):
     size = list_ref.shape[1] - 8
     count = list_ref[direction, size, chunk]
 
@@ -197,8 +201,8 @@
                 k_ref[tgt, pl.ds(pl.multiple_of(top + block + h, part), part), :] = imag
 
     def body(step, carry):
-        distances(step, even_ref)
-        entries(step, even_ref)
+        distances(step, q_ref)
+        entries(step, q_ref)
         return carry
 
     lax.fori_loop(0, lax.div(count + PAIR - 1, jnp.int32(PAIR)), body, 0)
@@ -265,7 +269,6 @@
         scratch_shapes=[
             pltpu.VMEM((FEATURES, rows), BF),
             pltpu.VMEM((patches, FEATURES), BF),
-            pltpu.VMEM((PAIR * block, block), F32),
             pltpu.VMEM((PAIR * block, block), F32),
         ],
         compiler_params=pltpu.CompilerParams(dimension_semantics=("arbitrary",), vmem_limit_bytes=ROOMY),
@@ -338,9 +341,29 @@
     block, per_chunk, pieces, scale, list_ref, own_ref, before_ref, after_ref, inc_ref, ends_ref, k0_ref, *rest
 ):
     piece_refs = rest[:pieces]
-    k_ref, fore_ref, back_ref, tf_ref, sf_ref, left_ref, acc_ref, even_ref, odd_ref = rest[pieces:]
+    k1_ref, fore_ref, back_ref, tf_ref, sf_ref, left_ref, acc_ref, q_ref = rest[pieces : pieces + 8]
+    in_ref, k_ref, in_sem, out_sem = rest[pieces + 8 :]
     chunk = pl.program_id(0)
+    chunks = pl.num_programs(0)
     channels = inc_ref.shape[0] // 2
+    rows = in_ref.shape[2]
+    slot = lax.rem(chunk, 2)
+
+    def fetch(c, place):
+        part = k0_ref.at[:, pl.ds(pl.multiple_of(c * rows, rows), rows), :]
+        return pltpu.make_async_copy(part, in_ref.at[place], in_sem.at[place])
+
+    def send(c, place):
+        part = k1_ref.at[:, pl.ds(pl.multiple_of(c * rows, rows), rows), :]
+        return pltpu.make_async_copy(k_ref.at[place], part, out_sem.at[place])
+
+    @pl.when(chunk == 0)
+    def _():
+        fetch(chunk, slot).start()
+
+    @pl.when(chunk + 1 < chunks)
+    def _():
+        fetch(chunk + 1, 1 - slot).start()
 
     @pl.when(chunk == 0)
     def _():
@@ -348,18 +371,29 @@
         for k, piece_ref in enumerate(piece_refs):
             load_piece(k, piece_ref, (before_ref, after_ref), left_ref, scale, block)
 
+    @pl.when(chunk >= 2)
+    def _():
+        send(chunk - 2, slot).wait()
+
     build_chunk(
-        1, chunk, block, k_ref.shape[0], list_ref, tf_ref, sf_ref, chunk * (per_chunk * block), k_ref,
-        even_ref, odd_ref,
-    )
-    accumulate(acc_ref, left_ref, chunk, {0: k0_ref, 1: k_ref})
-
-    @pl.when(chunk == pl.num_programs(0) - 1)
+        1, chunk, block, in_ref.shape[1], list_ref, tf_ref, sf_ref, chunk * (per_chunk * block),
+        k_ref.at[slot], q_ref,
+    )
+    send(chunk, slot).start()
+    fetch(chunk, slot).wait()
+    accumulate(acc_ref, left_ref, chunk, {0: in_ref.at[slot], 1: k_ref.at[slot]})
+
+    @pl.when(chunk == chunks - 1)
     def _():
         def store(d, value):
             (fore_ref, back_ref)[d][...] = value
 
         finish(acc_ref, inc_ref, (inc_ref[:channels], inc_ref[channels:]), ends_ref, store)
+        send(chunk, slot).wait()
+
+    @pl.when((chunk == chunks - 1) & (chunk >= 1))
+    def _():
+        send(chunk - 1, 1 - slot).wait()
 
 
 def call_build_sweep(block, per_chunk, scale, patches, lists, own, before, after, inc, ends, k0, pieces):
@@ -368,21 +402,24 @@
     targets = rows // block
     channels = inc.shape[0]
     part = jax.ShapeDtypeStruct((channels // 2, rows), BF)
-    spec = table_spec(targets, chunk_rows, block)
+    table = pl.BlockSpec(memory_space=pl.ANY)
     return pl.pallas_call(
         functools.partial(build_sweep_kernel, block, per_chunk, len(pieces), scale),
         grid=(patches // (block * per_chunk),),
         out_shape=(jax.ShapeDtypeStruct(k0.shape, BF), part, part),
         in_specs=[pl.BlockSpec(memory_space=pltpu.SMEM), whole(own), whole(before), whole(after), whole(inc),
-                  whole(ends), spec] + [whole(p) for p in pieces],
-        out_specs=(spec, whole(part), whole(part)),
+                  whole(ends), table] + [whole(p) for p in pieces],
+        out_specs=(table, whole(part), whole(part)),
         scratch_shapes=[
             pltpu.VMEM((FEATURES, rows), BF),
             pltpu.VMEM((patches, FEATURES), BF),
             pltpu.VMEM((2, channels, 2 * patches), BF),
             pltpu.VMEM((2, channels, rows), F32),
             pltpu.VMEM((PAIR * block, block), F32),
-            pltpu.VMEM((PAIR * block, block), F32),
+            pltpu.VMEM((2, targets, chunk_rows, block), BF),
+            pltpu.VMEM((2, targets, chunk_rows, block), BF),
+            pltpu.SemaphoreType.DMA((2,)),
+            pltpu.SemaphoreType.DMA((2,)),
         ],
         compiler_params=pltpu.CompilerParams(dimension_semantics=("arbitrary",), vmem_limit_bytes=ROOMY),
         name="build_sweep",

time: 94.8 us -> 89.7 us (0.946)
  Pallas kernels: 65.4 us -> 63.3 us
  starting transfers between devices: 19.8 us -> 17.9 us
  local copies, waits for them, and re-layouts: 1.82 us -> 0.01 us
    pallas_call x1, Pallas kernels: 28.6 us -> 26.6 us  [call_build_sweep(): pl.pallas_call(functools.partial(build_sweep_kernel, block, per_chunk, le...]
    unnamed x8 -> x4, local copies, waits for them, and re-layouts: 1.82 us -> 0.01 us
    ppermute x4, starting transfers between devices: 13.6 us -> 12 us  [shift(): lax.ppermute(value, 'seg', [(i, i + step) for i in range(count) if 0 <= i...]
  transfers between devices with their start and end apart: 10 -> 10, of which waited for: 4 -> 5; matrix products, arithmetic and copies ran while one was open for 0% -> 0% of each run, Pallas kernels for 26% -> 28%
where the time goes in v4:
time: 89.7 us; the launch traced here: 88.7 us
  Pallas kernels  63.3 us (71%)
  starting transfers between devices  17.9 us (20%)
  waiting for transfers between devices  7.41 us (8%)
    pallas_call x1, Pallas kernels, call_build_sweep(): pl.pallas_call(functools.partial(build_sweep_kernel, block, per_chunk, le...  26.6 us
    pallas_call x1, Pallas kernels, call_build(): pl.pallas_call(functools.partial(build_kernel, direction, block, per_chun...  20 us
    pallas_call x2, Pallas kernels, call_sweep(): pl.pallas_call(functools.partial(sweep_kernel, groups, block, scale, base...  15.1 us
    ppermute x4, starting transfers between devices, shift(): lax.ppermute(value, 'seg', [(i, i + step) for i in range(count) if 0 <= i...  12 us
    ppermute x4, waiting for transfers between devices, shift(): lax.ppermute(value, 'seg', [(i, i + step) for i in range(count) if 0 <= i...  6.24 us
    ppermute x6, starting transfers between devices, gather_patches(): lax.ppermute(value, 'patch', [(i, i ^ k) for i in range(count)])  5.89 us
  transfers between devices with their start and end apart: 10, of which 5 were waited for; matrix products, arithmetic and copies ran while one was open for 0% of the time, Pallas kernels for 28%

profile of v4, /device:TPU:17, one launch (start us, length us, event | category | flops | bytes accessed | tf_op | source)
XLA Modules:
  0.0 88.7 jit_solution(18162700090905537095)
XLA Ops:
  0.0 0.0 copy-start
  0.0 0.0 copy-start.1
  0.0 1.6 %prep.1 = (f32[48,1024]{1,0:T(8,128)S(1)}, f32[48,1024]{1,0:T(8,128)S(1)}, s32[2,72,4]{2,1,0:T(8,128)S(1)}) custom-call(f32[1,4096]{1,0:T(1,128)} %axial_ref.1, f32[1,4096]{1,0:T(1,128)} %angle_ref.1, f32[1,4096]{1,0:T(1,128)} %area_ref.1, bf16[64,1024]{1,0:T(8,128)(2,1)} %bitcast.2, s32[1,2,8,32]{3,2,1,0:T(8,128)} %vis_ref.1), custom_call_target="tpu_custom_call" | custom-call | tf_op jit(solution)/shard_map/prep/pallas_call | solution.py:152
  1.6 2.6 %collective-permute-start.1 = (f32[48,1024]{1,0:T(8,128)S(1)}, f32[48,1024]{1,0:T(8,128)S(1)}, u32[]{:S(2)}, u32[]{:S(2)}) collective-permute-start(f32[48,1024]{1,0:T(8,128)S(1)} %get-tuple-element.12), channel_id=1, source_target_pairs={{4,0},{8,4},{12,8},{16,12},{20,16},{24,20},{28,24},{5,1},{9,5},{13... | collective-permute-start | bytes 589832 | tf_op jit(solution)/shard_map/ppermute | solution.py:524
  4.2 3.1 %collective-permute-start = (f32[48,1024]{1,0:T(8,128)S(1)}, f32[48,1024]{1,0:T(8,128)S(1)}, u32[]{:S(2)}, u32[]{:S(2)}) collective-permute-start(f32[48,1024]{1,0:T(8,128)S(1)} %get-tuple-element.11.own_ref), channel_id=1, source_target_pairs={{0,4},{4,8},{8,12},{12,16},{16,20},{20,24},{24,28},{1,5},{5,9},{9,... | collective-permute-start | bytes 589832 | tf_op jit(solution)/shard_map/ppermute | solution.py:524
  7.3 1.7 %collective-permute-done.1.bottom_ref.after_ref.refs_1_ = f32[48,1024]{1,0:T(8,128)S(1)} collective-permute-done((f32[48,1024]{1,0:T(8,128)S(1)}, f32[48,1024]{1,0:T(8,128)S(1)}, u32[]{:S(2)}, u32[]{:S(2)}) %collective-permute-start.1) | collective-permute-done | bytes 196640 | tf_op jit(solution)/shard_map/ppermute | solution.py:524
  9.0 0.9 collective-permute-done.pack_ref.top_ref.before_ref.refs_0_
  9.9 2.2 %collective-permute-start.4 = (bf16[64,1024]{1,0:T(8,128)(2,1)S(1)}, bf16[64,1024]{1,0:T(8,128)(2,1)S(1)}, u32[]{:S(2)}, u32[]{:S(2)}) collective-permute-start(bf16[64,1024]{1,0:T(8,128)(2,1)S(1)} %join.2.rest_0_), channel_id=1, source_target_pairs={{0,3},{1,2},{2,1},{3,0},{4,7},{5,6},{6,5},{7,4},{8,11},{9,10},{10,... | collective-permute-start | bytes 393224 | tf_op jit(solution)/shard_map/ppermute | solution.py:532
  12.1 0.2 collective-permute-start.3
  12.4 0.3 collective-permute-start.2
  12.6 20.0 %build0.1.k0_ref.refs_6_ = bf16[8,8192,128]{2,1,0:T(8,128)(2,1)} custom-call(s32[2,72,4]{2,1,0:T(8,128)S(1)} %get-tuple-element.13.list_ref, f32[48,1024]{1,0:T(8,128)S(1)} %get-tuple-element.11.own_ref, f32[48,1024]{1,0:T(8,128)S(1)} %collective-permute-done.pack_ref.top_ref.before_ref.refs_0_), custom_call_target="tpu_custom_call" | custom-call | tf_op jit(solution)/shard_map/build0/pallas_call | solution.py:263
  32.6 0.0 collective-permute-done.4.rest_3_
  32.6 0.0 collective-permute-done.3.rest_2_
  32.6 0.0 collective-permute-done.2.rest_1_
  32.6 0.0 copy-done
  32.6 0.0 copy-done.1
  32.6 26.6 %build_sweep.1 = (bf16[8,8192,128]{2,1,0:T(8,128)(2,1)}, bf16[32,1024]{1,0:T(8,128)(2,1)S(1)}, bf16[32,1024]{1,0:T(8,128)(2,1)S(1)}) custom-call(s32[2,72,4]{2,1,0:T(8,128)S(1)} %get-tuple-element.13.list_ref, f32[48,1024]{1,0:T(8,128)S(1)} %get-tuple-element.11.own_ref, f32[48,1024]{1,0:T(8,128)S(1)} %collective-permute-done.pack_ref.top_ref.before_ref.refs_0_, ...), custom_call_target="tpu_custom_call" | custom-call | tf_op jit(solution)/shard_map/build_sweep/pallas_call | solution.py:406
  59.3 4.4 %collective-permute-start.5 = (bf16[32,1024]{1,0:T(8,128)(2,1)S(1)}, bf16[32,1024]{1,0:T(8,128)(2,1)S(1)}, u32[]{:S(2)}, u32[]{:S(2)}) collective-permute-start(bf16[32,1024]{1,0:T(8,128)(2,1)S(1)} %get-tuple-element.14.refs_3_), channel_id=1, source_target_pairs={{0,4},{4,8},{8,12},{12,16},{16,20},{20,24},{24,28},{1,5},{5,9},{9,... | collective-permute-start | bytes 196616 | tf_op jit(solution)/shard_map/ppermute | solution.py:524
  63.7 1.9 %collective-permute-start.6 = (bf16[32,1024]{1,0:T(8,128)(2,1)S(1)}, bf16[32,1024]{1,0:T(8,128)(2,1)S(1)}, u32[]{:S(2)}, u32[]{:S(2)}) collective-permute-start(bf16[32,1024]{1,0:T(8,128)(2,1)S(1)} %get-tuple-element.15.refs_4_), channel_id=1, source_target_pairs={{4,0},{8,4},{12,8},{16,12},{20,16},{24,20},{28,24},{5,1},{9,5},{13... | collective-permute-start | bytes 196616 | tf_op jit(solution)/shard_map/ppermute | solution.py:524
  65.6 0.0 collective-permute-done.5.top_ref
  65.6 3.6 %collective-permute-done.6.bottom_ref = bf16[32,1024]{1,0:T(8,128)(2,1)S(1)} collective-permute-done((bf16[32,1024]{1,0:T(8,128)(2,1)S(1)}, bf16[32,1024]{1,0:T(8,128)(2,1)S(1)}, u32[]{:S(2)}, u32[]{:S(2)}) %collective-permute-start.6) | collective-permute-done | bytes 65568 | tf_op jit(solution)/shard_map/ppermute | solution.py:524
  69.3 2.8 %collective-permute-start.9 = (bf16[64,1024]{1,0:T(8,128)(2,1)S(1)}, bf16[64,1024]{1,0:T(8,128)(2,1)S(1)}, u32[]{:S(2)}, u32[]{:S(2)}) collective-permute-start(bf16[64,1024]{1,0:T(8,128)(2,1)S(1)} %join.3.refs_8_), channel_id=1, source_target_pairs={{0,3},{1,2},{2,1},{3,0},{4,7},{5,6},{6,5},{7,4},{8,11},{9,10},{10,... | collective-permute-start | bytes 393224 | tf_op jit(solution)/shard_map/ppermute | solution.py:532
  72.1 0.0 collective-permute-start.8
  72.1 0.4 collective-permute-start.7
  72.5 4.7 %own_sweep.1.refs_11_ = f32[2,64,1024]{2,1,0:T(8,128)S(1)} custom-call(f32[48,1024]{1,0:T(8,128)S(1)} %collective-permute-done.pack_ref.top_ref.before_ref.refs_0_, f32[48,1024]{1,0:T(8,128)S(1)} %collective-permute-done.1.bottom_ref.after_ref.refs_1_, bf16[64,1024]{1,0:T(8,128)(2,1)S(1)} %bitcast.4, bf16[32,1024]{1,0:T(8,128)(2,1)S(1)} %get-tuple-element.14.refs_3_, ...), custom_call_target="tpu_custom_call" | custom-call | flops 536870912 | bytes 8388608 | tf_op jit(solution)/shard_map/own_sweep/pallas_call | solution.py:483
  77.2 0.0 collective-permute-done.9.refs_10_
  77.2 0.6 collective-permute-done.8.refs_9_
  77.8 0.5 collective-permute-done.7.refs_8_
  78.4 10.4 %sweep.1 = bf16[64,1024]{1,0:T(8,128)(2,1)} custom-call(f32[48,1024]{1,0:T(8,128)S(1)} %collective-permute-done.pack_ref.top_ref.before_ref.refs_0_, f32[48,1024]{1,0:T(8,128)S(1)} %collective-permute-done.1.bottom_ref.after_ref.refs_1_, bf16[64,1024]{1,0:T(8,128)(2,1)S(1)} %bitcast.5, bf16[32,1024]{1,0:T(8,128)(2,1)S(1)} %get-tuple-element.14.refs_3_, ...), custom_call_target="tpu_custom_call" | custom-call | flops 1610612736 | bytes 25165824 | tf_op jit(solution)/shard_map/sweep/pallas_call | solution.py:483
  (2 shorter events, 0.0 us)
Async XLA Ops:
  0.0 32.6 %copy-start = (bf16[1,64,1024]{2,1,0:T(8,128)(2,1)S(1)}, bf16[1,64,1024]{2,1,0:T(8,128)(2,1)}, u32[]{:S(2)}) copy-start(bf16[1,64,1024]{2,1,0:T(8,128)(2,1)} %param.6) | copy-start | bytes 393220
  0.0 32.6 %copy-start.1 = (f32[2,32]{1,0:T(2,128)S(1)}, f32[2,32]{1,0:T(2,128)}, u32[]{:S(2)}) copy-start(f32[2,32]{1,0:T(2,128)} %refs_5_.3) | copy-start | bytes 772
  1.6 7.4 %collective-permute-start.1 = (f32[48,1024]{1,0:T(8,128)S(1)}, f32[48,1024]{1,0:T(8,128)S(1)}, u32[]{:S(2)}, u32[]{:S(2)}) collective-permute-start(f32[48,1024]{1,0:T(8,128)S(1)} %get-tuple-element.12), channel_id=1, source_target_pairs={{4,0},{8,4},{12,8},{16,12},{20,16},{24,20},{28,24},{5,1},{9,5},{13... | collective-permute-start | bytes 589832 | tf_op jit(solution)/shard_map/ppermute | solution.py:524
  4.2 5.7 %collective-permute-start = (f32[48,1024]{1,0:T(8,128)S(1)}, f32[48,1024]{1,0:T(8,128)S(1)}, u32[]{:S(2)}, u32[]{:S(2)}) collective-permute-start(f32[48,1024]{1,0:T(8,128)S(1)} %get-tuple-element.11.own_ref), channel_id=1, source_target_pairs={{0,4},{4,8},{8,12},{12,16},{16,20},{20,24},{24,28},{1,5},{5,9},{9,... | collective-permute-start | bytes 589832 | tf_op jit(solution)/shard_map/ppermute | solution.py:524
  9.9 22.7 %collective-permute-start.4 = (bf16[64,1024]{1,0:T(8,128)(2,1)S(1)}, bf16[64,1024]{1,0:T(8,128)(2,1)S(1)}, u32[]{:S(2)}, u32[]{:S(2)}) collective-permute-start(bf16[64,1024]{1,0:T(8,128)(2,1)S(1)} %join.2.rest_0_), channel_id=1, source_target_pairs={{0,3},{1,2},{2,1},{3,0},{4,7},{5,6},{6,5},{7,4},{8,11},{9,10},{10,... | collective-permute-start | bytes 393224 | tf_op jit(solution)/shard_map/ppermute | solution.py:532
  12.1 20.5 %collective-permute-start.3 = (bf16[64,1024]{1,0:T(8,128)(2,1)S(1)}, bf16[64,1024]{1,0:T(8,128)(2,1)S(1)}, u32[]{:S(2)}, u32[]{:S(2)}) collective-permute-start(bf16[64,1024]{1,0:T(8,128)(2,1)S(1)} %join.2.rest_0_), channel_id=1, source_target_pairs={{0,2},{1,3},{2,0},{3,1},{4,6},{5,7},{6,4},{7,5},{8,10},{9,11},{10,... | collective-permute-start | bytes 393224 | tf_op jit(solution)/shard_map/ppermute | solution.py:532
  12.4 20.3 %collective-permute-start.2 = (bf16[64,1024]{1,0:T(8,128)(2,1)S(1)}, bf16[64,1024]{1,0:T(8,128)(2,1)S(1)}, u32[]{:S(2)}, u32[]{:S(2)}) collective-permute-start(bf16[64,1024]{1,0:T(8,128)(2,1)S(1)} %join.2.rest_0_), channel_id=1, source_target_pairs={{0,1},{1,0},{2,3},{3,2},{4,5},{5,4},{6,7},{7,6},{8,9},{9,8},{10,11... | collective-permute-start | bytes 393224 | tf_op jit(solution)/shard_map/ppermute | solution.py:532
  59.3 6.4 %collective-permute-start.5 = (bf16[32,1024]{1,0:T(8,128)(2,1)S(1)}, bf16[32,1024]{1,0:T(8,128)(2,1)S(1)}, u32[]{:S(2)}, u32[]{:S(2)}) collective-permute-start(bf16[32,1024]{1,0:T(8,128)(2,1)S(1)} %get-tuple-element.14.refs_3_), channel_id=1, source_target_pairs={{0,4},{4,8},{8,12},{12,16},{16,20},{20,24},{24,28},{1,5},{5,9},{9,... | collective-permute-start | bytes 196616 | tf_op jit(solution)/shard_map/ppermute | solution.py:524
  63.7 5.6 %collective-permute-start.6 = (bf16[32,1024]{1,0:T(8,128)(2,1)S(1)}, bf16[32,1024]{1,0:T(8,128)(2,1)S(1)}, u32[]{:S(2)}, u32[]{:S(2)}) collective-permute-start(bf16[32,1024]{1,0:T(8,128)(2,1)S(1)} %get-tuple-element.15.refs_4_), channel_id=1, source_target_pairs={{4,0},{8,4},{12,8},{16,12},{20,16},{24,20},{28,24},{5,1},{9,5},{13... | collective-permute-start | bytes 196616 | tf_op jit(solution)/shard_map/ppermute | solution.py:524
  69.3 7.9 %collective-permute-start.9 = (bf16[64,1024]{1,0:T(8,128)(2,1)S(1)}, bf16[64,1024]{1,0:T(8,128)(2,1)S(1)}, u32[]{:S(2)}, u32[]{:S(2)}) collective-permute-start(bf16[64,1024]{1,0:T(8,128)(2,1)S(1)} %join.3.refs_8_), channel_id=1, source_target_pairs={{0,3},{1,2},{2,1},{3,0},{4,7},{5,6},{6,5},{7,4},{8,11},{9,10},{10,... | collective-permute-start | bytes 393224 | tf_op jit(solution)/shard_map/ppermute | solution.py:532
  72.1 5.7 %collective-permute-start.8 = (bf16[64,1024]{1,0:T(8,128)(2,1)S(1)}, bf16[64,1024]{1,0:T(8,128)(2,1)S(1)}, u32[]{:S(2)}, u32[]{:S(2)}) collective-permute-start(bf16[64,1024]{1,0:T(8,128)(2,1)S(1)} %join.3.refs_8_), channel_id=1, source_target_pairs={{0,2},{1,3},{2,0},{3,1},{4,6},{5,7},{6,4},{7,5},{8,10},{9,11},{10,... | collective-permute-start | bytes 393224 | tf_op jit(solution)/shard_map/ppermute | solution.py:532
  72.1 6.2 %collective-permute-start.7 = (bf16[64,1024]{1,0:T(8,128)(2,1)S(1)}, bf16[64,1024]{1,0:T(8,128)(2,1)S(1)}, u32[]{:S(2)}, u32[]{:S(2)}) collective-permute-start(bf16[64,1024]{1,0:T(8,128)(2,1)S(1)} %join.3.refs_8_), channel_id=1, source_target_pairs={{0,1},{1,0},{2,3},{3,2},{4,5},{5,4},{6,7},{7,6},{8,9},{9,8},{10,11... | collective-permute-start | bytes 393224 | tf_op jit(solution)/shard_map/ppermute | solution.py:532

commit v5 on v4

--- a/solution.py
+++ b/solution.py
@@ -120,7 +120,14 @@
     return codes.astype(jnp.int32), counts.astype(jnp.int32)
 
 
-def prep_kernel(per_chunk, axial_ref, angle_ref, area_ref, inc_ref, vis_ref, up_ref, down_ref, list_ref):
+def by_parity(even, odd):
+    is_odd = lax.rem(lax.axis_index("seg"), 2) == 1
+    wide = [x.astype(F32) for x in (even, odd)]
+    pair = jnp.where(is_odd, wide[1], wide[0]), jnp.where(is_odd, wide[0], wide[1])
+    return tuple(x.astype(even.dtype) for x in pair)
+
+
+def prep_kernel(per_chunk, axial_ref, angle_ref, area_ref, inc_ref, vis_ref, swap_ref, cross_ref, list_ref):
     rows = inc_ref.shape[1]
     channels = inc_ref.shape[0] // 2
     half = angle_ref[...] * 0.5
@@ -130,10 +137,10 @@
     geo = [axial_ref[...], 1.0 - 2.0 * sine * sine, 2.0 * sine * cosine, area_ref[...]]
     for j in range(axial_ref.shape[1] // rows):
         part = jnp.concatenate([g[:, j * rows : (j + 1) * rows] for g in geo], 0)
-        up_ref[channels + 4 * j : channels + 4 * j + 4] = part
-        down_ref[channels + 4 * j : channels + 4 * j + 4] = part
-    up_ref[:channels] = inc_ref[:channels].astype(F32)
-    down_ref[:channels] = inc_ref[channels:].astype(F32)
+        swap_ref[channels + 4 * j : channels + 4 * j + 4] = part
+        cross_ref[channels + 4 * j : channels + 4 * j + 4] = part
+    fore, back = inc_ref[:channels].astype(F32), inc_ref[channels:].astype(F32)
+    swap_ref[:channels], cross_ref[:channels] = by_parity(fore, back)
     for d in range(2):
         codes, counts = make_lists(vis_ref[0, d].astype(F32), per_chunk)
         list_ref[d, : codes.shape[0]] = codes
@@ -232,7 +239,7 @@
     rows = own_ref.shape[1]
     own = pick(quarters(own_ref, channels), lax.axis_index("patch"))
     tf_ref[...] = target_features(own, direction).astype(BF)
-    for j, geo in enumerate(quarters(pack_ref, channels)):
+    for j, geo in enumerate(quarters(pack_ref, 0)):
         sf_ref[j * rows : (j + 1) * rows] = source_features(geo, direction).T.astype(BF)
 
 
@@ -283,7 +290,7 @@
     gathered = width != packs[0].shape[1]
     group = lax.axis_index("patch") ^ k
     for d, pack_ref in enumerate(packs):
-        areas = [pack_ref[r + 3 : r + 4] for r in range(channels, pack_ref.shape[0], 4)]
+        areas = [pack_ref[r + 3 : r + 4] for r in range(0, pack_ref.shape[0], 4)]
         area = jnp.concatenate(areas, 1) if gathered else pick(areas, group)
         area = area * scale
         for n in range(width // block):
@@ -385,10 +392,9 @@
 
     @pl.when(chunk == chunks - 1)
     def _():
-        def store(d, value):
-            (fore_ref, back_ref)[d][...] = value
-
-        finish(acc_ref, inc_ref, (inc_ref[:channels], inc_ref[channels:]), ends_ref, store)
+        state = {}
+        finish(acc_ref, inc_ref, (inc_ref[:channels], inc_ref[channels:]), ends_ref, state.__setitem__)
+        fore_ref[...], back_ref[...] = by_parity(state[0], state[1])
         send(chunk, slot).wait()
 
     @pl.when((chunk == chunks - 1) & (chunk >= 1))
@@ -469,7 +475,7 @@
         def store(d, value):
             out_ref[d * half : (d + 1) * half] = value
 
-        finish(acc_ref, inc_ref, (fore_ref[...], back_ref[...]), ends_ref, store)
+        finish(acc_ref, inc_ref, by_parity(fore_ref[...], back_ref[...]), ends_ref, store)
 
 
 def call_sweep(groups, block, scale, before, after, inc, fore, back, ends, k0, k1, pieces, base, last):
@@ -501,27 +507,37 @@
     )(before, after, inc, fore, back, ends, k0, k1, *pieces, *extra)
 
 
-def join_kernel(top_ref, bottom_ref, out_ref):
+def join_kernel(swap_ref, cross_ref, out_ref, *geo_refs):
     half = out_ref.shape[0] // 2
-    out_ref[:half] = top_ref[:half].astype(BF)
-    out_ref[half:] = bottom_ref[:half].astype(BF)
-
-
-def join(top, bottom, channels):
+    after, before = by_parity(swap_ref[...], cross_ref[...])
+    out_ref[:half] = before[:half].astype(BF)
+    out_ref[half:] = after[:half].astype(BF)
+    for ref, value in zip(geo_refs, (before, after)):
+        ref[...] = value[half:]
+
+
+def join(swapped, crossed, channels):
     vmem = pl.BlockSpec(memory_space=pltpu.VMEM)
+    rows, width = swapped.shape
+    geo = rows - channels // 2
+    extra = [jax.ShapeDtypeStruct((geo, width), F32)] * 2 if geo else []
     return pl.pallas_call(
         join_kernel,
-        out_shape=jax.ShapeDtypeStruct((channels, top.shape[1]), BF),
+        out_shape=[jax.ShapeDtypeStruct((channels, width), BF)] + extra,
         in_specs=[vmem] * 2,
-        out_specs=vmem,
+        out_specs=[vmem] * (1 + len(extra)),
         compiler_params=pltpu.CompilerParams(vmem_limit_bytes=4 * 2**20),
         name="join",
-    )(top, bottom)
-
-
-def shift(value, step):
+    )(swapped, crossed)
+
+
+def neighbours(first, second):
     count = lax.axis_size("seg")
-    return lax.ppermute(value, "seg", [(i, i + step) for i in range(count) if 0 <= i + step < count])
+    moves = []
+    for start in range(2):
+        pairs = [(i, i + 1) for i in range(start, count - 1, 2)]
+        moves.append(pairs + [(j, i) for i, j in pairs])
+    return lax.ppermute(first, "seg", moves[0]), lax.ppermute(second, "seg", moves[1])
 
 
 def gather_patches(value):
@@ -541,24 +557,24 @@
     per_chunk = min(8, patches // block)
     scale = KAPPA / math.sqrt(patches)
     inc = incident[0]
-    up, down, lists = call_prep(per_chunk, wall_axial, wall_angle, wall_area, inc, visibility)
-    before, after = shift(up, 1), shift(down, -1)
-    pieces = gather_patches(join(before, after, channels))
-    k0 = call_build(0, block, per_chunk, half, lists, up, before, patches)
-    k1, fore, back = call_build_sweep(
-        block, per_chunk, scale, patches, lists, up, before, after, inc, end_reflection, k0, pieces
+    own, other, lists = call_prep(per_chunk, wall_axial, wall_angle, wall_area, inc, visibility)
+    moved, before, after = join(*neighbours(own, other), channels)
+    pieces = gather_patches(moved)
+    k0 = call_build(0, block, per_chunk, half, lists, own, before, patches)
+    k1, first, second = call_build_sweep(
+        block, per_chunk, scale, patches, lists, own, before, after, inc, end_reflection, k0, pieces
     )
     for sweep in range(1, ITERS):
-        pieces = gather_patches(join(shift(fore, 1), shift(back, -1), channels))
+        pieces = gather_patches(join(*neighbours(first, second), channels)[0])
         groups = tuple(range(len(pieces)))
-        common = (block, scale, before, after, inc, fore, back, end_reflection, k0, k1)
+        common = (block, scale, before, after, inc, first, second, end_reflection, k0, k1)
         base = None
         if len(groups) > 1:
             base = call_sweep(groups[:1], *common, pieces[:1], None, False)
             groups, pieces = groups[1:], pieces[1:]
         state = call_sweep(groups, *common, pieces, base, True)
         if sweep + 1 < ITERS:
-            fore, back = state[:half], state[half:]
+            first, second = by_parity(state[:half], state[half:])
     return state[None]
 
 

time: 89.7 us -> 85.2 us (0.950)
  starting transfers between devices: 17.9 us -> 13.1 us
  waiting for transfers between devices: 7.41 us -> 8.67 us
    ppermute x4, starting transfers between devices: 12 us -> 7.6 us  [the longest x2 5.78 us: neighbours(): lax.ppermute(second, 'seg', moves[1])]
  transfers between devices with their start and end apart: 10 -> 10, of which waited for: 5 -> 3; matrix products, arithmetic and copies ran while one was open for 0% -> 0% of each run, Pallas kernels for 28% -> 30%
where the time goes in v5:
time: 85.2 us; the launch traced here: 84.9 us
  Pallas kernels  63 us (74%)
  starting transfers between devices  13.1 us (15%)
  waiting for transfers between devices  8.67 us (10%)
    pallas_call x1, Pallas kernels, call_build_sweep(): pl.pallas_call(functools.partial(build_sweep_kernel, block, per_chunk, le...  25.8 us
    pallas_call x1, Pallas kernels, call_build(): pl.pallas_call(functools.partial(build_kernel, direction, block, per_chun...  20.5 us
    pallas_call x2, Pallas kernels, call_sweep(): pl.pallas_call(functools.partial(sweep_kernel, groups, block, scale, base...  15.1 us
    ppermute x2, waiting for transfers between devices, neighbours(): lax.ppermute(second, 'seg', moves[1])  6.95 us
    ppermute x2, starting transfers between devices, neighbours(): lax.ppermute(second, 'seg', moves[1])  5.78 us
    ppermute x6, starting transfers between devices, gather_patches(): lax.ppermute(value, 'patch', [(i, i ^ k) for i in range(count)])  5.51 us
    ppermute x2, starting transfers between devices, neighbours(): lax.ppermute(first, 'seg', moves[0])  1.82 us
    ppermute x6, waiting for transfers between devices, gather_patches(): lax.ppermute(value, 'patch', [(i, i ^ k) for i in range(count)])  1.71 us
  transfers between devices with their start and end apart: 10, of which 3 were waited for; matrix products, arithmetic and copies ran while one was open for 0% of the time, Pallas kernels for 30%

profile of v5, /device:TPU:17, one launch (start us, length us, event | category | flops | bytes accessed | tf_op | source)
XLA Modules:
  0.0 84.9 jit_solution(10064734526397252547)
XLA Ops:
  0.0 0.0 copy-start
  0.0 0.0 copy-start.1
  0.0 1.6 %prep.1 = (f32[48,1024]{1,0:T(8,128)S(1)}, f32[48,1024]{1,0:T(8,128)S(1)}, s32[2,72,4]{2,1,0:T(8,128)S(1)}) custom-call(f32[1,4096]{1,0:T(1,128)} %axial_ref.1, f32[1,4096]{1,0:T(1,128)} %angle_ref.1, f32[1,4096]{1,0:T(1,128)} %area_ref.1, bf16[64,1024]{1,0:T(8,128)(2,1)} %bitcast.2, s32[1,2,8,32]{3,2,1,0:T(8,128)} %vis_ref.1), custom_call_target="tpu_custom_call" | custom-call | tf_op jit(solution)/shard_map/prep/pallas_call | solution.py:159
  1.6 3.8 %collective-permute-start.1 = (f32[48,1024]{1,0:T(8,128)S(1)}, f32[48,1024]{1,0:T(8,128)S(1)}, u32[]{:S(2)}, u32[]{:S(2)}) collective-permute-start(f32[48,1024]{1,0:T(8,128)S(1)} %get-tuple-element.15), channel_id=1, source_target_pairs={{4,8},{12,16},{20,24},{8,4},{16,12},{24,20},{5,9},{13,17},{21,25},... | collective-permute-start | bytes 589832 | tf_op jit(solution)/shard_map/ppermute | solution.py:540
  5.4 0.1 collective-permute-start
  5.5 3.4 %collective-permute-done.1.cross_ref = f32[48,1024]{1,0:T(8,128)S(1)} collective-permute-done((f32[48,1024]{1,0:T(8,128)S(1)}, f32[48,1024]{1,0:T(8,128)S(1)}, u32[]{:S(2)}, u32[]{:S(2)}) %collective-permute-start.1) | collective-permute-done | bytes 196640 | tf_op jit(solution)/shard_map/ppermute | solution.py:540
  8.9 0.0 collective-permute-done.swap_ref
  8.9 2.2 %collective-permute-start.4 = (bf16[64,1024]{1,0:T(8,128)(2,1)S(1)}, bf16[64,1024]{1,0:T(8,128)(2,1)S(1)}, u32[]{:S(2)}, u32[]{:S(2)}) collective-permute-start(bf16[64,1024]{1,0:T(8,128)(2,1)S(1)} %get-tuple-element.19.rest_0_), channel_id=1, source_target_pairs={{0,3},{1,2},{2,1},{3,0},{4,7},{5,6},{6,5},{7,4},{8,11},{9,10},{10,... | collective-permute-start | bytes 393224 | tf_op jit(solution)/shard_map/ppermute | solution.py:548
  11.1 0.2 collective-permute-start.3
  11.4 0.3 collective-permute-start.2
  11.6 20.5 %build0.1.k0_ref.refs_6_ = bf16[8,8192,128]{2,1,0:T(8,128)(2,1)} custom-call(s32[2,72,4]{2,1,0:T(8,128)S(1)} %get-tuple-element.18.list_ref, f32[48,1024]{1,0:T(8,128)S(1)} %get-tuple-element.14.own_ref, f32[16,1024]{1,0:T(8,128)S(1)} %get-tuple-element.16.pack_ref.before_ref.refs_0_), custom_call_target="tpu_custom_call" | custom-call | tf_op jit(solution)/shard_map/build0/pallas_call | solution.py:270
  32.1 0.0 collective-permute-done.4.rest_3_
  32.1 0.0 collective-permute-done.3.rest_2_
  32.1 0.0 collective-permute-done.2.rest_1_
  32.1 0.0 copy-done
  32.1 0.0 copy-done.1
  32.1 25.8 %build_sweep.1 = (bf16[8,8192,128]{2,1,0:T(8,128)(2,1)}, bf16[32,1024]{1,0:T(8,128)(2,1)S(1)}, bf16[32,1024]{1,0:T(8,128)(2,1)S(1)}) custom-call(s32[2,72,4]{2,1,0:T(8,128)S(1)} %get-tuple-element.18.list_ref, f32[48,1024]{1,0:T(8,128)S(1)} %get-tuple-element.14.own_ref, f32[16,1024]{1,0:T(8,128)S(1)} %get-tuple-element.16.pack_ref.before_ref.refs_0_, ...), custom_call_target="tpu_custom_call" | custom-call | tf_op jit(solution)/shard_map/build_sweep/pallas_call | solution.py:412
  57.9 1.7 %collective-permute-start.5 = (bf16[32,1024]{1,0:T(8,128)(2,1)S(1)}, bf16[32,1024]{1,0:T(8,128)(2,1)S(1)}, u32[]{:S(2)}, u32[]{:S(2)}) collective-permute-start(bf16[32,1024]{1,0:T(8,128)(2,1)S(1)} %get-tuple-element.20.refs_3_), channel_id=1, source_target_pairs={{0,4},{8,12},{16,20},{24,28},{4,0},{12,8},{20,16},{28,24},{1,5},{9... | collective-permute-start | bytes 196616 | tf_op jit(solution)/shard_map/ppermute | solution.py:540
  59.7 2.0 %collective-permute-start.6 = (bf16[32,1024]{1,0:T(8,128)(2,1)S(1)}, bf16[32,1024]{1,0:T(8,128)(2,1)S(1)}, u32[]{:S(2)}, u32[]{:S(2)}) collective-permute-start(bf16[32,1024]{1,0:T(8,128)(2,1)S(1)} %get-tuple-element.21.refs_4_), channel_id=1, source_target_pairs={{4,8},{12,16},{20,24},{8,4},{16,12},{24,20},{5,9},{13,17},{21,25},... | collective-permute-start | bytes 196616 | tf_op jit(solution)/shard_map/ppermute | solution.py:540
  61.7 0.0 collective-permute-done.5.swap_ref
  61.7 3.5 %collective-permute-done.6.cross_ref = bf16[32,1024]{1,0:T(8,128)(2,1)S(1)} collective-permute-done((bf16[32,1024]{1,0:T(8,128)(2,1)S(1)}, bf16[32,1024]{1,0:T(8,128)(2,1)S(1)}, u32[]{:S(2)}, u32[]{:S(2)}) %collective-permute-start.6) | collective-permute-done | bytes 65568 | tf_op jit(solution)/shard_map/ppermute | solution.py:540
  65.3 1.5 %collective-permute-start.9 = (bf16[64,1024]{1,0:T(8,128)(2,1)S(1)}, bf16[64,1024]{1,0:T(8,128)(2,1)S(1)}, u32[]{:S(2)}, u32[]{:S(2)}) collective-permute-start(bf16[64,1024]{1,0:T(8,128)(2,1)S(1)} %join.3.refs_8_), channel_id=1, source_target_pairs={{0,3},{1,2},{2,1},{3,0},{4,7},{5,6},{6,5},{7,4},{8,11},{9,10},{10,... | collective-permute-start | bytes 393224 | tf_op jit(solution)/shard_map/ppermute | solution.py:548
  66.7 1.0 %collective-permute-start.8 = (bf16[64,1024]{1,0:T(8,128)(2,1)S(1)}, bf16[64,1024]{1,0:T(8,128)(2,1)S(1)}, u32[]{:S(2)}, u32[]{:S(2)}) collective-permute-start(bf16[64,1024]{1,0:T(8,128)(2,1)S(1)} %join.3.refs_8_), channel_id=1, source_target_pairs={{0,2},{1,3},{2,0},{3,1},{4,6},{5,7},{6,4},{7,5},{8,10},{9,11},{10,... | collective-permute-start | bytes 393224 | tf_op jit(solution)/shard_map/ppermute | solution.py:548
  67.7 0.4 collective-permute-start.7
  68.1 4.7 %own_sweep.1.refs_11_ = f32[2,64,1024]{2,1,0:T(8,128)S(1)} custom-call(f32[16,1024]{1,0:T(8,128)S(1)} %get-tuple-element.16.pack_ref.before_ref.refs_0_, f32[16,1024]{1,0:T(8,128)S(1)} %get-tuple-element.17.after_ref.refs_1_, bf16[64,1024]{1,0:T(8,128)(2,1)S(1)} %bitcast.4, bf16[32,1024]{1,0:T(8,128)(2,1)S(1)} %get-tuple-element.20.refs_3_, ...), custom_call_target="tpu_custom_call" | custom-call | flops 536870912 | bytes 8388608 | tf_op jit(solution)/shard_map/own_sweep/pallas_call | solution.py:489
  72.8 0.0 collective-permute-done.9.refs_10_
  72.8 1.7 %collective-permute-done.8.refs_9_ = bf16[64,1024]{1,0:T(8,128)(2,1)S(1)} collective-permute-done((bf16[64,1024]{1,0:T(8,128)(2,1)S(1)}, bf16[64,1024]{1,0:T(8,128)(2,1)S(1)}, u32[]{:S(2)}, u32[]{:S(2)}) %collective-permute-start.8) | collective-permute-done | bytes 131104 | tf_op jit(solution)/shard_map/ppermute | solution.py:548
  74.5 0.0 collective-permute-done.7.refs_8_
  74.5 10.4 %sweep.1 = bf16[64,1024]{1,0:T(8,128)(2,1)} custom-call(f32[16,1024]{1,0:T(8,128)S(1)} %get-tuple-element.16.pack_ref.before_ref.refs_0_, f32[16,1024]{1,0:T(8,128)S(1)} %get-tuple-element.17.after_ref.refs_1_, bf16[64,1024]{1,0:T(8,128)(2,1)S(1)} %bitcast.5, bf16[32,1024]{1,0:T(8,128)(2,1)S(1)} %get-tuple-element.20.refs_3_, ...), custom_call_target="tpu_custom_call" | custom-call | flops 1610612736 | bytes 25165824 | tf_op jit(solution)/shard_map/sweep/pallas_call | solution.py:489
  (2 shorter events, 0.1 us)
Async XLA Ops:
  0.0 32.1 %copy-start = (bf16[1,64,1024]{2,1,0:T(8,128)(2,1)S(1)}, bf16[1,64,1024]{2,1,0:T(8,128)(2,1)}, u32[]{:S(2)}) copy-start(bf16[1,64,1024]{2,1,0:T(8,128)(2,1)} %param.6) | copy-start | bytes 393220
  0.0 32.1 %copy-start.1 = (f32[2,32]{1,0:T(2,128)S(1)}, f32[2,32]{1,0:T(2,128)}, u32[]{:S(2)}) copy-start(f32[2,32]{1,0:T(2,128)} %refs_5_.3) | copy-start | bytes 772
  1.6 7.3 %collective-permute-start.1 = (f32[48,1024]{1,0:T(8,128)S(1)}, f32[48,1024]{1,0:T(8,128)S(1)}, u32[]{:S(2)}, u32[]{:S(2)}) collective-permute-start(f32[48,1024]{1,0:T(8,128)S(1)} %get-tuple-element.15), channel_id=1, source_target_pairs={{4,8},{12,16},{20,24},{8,4},{16,12},{24,20},{5,9},{13,17},{21,25},... | collective-permute-start | bytes 589832 | tf_op jit(solution)/shard_map/ppermute | solution.py:540
  5.4 3.5 %collective-permute-start = (f32[48,1024]{1,0:T(8,128)S(1)}, f32[48,1024]{1,0:T(8,128)S(1)}, u32[]{:S(2)}, u32[]{:S(2)}) collective-permute-start(f32[48,1024]{1,0:T(8,128)S(1)} %get-tuple-element.14.own_ref), channel_id=1, source_target_pairs={{0,4},{8,12},{16,20},{24,28},{4,0},{12,8},{20,16},{28,24},{1,5},{9... | collective-permute-start | bytes 589832 | tf_op jit(solution)/shard_map/ppermute | solution.py:540
  8.9 23.2 %collective-permute-start.4 = (bf16[64,1024]{1,0:T(8,128)(2,1)S(1)}, bf16[64,1024]{1,0:T(8,128)(2,1)S(1)}, u32[]{:S(2)}, u32[]{:S(2)}) collective-permute-start(bf16[64,1024]{1,0:T(8,128)(2,1)S(1)} %get-tuple-element.19.rest_0_), channel_id=1, source_target_pairs={{0,3},{1,2},{2,1},{3,0},{4,7},{5,6},{6,5},{7,4},{8,11},{9,10},{10,... | collective-permute-start | bytes 393224 | tf_op jit(solution)/shard_map/ppermute | solution.py:548
  11.1 21.0 %collective-permute-start.3 = (bf16[64,1024]{1,0:T(8,128)(2,1)S(1)}, bf16[64,1024]{1,0:T(8,128)(2,1)S(1)}, u32[]{:S(2)}, u32[]{:S(2)}) collective-permute-start(bf16[64,1024]{1,0:T(8,128)(2,1)S(1)} %get-tuple-element.19.rest_0_), channel_id=1, source_target_pairs={{0,2},{1,3},{2,0},{3,1},{4,6},{5,7},{6,4},{7,5},{8,10},{9,11},{10,... | collective-permute-start | bytes 393224 | tf_op jit(solution)/shard_map/ppermute | solution.py:548
  11.4 20.7 %collective-permute-start.2 = (bf16[64,1024]{1,0:T(8,128)(2,1)S(1)}, bf16[64,1024]{1,0:T(8,128)(2,1)S(1)}, u32[]{:S(2)}, u32[]{:S(2)}) collective-permute-start(bf16[64,1024]{1,0:T(8,128)(2,1)S(1)} %get-tuple-element.19.rest_0_), channel_id=1, source_target_pairs={{0,1},{1,0},{2,3},{3,2},{4,5},{5,4},{6,7},{7,6},{8,9},{9,8},{10,11... | collective-permute-start | bytes 393224 | tf_op jit(solution)/shard_map/ppermute | solution.py:548
  57.9 3.8 %collective-permute-start.5 = (bf16[32,1024]{1,0:T(8,128)(2,1)S(1)}, bf16[32,1024]{1,0:T(8,128)(2,1)S(1)}, u32[]{:S(2)}, u32[]{:S(2)}) collective-permute-start(bf16[32,1024]{1,0:T(8,128)(2,1)S(1)} %get-tuple-element.20.refs_3_), channel_id=1, source_target_pairs={{0,4},{8,12},{16,20},{24,28},{4,0},{12,8},{20,16},{28,24},{1,5},{9... | collective-permute-start | bytes 196616 | tf_op jit(solution)/shard_map/ppermute | solution.py:540
  59.7 5.6 %collective-permute-start.6 = (bf16[32,1024]{1,0:T(8,128)(2,1)S(1)}, bf16[32,1024]{1,0:T(8,128)(2,1)S(1)}, u32[]{:S(2)}, u32[]{:S(2)}) collective-permute-start(bf16[32,1024]{1,0:T(8,128)(2,1)S(1)} %get-tuple-element.21.refs_4_), channel_id=1, source_target_pairs={{4,8},{12,16},{20,24},{8,4},{16,12},{24,20},{5,9},{13,17},{21,25},... | collective-permute-start | bytes 196616 | tf_op jit(solution)/shard_map/ppermute | solution.py:540
  65.3 7.5 %collective-permute-start.9 = (bf16[64,1024]{1,0:T(8,128)(2,1)S(1)}, bf16[64,1024]{1,0:T(8,128)(2,1)S(1)}, u32[]{:S(2)}, u32[]{:S(2)}) collective-permute-start(bf16[64,1024]{1,0:T(8,128)(2,1)S(1)} %join.3.refs_8_), channel_id=1, source_target_pairs={{0,3},{1,2},{2,1},{3,0},{4,7},{5,6},{6,5},{7,4},{8,11},{9,10},{10,... | collective-permute-start | bytes 393224 | tf_op jit(solution)/shard_map/ppermute | solution.py:548
  66.7 7.8 %collective-permute-start.8 = (bf16[64,1024]{1,0:T(8,128)(2,1)S(1)}, bf16[64,1024]{1,0:T(8,128)(2,1)S(1)}, u32[]{:S(2)}, u32[]{:S(2)}) collective-permute-start(bf16[64,1024]{1,0:T(8,128)(2,1)S(1)} %join.3.refs_8_), channel_id=1, source_target_pairs={{0,2},{1,3},{2,0},{3,1},{4,6},{5,7},{6,4},{7,5},{8,10},{9,11},{10,... | collective-permute-start | bytes 393224 | tf_op jit(solution)/shard_map/ppermute | solution.py:548
  67.7 6.8 %collective-permute-start.7 = (bf16[64,1024]{1,0:T(8,128)(2,1)S(1)}, bf16[64,1024]{1,0:T(8,128)(2,1)S(1)}, u32[]{:S(2)}, u32[]{:S(2)}) collective-permute-start(bf16[64,1024]{1,0:T(8,128)(2,1)S(1)} %join.3.refs_8_), channel_id=1, source_target_pairs={{0,1},{1,0},{2,3},{3,2},{4,5},{5,4},{6,7},{7,6},{8,9},{9,8},{10,11... | collective-permute-start | bytes 393224 | tf_op jit(solution)/shard_map/ppermute | solution.py:548

commit v6 on v5

--- a/solution.py
+++ b/solution.py
@@ -349,7 +349,7 @@
 ):
     piece_refs = rest[:pieces]
     k1_ref, fore_ref, back_ref, tf_ref, sf_ref, left_ref, acc_ref, q_ref = rest[pieces : pieces + 8]
-    in_ref, k_ref, in_sem, out_sem = rest[pieces + 8 :]
+    in_ref, in_sem = rest[pieces + 8 :]
     chunk = pl.program_id(0)
     chunks = pl.num_programs(0)
     channels = inc_ref.shape[0] // 2
@@ -360,9 +360,7 @@
         part = k0_ref.at[:, pl.ds(pl.multiple_of(c * rows, rows), rows), :]
         return pltpu.make_async_copy(part, in_ref.at[place], in_sem.at[place])
 
-    def send(c, place):
-        part = k1_ref.at[:, pl.ds(pl.multiple_of(c * rows, rows), rows), :]
-        return pltpu.make_async_copy(k_ref.at[place], part, out_sem.at[place])
+    k_ref = k1_ref.at[:, pl.ds(pl.multiple_of(chunk * rows, rows), rows), :]
 
     @pl.when(chunk == 0)
     def _():
@@ -378,28 +376,18 @@
         for k, piece_ref in enumerate(piece_refs):
             load_piece(k, piece_ref, (before_ref, after_ref), left_ref, scale, block)
 
-    @pl.when(chunk >= 2)
-    def _():
-        send(chunk - 2, slot).wait()
-
     build_chunk(
         1, chunk, block, in_ref.shape[1], list_ref, tf_ref, sf_ref, chunk * (per_chunk * block),
-        k_ref.at[slot], q_ref,
-    )
-    send(chunk, slot).start()
+        k_ref, q_ref,
+    )
     fetch(chunk, slot).wait()
-    accumulate(acc_ref, left_ref, chunk, {0: in_ref.at[slot], 1: k_ref.at[slot]})
+    accumulate(acc_ref, left_ref, chunk, {0: in_ref.at[slot], 1: k_ref})
 
     @pl.when(chunk == chunks - 1)
     def _():
         state = {}
         finish(acc_ref, inc_ref, (inc_ref[:channels], inc_ref[channels:]), ends_ref, state.__setitem__)
         fore_ref[...], back_ref[...] = by_parity(state[0], state[1])
-        send(chunk, slot).wait()
-
-    @pl.when((chunk == chunks - 1) & (chunk >= 1))
-    def _():
-        send(chunk - 1, 1 - slot).wait()
 
 
 def call_build_sweep(block, per_chunk, scale, patches, lists, own, before, after, inc, ends, k0, pieces):
@@ -408,14 +396,15 @@
     targets = rows // block
     channels = inc.shape[0]
     part = jax.ShapeDtypeStruct((channels // 2, rows), BF)
+    k0 = pltpu.with_memory_space_constraint(k0, pltpu.HBM)
     table = pl.BlockSpec(memory_space=pl.ANY)
     return pl.pallas_call(
         functools.partial(build_sweep_kernel, block, per_chunk, len(pieces), scale),
         grid=(patches // (block * per_chunk),),
-        out_shape=(jax.ShapeDtypeStruct(k0.shape, BF), part, part),
+        out_shape=(pltpu.VMEM(k0.shape, BF), part, part),
         in_specs=[pl.BlockSpec(memory_space=pltpu.SMEM), whole(own), whole(before), whole(after), whole(inc),
                   whole(ends), table] + [whole(p) for p in pieces],
-        out_specs=(table, whole(part), whole(part)),
+        out_specs=(pl.BlockSpec(memory_space=pltpu.VMEM), whole(part), whole(part)),
         scratch_shapes=[
             pltpu.VMEM((FEATURES, rows), BF),
             pltpu.VMEM((patches, FEATURES), BF),
@@ -423,11 +412,9 @@
             pltpu.VMEM((2, channels, rows), F32),
             pltpu.VMEM((PAIR * block, block), F32),
             pltpu.VMEM((2, targets, chunk_rows, block), BF),
-            pltpu.VMEM((2, targets, chunk_rows, block), BF),
-            pltpu.SemaphoreType.DMA((2,)),
             pltpu.SemaphoreType.DMA((2,)),
         ],
-        compiler_params=pltpu.CompilerParams(dimension_semantics=("arbitrary",), vmem_limit_bytes=ROOMY),
+        compiler_params=pltpu.CompilerParams(dimension_semantics=("arbitrary",), vmem_limit_bytes=24 * 2**20),
         name="build_sweep",
     )(lists, own, before, after, inc, ends, k0, *pieces)
 
@@ -443,13 +430,14 @@
     acc_ref = refs[0] if last else out_ref
     left_ref, buf_ref, sem_ref = refs[-3:]
     targets = k0_ref.shape[0]
-    rows = buf_ref.shape[3]
-    copies = {}
+    rows = buf_ref.shape[2]
+    copies, starts = {}, []
     for g, k in enumerate(groups):
         start = pl.multiple_of((lax.axis_index("patch") ^ k) * rows, block) if rows < k0_ref.shape[1] else 0
-        for d, k_ref in enumerate((k0_ref, k1_ref)):
+        starts.append(start)
+        for d, k_ref in enumerate((k0_ref,)):
             copies[g, d] = pltpu.make_async_copy(
-                k_ref.at[:, pl.ds(start, rows), :], buf_ref.at[g, d], sem_ref.at[g, d]
+                k_ref.at[:, pl.ds(start, rows), :], buf_ref.at[g], sem_ref.at[g]
             )
             copies[g, d].start()
     for g, (k, piece_ref) in enumerate(zip(groups, piece_refs)):
@@ -457,12 +445,17 @@
     if not first:
         acc_ref[...] = base_ref[...]
     unit = 2 if targets % 2 == 0 else 1
-    for g in range(count):
-        for d in range(2):
-            copies[g, d].wait()
+    for d in (1, 0):
+        for g in range(count):
+            if d == 0:
+                copies[g, d].wait()
 
             def body(n, carry, g=g, d=d):
-                right = jnp.concatenate([buf_ref[g, d, n * unit + u] for u in range(unit)], 1)
+                if d == 0:
+                    parts = [buf_ref[g, n * unit + u] for u in range(unit)]
+                else:
+                    parts = [k1_ref[n * unit + u, pl.ds(starts[g], rows), :] for u in range(unit)]
+                right = jnp.concatenate(parts, 1)
                 lanes = pl.ds(pl.multiple_of(n * (unit * block), unit * block), unit * block)
                 part = jnp.dot(left_ref[g, d], right, preferred_element_type=F32)
                 acc_ref[d, :, lanes] = part if first and g == 0 else acc_ref[d, :, lanes] + part
@@ -482,6 +475,8 @@
     channels, rows = inc.shape
     targets = k0.shape[0]
     depth = 2 * pieces[0].shape[1]
+    k0 = pltpu.with_memory_space_constraint(k0, pltpu.HBM)
+    k1 = pltpu.with_memory_space_constraint(k1, pltpu.VMEM)
     vmem = pl.BlockSpec(memory_space=pltpu.VMEM)
     table = pl.BlockSpec(memory_space=pl.ANY)
     extra = [] if base is None else [base]
@@ -489,20 +484,20 @@
     return pl.pallas_call(
         functools.partial(sweep_kernel, groups, block, scale, base is None, last),
         out_shape=jax.ShapeDtypeStruct(inc.shape, BF) if last else sums,
-        in_specs=[vmem] * 6 + [table] * 2 + [vmem] * (len(pieces) + len(extra)),
+        in_specs=[vmem] * 6 + [table, vmem] + [vmem] * (len(pieces) + len(extra)),
         out_specs=vmem,
         scratch_shapes=([pltpu.VMEM(sums.shape, F32)] if last else [])
         + [
             pltpu.VMEM((len(groups), 2, channels, depth), BF),
-            pltpu.VMEM((len(groups), 2, targets, depth, block), BF),
-            pltpu.SemaphoreType.DMA((len(groups), 2)),
+            pltpu.VMEM((len(groups), targets, depth, block), BF),
+            pltpu.SemaphoreType.DMA((len(groups),)),
         ],
         cost_estimate=pl.CostEstimate(
             flops=4 * len(groups) * channels * rows * depth,
             bytes_accessed=4 * len(groups) * rows * depth,
             transcendentals=0,
         ),
-        compiler_params=pltpu.CompilerParams(vmem_limit_bytes=ROOMY),
+        compiler_params=pltpu.CompilerParams(vmem_limit_bytes=24 * 2**20),
         name="sweep" if last else "own_sweep",
     )(before, after, inc, fore, back, ends, k0, k1, *pieces, *extra)
 

time: 85.2 us -> 84.1 us (0.987)
  Pallas kernels: 63 us -> 59.9 us
  starting transfers between devices: 13.1 us -> 15.4 us
    pallas_call x2, Pallas kernels: 15.1 us -> 11.9 us  [call_sweep(): pl.pallas_call(functools.partial(sweep_kernel, groups, block, scale, base...]
    ppermute x6, starting transfers between devices: 5.51 us -> 7.06 us  [gather_patches(): lax.ppermute(value, 'patch', [(i, i ^ k) for i in range(count)])]
    ppermute x2, waiting for transfers between devices: 6.95 us -> 5.58 us  [neighbours(): lax.ppermute(second, 'seg', moves[1])]
    ppermute x2, starting transfers between devices: 5.78 us -> 7.16 us  [neighbours(): lax.ppermute(second, 'seg', moves[1])]
    ppermute x6, waiting for transfers between devices: 1.71 us -> 3.02 us  [gather_patches(): lax.ppermute(value, 'patch', [(i, i ^ k) for i in range(count)])]
    pallas_call x1, Pallas kernels: 25.8 us -> 26.8 us  [call_build_sweep(): pl.pallas_call(functools.partial(build_sweep_kernel, block, per_chunk, le...]
    pallas_call x1, Pallas kernels: 20.5 us -> 19.6 us  [call_build(): pl.pallas_call(functools.partial(build_kernel, direction, block, per_chun...]
  transfers between devices with their start and end apart: 10 -> 10, of which waited for: 3 -> 4; matrix products, arithmetic and copies ran while one was open for 0% -> 0% of each run, Pallas kernels for 30% -> 27%
where the time goes in v6:
time: 84.1 us
  Pallas kernels  59.9 us (71%)
  starting transfers between devices  15.4 us (18%)
  waiting for transfers between devices  8.6 us (10%)
    pallas_call x1, Pallas kernels, call_build_sweep(): pl.pallas_call(functools.partial(build_sweep_kernel, block, per_chunk, le...  26.8 us
    pallas_call x1, Pallas kernels, call_build(): pl.pallas_call(functools.partial(build_kernel, direction, block, per_chun...  19.6 us
    pallas_call x2, Pallas kernels, call_sweep(): pl.pallas_call(functools.partial(sweep_kernel, groups, block, scale, base...  11.9 us
    ppermute x2, starting transfers between devices, neighbours(): lax.ppermute(second, 'seg', moves[1])  7.16 us
    ppermute x6, starting transfers between devices, gather_patches(): lax.ppermute(value, 'patch', [(i, i ^ k) for i in range(count)])  7.06 us
    ppermute x2, waiting for transfers between devices, neighbours(): lax.ppermute(second, 'seg', moves[1])  5.58 us
    ppermute x6, waiting for transfers between devices, gather_patches(): lax.ppermute(value, 'patch', [(i, i ^ k) for i in range(count)])  3.02 us
  transfers between devices with their start and end apart: 10, of which 4 were waited for; matrix products, arithmetic and copies ran while one was open for 0% of the time, Pallas kernels for 27%

profile of v6, /device:TPU:17, one launch (start us, length us, event | category | flops | bytes accessed | tf_op | source)
XLA Modules:
  0.0 84.1 jit_solution(5683253198427106161)
XLA Ops:
  0.0 0.0 copy-start
  0.0 0.0 copy-start.1
  0.0 1.6 %prep.1 = (f32[48,1024]{1,0:T(8,128)S(1)}, f32[48,1024]{1,0:T(8,128)S(1)}, s32[2,72,4]{2,1,0:T(8,128)S(1)}) custom-call(f32[1,4096]{1,0:T(1,128)} %axial_ref.1, f32[1,4096]{1,0:T(1,128)} %angle_ref.1, f32[1,4096]{1,0:T(1,128)} %area_ref.1, bf16[64,1024]{1,0:T(8,128)(2,1)} %bitcast.2, s32[1,2,8,32]{3,2,1,0:T(8,128)} %vis_ref.1), custom_call_target="tpu_custom_call" | custom-call | tf_op jit(solution)/shard_map/prep/pallas_call | solution.py:159
  1.6 3.8 %collective-permute-start.1 = (f32[48,1024]{1,0:T(8,128)S(1)}, f32[48,1024]{1,0:T(8,128)S(1)}, u32[]{:S(2)}, u32[]{:S(2)}) collective-permute-start(f32[48,1024]{1,0:T(8,128)S(1)} %get-tuple-element.15), channel_id=1, source_target_pairs={{4,8},{12,16},{20,24},{8,4},{16,12},{24,20},{5,9},{13,17},{21,25},... | collective-permute-start | bytes 589832 | tf_op jit(solution)/shard_map/ppermute | solution.py:535
  5.4 0.1 collective-permute-start
  5.5 3.4 %collective-permute-done.1.cross_ref = f32[48,1024]{1,0:T(8,128)S(1)} collective-permute-done((f32[48,1024]{1,0:T(8,128)S(1)}, f32[48,1024]{1,0:T(8,128)S(1)}, u32[]{:S(2)}, u32[]{:S(2)}) %collective-permute-start.1) | collective-permute-done | bytes 196640 | tf_op jit(solution)/shard_map/ppermute | solution.py:535
  8.9 0.0 collective-permute-done.swap_ref
  8.9 2.2 %collective-permute-start.4 = (bf16[64,1024]{1,0:T(8,128)(2,1)S(1)}, bf16[64,1024]{1,0:T(8,128)(2,1)S(1)}, u32[]{:S(2)}, u32[]{:S(2)}) collective-permute-start(bf16[64,1024]{1,0:T(8,128)(2,1)S(1)} %get-tuple-element.19.rest_0_), channel_id=1, source_target_pairs={{0,3},{1,2},{2,1},{3,0},{4,7},{5,6},{6,5},{7,4},{8,11},{9,10},{10,... | collective-permute-start | bytes 393224 | tf_op jit(solution)/shard_map/ppermute | solution.py:543
  11.1 0.2 collective-permute-start.3
  11.4 0.3 collective-permute-start.2
  11.6 19.6 %build0.1.k0_ref.refs_6_ = bf16[8,8192,128]{2,1,0:T(8,128)(2,1)} custom-call(s32[2,72,4]{2,1,0:T(8,128)S(1)} %get-tuple-element.18.list_ref, f32[48,1024]{1,0:T(8,128)S(1)} %get-tuple-element.14.own_ref, f32[16,1024]{1,0:T(8,128)S(1)} %get-tuple-element.16.pack_ref.before_ref.refs_0_), custom_call_target="tpu_custom_call" | custom-call | tf_op jit(solution)/shard_map/build0/pallas_call | solution.py:270
  31.2 0.0 collective-permute-done.4.rest_3_
  31.2 0.0 collective-permute-done.3.rest_2_
  31.2 0.0 collective-permute-done.2.rest_1_
  31.2 0.0 copy-done
  31.2 0.0 copy-done.1
  31.2 26.8 %build_sweep.1 = (bf16[8,8192,128]{2,1,0:T(8,128)(2,1)S(1)}, bf16[32,1024]{1,0:T(8,128)(2,1)S(1)}, bf16[32,1024]{1,0:T(8,128)(2,1)S(1)}) custom-call(s32[2,72,4]{2,1,0:T(8,128)S(1)} %get-tuple-element.18.list_ref, f32[48,1024]{1,0:T(8,128)S(1)} %get-tuple-element.14.own_ref, f32[16,1024]{1,0:T(8,128)S(1)} %get-tuple-element.16.pack_ref.before_ref.refs_0_, ...), custom_call_target="tpu_custom_call" | custom-call | tf_op jit(solution)/shard_map/build_sweep/pallas_call | solution.py:401
  58.1 1.1 %collective-permute-start.5 = (bf16[32,1024]{1,0:T(8,128)(2,1)S(1)}, bf16[32,1024]{1,0:T(8,128)(2,1)S(1)}, u32[]{:S(2)}, u32[]{:S(2)}) collective-permute-start(bf16[32,1024]{1,0:T(8,128)(2,1)S(1)} %get-tuple-element.20.refs_3_), channel_id=1, source_target_pairs={{0,4},{8,12},{16,20},{24,28},{4,0},{12,8},{20,16},{28,24},{1,5},{9... | collective-permute-start | bytes 196616 | tf_op jit(solution)/shard_map/ppermute | solution.py:535
  59.2 3.4 %collective-permute-start.6 = (bf16[32,1024]{1,0:T(8,128)(2,1)S(1)}, bf16[32,1024]{1,0:T(8,128)(2,1)S(1)}, u32[]{:S(2)}, u32[]{:S(2)}) collective-permute-start(bf16[32,1024]{1,0:T(8,128)(2,1)S(1)} %get-tuple-element.21.refs_4_), channel_id=1, source_target_pairs={{4,8},{12,16},{20,24},{8,4},{16,12},{24,20},{5,9},{13,17},{21,25},... | collective-permute-start | bytes 196616 | tf_op jit(solution)/shard_map/ppermute | solution.py:535
  62.6 0.0 collective-permute-done.5.swap_ref
  62.6 2.2 %collective-permute-done.6.cross_ref = bf16[32,1024]{1,0:T(8,128)(2,1)S(1)} collective-permute-done((bf16[32,1024]{1,0:T(8,128)(2,1)S(1)}, bf16[32,1024]{1,0:T(8,128)(2,1)S(1)}, u32[]{:S(2)}, u32[]{:S(2)}) %collective-permute-start.6) | collective-permute-done | bytes 65568 | tf_op jit(solution)/shard_map/ppermute | solution.py:535
  64.8 4.0 %collective-permute-start.9 = (bf16[64,1024]{1,0:T(8,128)(2,1)S(1)}, bf16[64,1024]{1,0:T(8,128)(2,1)S(1)}, u32[]{:S(2)}, u32[]{:S(2)}) collective-permute-start(bf16[64,1024]{1,0:T(8,128)(2,1)S(1)} %join.3.refs_8_), channel_id=1, source_target_pairs={{0,3},{1,2},{2,1},{3,0},{4,7},{5,6},{6,5},{7,4},{8,11},{9,10},{10,... | collective-permute-start | bytes 393224 | tf_op jit(solution)/shard_map/ppermute | solution.py:543
  68.8 0.0 collective-permute-start.8
  68.8 0.4 collective-permute-start.7
  69.2 3.4 %own_sweep.1.refs_11_ = f32[2,64,1024]{2,1,0:T(8,128)S(1)} custom-call(f32[16,1024]{1,0:T(8,128)S(1)} %get-tuple-element.16.pack_ref.before_ref.refs_0_, f32[16,1024]{1,0:T(8,128)S(1)} %get-tuple-element.17.after_ref.refs_1_, bf16[64,1024]{1,0:T(8,128)(2,1)S(1)} %bitcast.4, bf16[32,1024]{1,0:T(8,128)(2,1)S(1)} %get-tuple-element.20.refs_3_, ...), custom_call_target="tpu_custom_call" | custom-call | flops 536870912 | bytes 8388608 | tf_op jit(solution)/shard_map/own_sweep/pallas_call | solution.py:484
  72.6 0.1 collective-permute-done.9.refs_10_
  72.7 2.9 %collective-permute-done.8.refs_9_ = bf16[64,1024]{1,0:T(8,128)(2,1)S(1)} collective-permute-done((bf16[64,1024]{1,0:T(8,128)(2,1)S(1)}, bf16[64,1024]{1,0:T(8,128)(2,1)S(1)}, u32[]{:S(2)}, u32[]{:S(2)}) %collective-permute-start.8) | collective-permute-done | bytes 131104 | tf_op jit(solution)/shard_map/ppermute | solution.py:543
  75.6 0.0 collective-permute-done.7.refs_8_
  75.6 8.5 %sweep.1 = bf16[64,1024]{1,0:T(8,128)(2,1)} custom-call(f32[16,1024]{1,0:T(8,128)S(1)} %get-tuple-element.16.pack_ref.before_ref.refs_0_, f32[16,1024]{1,0:T(8,128)S(1)} %get-tuple-element.17.after_ref.refs_1_, bf16[64,1024]{1,0:T(8,128)(2,1)S(1)} %bitcast.5, bf16[32,1024]{1,0:T(8,128)(2,1)S(1)} %get-tuple-element.20.refs_3_, ...), custom_call_target="tpu_custom_call" | custom-call | flops 1610612736 | bytes 25165824 | tf_op jit(solution)/shard_map/sweep/pallas_call | solution.py:484
  (2 shorter events, 0.1 us)
Async XLA Ops:
  0.0 31.2 %copy-start = (bf16[1,64,1024]{2,1,0:T(8,128)(2,1)S(1)}, bf16[1,64,1024]{2,1,0:T(8,128)(2,1)}, u32[]{:S(2)}) copy-start(bf16[1,64,1024]{2,1,0:T(8,128)(2,1)} %param.6) | copy-start | bytes 393220
  0.0 31.2 %copy-start.1 = (f32[2,32]{1,0:T(2,128)S(1)}, f32[2,32]{1,0:T(2,128)}, u32[]{:S(2)}) copy-start(f32[2,32]{1,0:T(2,128)} %refs_5_.3) | copy-start | bytes 772
  1.6 7.3 %collective-permute-start.1 = (f32[48,1024]{1,0:T(8,128)S(1)}, f32[48,1024]{1,0:T(8,128)S(1)}, u32[]{:S(2)}, u32[]{:S(2)}) collective-permute-start(f32[48,1024]{1,0:T(8,128)S(1)} %get-tuple-element.15), channel_id=1, source_target_pairs={{4,8},{12,16},{20,24},{8,4},{16,12},{24,20},{5,9},{13,17},{21,25},... | collective-permute-start | bytes 589832 | tf_op jit(solution)/shard_map/ppermute | solution.py:535
  5.4 3.5 %collective-permute-start = (f32[48,1024]{1,0:T(8,128)S(1)}, f32[48,1024]{1,0:T(8,128)S(1)}, u32[]{:S(2)}, u32[]{:S(2)}) collective-permute-start(f32[48,1024]{1,0:T(8,128)S(1)} %get-tuple-element.14.own_ref), channel_id=1, source_target_pairs={{0,4},{8,12},{16,20},{24,28},{4,0},{12,8},{20,16},{28,24},{1,5},{9... | collective-permute-start | bytes 589832 | tf_op jit(solution)/shard_map/ppermute | solution.py:535
  8.9 22.3 %collective-permute-start.4 = (bf16[64,1024]{1,0:T(8,128)(2,1)S(1)}, bf16[64,1024]{1,0:T(8,128)(2,1)S(1)}, u32[]{:S(2)}, u32[]{:S(2)}) collective-permute-start(bf16[64,1024]{1,0:T(8,128)(2,1)S(1)} %get-tuple-element.19.rest_0_), channel_id=1, source_target_pairs={{0,3},{1,2},{2,1},{3,0},{4,7},{5,6},{6,5},{7,4},{8,11},{9,10},{10,... | collective-permute-start | bytes 393224 | tf_op jit(solution)/shard_map/ppermute | solution.py:543
  11.1 20.1 %collective-permute-start.3 = (bf16[64,1024]{1,0:T(8,128)(2,1)S(1)}, bf16[64,1024]{1,0:T(8,128)(2,1)S(1)}, u32[]{:S(2)}, u32[]{:S(2)}) collective-permute-start(bf16[64,1024]{1,0:T(8,128)(2,1)S(1)} %get-tuple-element.19.rest_0_), channel_id=1, source_target_pairs={{0,2},{1,3},{2,0},{3,1},{4,6},{5,7},{6,4},{7,5},{8,10},{9,11},{10,... | collective-permute-start | bytes 393224 | tf_op jit(solution)/shard_map/ppermute | solution.py:543
  11.4 19.8 %collective-permute-start.2 = (bf16[64,1024]{1,0:T(8,128)(2,1)S(1)}, bf16[64,1024]{1,0:T(8,128)(2,1)S(1)}, u32[]{:S(2)}, u32[]{:S(2)}) collective-permute-start(bf16[64,1024]{1,0:T(8,128)(2,1)S(1)} %get-tuple-element.19.rest_0_), channel_id=1, source_target_pairs={{0,1},{1,0},{2,3},{3,2},{4,5},{5,4},{6,7},{7,6},{8,9},{9,8},{10,11... | collective-permute-start | bytes 393224 | tf_op jit(solution)/shard_map/ppermute | solution.py:543
  58.1 4.5 %collective-permute-start.5 = (bf16[32,1024]{1,0:T(8,128)(2,1)S(1)}, bf16[32,1024]{1,0:T(8,128)(2,1)S(1)}, u32[]{:S(2)}, u32[]{:S(2)}) collective-permute-start(bf16[32,1024]{1,0:T(8,128)(2,1)S(1)} %get-tuple-element.20.refs_3_), channel_id=1, source_target_pairs={{0,4},{8,12},{16,20},{24,28},{4,0},{12,8},{20,16},{28,24},{1,5},{9... | collective-permute-start | bytes 196616 | tf_op jit(solution)/shard_map/ppermute | solution.py:535
  59.2 5.6 %collective-permute-start.6 = (bf16[32,1024]{1,0:T(8,128)(2,1)S(1)}, bf16[32,1024]{1,0:T(8,128)(2,1)S(1)}, u32[]{:S(2)}, u32[]{:S(2)}) collective-permute-start(bf16[32,1024]{1,0:T(8,128)(2,1)S(1)} %get-tuple-element.21.refs_4_), channel_id=1, source_target_pairs={{4,8},{12,16},{20,24},{8,4},{16,12},{24,20},{5,9},{13,17},{21,25},... | collective-permute-start | bytes 196616 | tf_op jit(solution)/shard_map/ppermute | solution.py:535
  64.8 7.8 %collective-permute-start.9 = (bf16[64,1024]{1,0:T(8,128)(2,1)S(1)}, bf16[64,1024]{1,0:T(8,128)(2,1)S(1)}, u32[]{:S(2)}, u32[]{:S(2)}) collective-permute-start(bf16[64,1024]{1,0:T(8,128)(2,1)S(1)} %join.3.refs_8_), channel_id=1, source_target_pairs={{0,3},{1,2},{2,1},{3,0},{4,7},{5,6},{6,5},{7,4},{8,11},{9,10},{10,... | collective-permute-start | bytes 393224 | tf_op jit(solution)/shard_map/ppermute | solution.py:543
  68.8 6.8 %collective-permute-start.8 = (bf16[64,1024]{1,0:T(8,128)(2,1)S(1)}, bf16[64,1024]{1,0:T(8,128)(2,1)S(1)}, u32[]{:S(2)}, u32[]{:S(2)}) collective-permute-start(bf16[64,1024]{1,0:T(8,128)(2,1)S(1)} %join.3.refs_8_), channel_id=1, source_target_pairs={{0,2},{1,3},{2,0},{3,1},{4,6},{5,7},{6,4},{7,5},{8,10},{9,11},{10,... | collective-permute-start | bytes 393224 | tf_op jit(solution)/shard_map/ppermute | solution.py:543
  68.8 6.8 %collective-permute-start.7 = (bf16[64,1024]{1,0:T(8,128)(2,1)S(1)}, bf16[64,1024]{1,0:T(8,128)(2,1)S(1)}, u32[]{:S(2)}, u32[]{:S(2)}) collective-permute-start(bf16[64,1024]{1,0:T(8,128)(2,1)S(1)} %join.3.refs_8_), channel_id=1, source_target_pairs={{0,1},{1,0},{2,3},{3,2},{4,5},{5,4},{6,7},{7,6},{8,9},{9,8},{10,11... | collective-permute-start | bytes 393224 | tf_op jit(solution)/shard_map/ppermute | solution.py:543

commit v7 on v6

--- a/solution.py
+++ b/solution.py
@@ -26,7 +26,7 @@
                2.476016133696864e-05, -2.605149496508554e-07)
 
 FEATURES = 32
-ROOMY = 50 * 2**20
+ROOMY = 12 * 2**20
 PAIR = 8
 BF = jnp.bfloat16
 F32 = jnp.float32
@@ -251,8 +251,13 @@
         build_features(direction, channels, own_ref, pack_ref, tf_ref, sf_ref)
 
     build_chunk(
-        direction, chunk, block, k_ref.shape[0], list_ref, tf_ref, sf_ref, chunk * (per_chunk * block), k_ref, *q
-    )
+        direction, chunk, block, k_ref.shape[0], list_ref, tf_ref, sf_ref, chunk * (per_chunk * block),
+        rows_of(k_ref, chunk, 2 * per_chunk * block), *q
+    )
+
+
+def rows_of(k_ref, chunk, rows):
+    return k_ref.at[:, pl.ds(pl.multiple_of(chunk * rows, rows), rows), :]
 
 
 def whole(x):
@@ -270,9 +275,9 @@
     return pl.pallas_call(
         functools.partial(build_kernel, direction, block, per_chunk, channels),
         grid=(patches // (block * per_chunk),),
-        out_shape=jax.ShapeDtypeStruct((targets, 2 * patches, block), BF),
+        out_shape=pltpu.VMEM((targets, 2 * patches, block), BF),
         in_specs=[pl.BlockSpec(memory_space=pltpu.SMEM), whole(own), whole(pack)],
-        out_specs=table_spec(targets, chunk_rows, block),
+        out_specs=pl.BlockSpec(memory_space=pltpu.VMEM),
         scratch_shapes=[
             pltpu.VMEM((FEATURES, rows), BF),
             pltpu.VMEM((patches, FEATURES), BF),
@@ -348,27 +353,17 @@
     block, per_chunk, pieces, scale, list_ref, own_ref, before_ref, after_ref, inc_ref, ends_ref, k0_ref, *rest
 ):
     piece_refs = rest[:pieces]
-    k1_ref, fore_ref, back_ref, tf_ref, sf_ref, left_ref, acc_ref, q_ref = rest[pieces : pieces + 8]
-    in_ref, in_sem = rest[pieces + 8 :]
+    k1_ref, kept_ref, fore_ref, back_ref, tf_ref, sf_ref, left_ref, acc_ref, q_ref, sem_ref = rest[pieces:]
     chunk = pl.program_id(0)
     chunks = pl.num_programs(0)
     channels = inc_ref.shape[0] // 2
-    rows = in_ref.shape[2]
-    slot = lax.rem(chunk, 2)
-
-    def fetch(c, place):
-        part = k0_ref.at[:, pl.ds(pl.multiple_of(c * rows, rows), rows), :]
-        return pltpu.make_async_copy(part, in_ref.at[place], in_sem.at[place])
-
-    k_ref = k1_ref.at[:, pl.ds(pl.multiple_of(chunk * rows, rows), rows), :]
+    rows = 2 * per_chunk * block
+    k_ref = rows_of(k1_ref, chunk, rows)
+    keep = pltpu.make_async_copy(k0_ref, kept_ref, sem_ref)
 
     @pl.when(chunk == 0)
     def _():
-        fetch(chunk, slot).start()
-
-    @pl.when(chunk + 1 < chunks)
-    def _():
-        fetch(chunk + 1, 1 - slot).start()
+        keep.start()
 
     @pl.when(chunk == 0)
     def _():
@@ -377,17 +372,17 @@
             load_piece(k, piece_ref, (before_ref, after_ref), left_ref, scale, block)
 
     build_chunk(
-        1, chunk, block, in_ref.shape[1], list_ref, tf_ref, sf_ref, chunk * (per_chunk * block),
+        1, chunk, block, k1_ref.shape[0], list_ref, tf_ref, sf_ref, chunk * (per_chunk * block),
         k_ref, q_ref,
     )
-    fetch(chunk, slot).wait()
-    accumulate(acc_ref, left_ref, chunk, {0: in_ref.at[slot], 1: k_ref})
+    accumulate(acc_ref, left_ref, chunk, {0: rows_of(k0_ref, chunk, rows), 1: k_ref})
 
     @pl.when(chunk == chunks - 1)
     def _():
         state = {}
         finish(acc_ref, inc_ref, (inc_ref[:channels], inc_ref[channels:]), ends_ref, state.__setitem__)
         fore_ref[...], back_ref[...] = by_parity(state[0], state[1])
+        keep.wait()
 
 
 def call_build_sweep(block, per_chunk, scale, patches, lists, own, before, after, inc, ends, k0, pieces):
@@ -396,25 +391,24 @@
     targets = rows // block
     channels = inc.shape[0]
     part = jax.ShapeDtypeStruct((channels // 2, rows), BF)
-    k0 = pltpu.with_memory_space_constraint(k0, pltpu.HBM)
-    table = pl.BlockSpec(memory_space=pl.ANY)
+    k0 = pltpu.with_memory_space_constraint(k0, pltpu.VMEM)
+    table = pl.BlockSpec(memory_space=pltpu.VMEM)
     return pl.pallas_call(
         functools.partial(build_sweep_kernel, block, per_chunk, len(pieces), scale),
         grid=(patches // (block * per_chunk),),
-        out_shape=(pltpu.VMEM(k0.shape, BF), part, part),
+        out_shape=(pltpu.VMEM(k0.shape, BF), jax.ShapeDtypeStruct(k0.shape, BF), part, part),
         in_specs=[pl.BlockSpec(memory_space=pltpu.SMEM), whole(own), whole(before), whole(after), whole(inc),
                   whole(ends), table] + [whole(p) for p in pieces],
-        out_specs=(pl.BlockSpec(memory_space=pltpu.VMEM), whole(part), whole(part)),
+        out_specs=(table, pl.BlockSpec(memory_space=pl.ANY), whole(part), whole(part)),
         scratch_shapes=[
             pltpu.VMEM((FEATURES, rows), BF),
             pltpu.VMEM((patches, FEATURES), BF),
             pltpu.VMEM((2, channels, 2 * patches), BF),
             pltpu.VMEM((2, channels, rows), F32),
             pltpu.VMEM((PAIR * block, block), F32),
-            pltpu.VMEM((2, targets, chunk_rows, block), BF),
-            pltpu.SemaphoreType.DMA((2,)),
+            pltpu.SemaphoreType.DMA,
         ],
-        compiler_params=pltpu.CompilerParams(dimension_semantics=("arbitrary",), vmem_limit_bytes=24 * 2**20),
+        compiler_params=pltpu.CompilerParams(dimension_semantics=("arbitrary",), vmem_limit_bytes=12 * 2**20),
         name="build_sweep",
     )(lists, own, before, after, inc, ends, k0, *pieces)
 
@@ -556,7 +550,7 @@
     moved, before, after = join(*neighbours(own, other), channels)
     pieces = gather_patches(moved)
     k0 = call_build(0, block, per_chunk, half, lists, own, before, patches)
-    k1, first, second = call_build_sweep(
+    k1, k0, first, second = call_build_sweep(
         block, per_chunk, scale, patches, lists, own, before, after, inc, end_reflection, k0, pieces
     )
     for sweep in range(1, ITERS):

time: 84.1 us -> 82.2 us (0.977)
  Pallas kernels: 59.9 us -> 57.5 us
    pallas_call x1, Pallas kernels: 19.6 us -> 17.4 us  [call_build(): pl.pallas_call(functools.partial(build_kernel, direction, block, per_chun...]
  transfers between devices with their start and end apart: 10 -> 10, of which waited for: 4 -> 4; matrix products, arithmetic and copies ran while one was open for 0% -> 0% of each run, Pallas kernels for 27% -> 25%
where the time goes in v7:
time: 82.2 us; the launch traced here: 82 us
  Pallas kernels  57.5 us (70%)
  starting transfers between devices  15.8 us (19%)
  waiting for transfers between devices  8.55 us (10%)
    pallas_call x1, Pallas kernels, call_build_sweep(): pl.pallas_call(functools.partial(build_sweep_kernel, block, per_chunk, le...  26.5 us
    pallas_call x1, Pallas kernels, call_build(): pl.pallas_call(functools.partial(build_kernel, direction, block, per_chun...  17.4 us
    pallas_call x2, Pallas kernels, call_sweep(): pl.pallas_call(functools.partial(sweep_kernel, groups, block, scale, base...  11.9 us
    ppermute x2, starting transfers between devices, neighbours(): lax.ppermute(second, 'seg', moves[1])  7.18 us
    ppermute x6, starting transfers between devices, gather_patches(): lax.ppermute(value, 'patch', [(i, i ^ k) for i in range(count)])  6.65 us
    ppermute x2, waiting for transfers between devices, neighbours(): lax.ppermute(second, 'seg', moves[1])  5.56 us
    ppermute x6, waiting for transfers between devices, gather_patches(): lax.ppermute(value, 'patch', [(i, i ^ k) for i in range(count)])  2.99 us
    ppermute x2, starting transfers between devices, neighbours(): lax.ppermute(first, 'seg', moves[0])  1.98 us
  transfers between devices with their start and end apart: 10, of which 4 were waited for; matrix products, arithmetic and copies ran while one was open for 0% of the time, Pallas kernels for 25%

profile of v7, /device:TPU:17, one launch (start us, length us, event | category | flops | bytes accessed | tf_op | source)
XLA Modules:
  0.0 82.0 jit_solution(589170491734580875)
XLA Ops:
  0.0 0.0 copy-start
  0.0 0.0 copy-start.1
  0.0 1.6 %prep.1 = (f32[48,1024]{1,0:T(8,128)S(1)}, f32[48,1024]{1,0:T(8,128)S(1)}, s32[2,72,4]{2,1,0:T(8,128)S(1)}) custom-call(f32[1,4096]{1,0:T(1,128)} %axial_ref.1, f32[1,4096]{1,0:T(1,128)} %angle_ref.1, f32[1,4096]{1,0:T(1,128)} %area_ref.1, bf16[64,1024]{1,0:T(8,128)(2,1)} %bitcast.2, s32[1,2,8,32]{3,2,1,0:T(8,128)} %vis_ref.1), custom_call_target="tpu_custom_call" | custom-call | tf_op jit(solution)/shard_map/prep/pallas_call | solution.py:159
  1.6 3.8 %collective-permute-start.1 = (f32[48,1024]{1,0:T(8,128)S(1)}, f32[48,1024]{1,0:T(8,128)S(1)}, u32[]{:S(2)}, u32[]{:S(2)}) collective-permute-start(f32[48,1024]{1,0:T(8,128)S(1)} %get-tuple-element.16), channel_id=1, source_target_pairs={{4,8},{12,16},{20,24},{8,4},{16,12},{24,20},{5,9},{13,17},{21,25},... | collective-permute-start | bytes 589832 | tf_op jit(solution)/shard_map/ppermute | solution.py:529
  5.4 0.1 collective-permute-start
  5.5 3.4 %collective-permute-done.1.cross_ref = f32[48,1024]{1,0:T(8,128)S(1)} collective-permute-done((f32[48,1024]{1,0:T(8,128)S(1)}, f32[48,1024]{1,0:T(8,128)S(1)}, u32[]{:S(2)}, u32[]{:S(2)}) %collective-permute-start.1) | collective-permute-done | bytes 196640 | tf_op jit(solution)/shard_map/ppermute | solution.py:529
  8.9 0.0 collective-permute-done.swap_ref
  8.9 2.2 %collective-permute-start.4 = (bf16[64,1024]{1,0:T(8,128)(2,1)S(1)}, bf16[64,1024]{1,0:T(8,128)(2,1)S(1)}, u32[]{:S(2)}, u32[]{:S(2)}) collective-permute-start(bf16[64,1024]{1,0:T(8,128)(2,1)S(1)} %get-tuple-element.20.rest_0_), channel_id=1, source_target_pairs={{0,3},{1,2},{2,1},{3,0},{4,7},{5,6},{6,5},{7,4},{8,11},{9,10},{10,... | collective-permute-start | bytes 393224 | tf_op jit(solution)/shard_map/ppermute | solution.py:537
  11.2 0.2 collective-permute-start.3
  11.4 0.3 collective-permute-start.2
  11.6 17.4 %build0.1.k0_ref = bf16[8,8192,128]{2,1,0:T(8,128)(2,1)S(1)} custom-call(s32[2,72,4]{2,1,0:T(8,128)S(1)} %get-tuple-element.19.list_ref, f32[48,1024]{1,0:T(8,128)S(1)} %get-tuple-element.15.own_ref, f32[16,1024]{1,0:T(8,128)S(1)} %get-tuple-element.17.pack_ref.before_ref.refs_0_), custom_call_target="tpu_custom_call" | custom-call | tf_op jit(solution)/shard_map/build0/pallas_call | solution.py:275
  29.1 0.0 collective-permute-done.4.rest_3_
  29.1 0.0 collective-permute-done.3.rest_2_
  29.1 0.0 collective-permute-done.2.rest_1_
  29.1 0.0 copy-done
  29.1 0.0 copy-done.1
  29.1 26.5 %build_sweep.1 = (bf16[8,8192,128]{2,1,0:T(8,128)(2,1)S(1)}, bf16[8,8192,128]{2,1,0:T(8,128)(2,1)}, bf16[32,1024]{1,0:T(8,128)(2,1)S(1)}, bf16[32,1024]{1,0:T(8,128)(2,1)S(1)}) custom-call(s32[2,72,4]{2,1,0:T(8,128)S(1)} %get-tuple-element.19.list_ref, f32[48,1024]{1,0:T(8,128)S(1)} %get-tuple-element.15.own_ref, ...), custom_call_target="tpu_custom_call" | custom-call | tf_op jit(solution)/shard_map/build_sweep/pallas_call | solution.py:396
  55.7 1.9 %collective-permute-start.5 = (bf16[32,1024]{1,0:T(8,128)(2,1)S(1)}, bf16[32,1024]{1,0:T(8,128)(2,1)S(1)}, u32[]{:S(2)}, u32[]{:S(2)}) collective-permute-start(bf16[32,1024]{1,0:T(8,128)(2,1)S(1)} %get-tuple-element.21.refs_3_), channel_id=1, source_target_pairs={{0,4},{8,12},{16,20},{24,28},{4,0},{12,8},{20,16},{28,24},{1,5},{9... | collective-permute-start | bytes 196616 | tf_op jit(solution)/shard_map/ppermute | solution.py:529
  57.6 3.4 %collective-permute-start.6 = (bf16[32,1024]{1,0:T(8,128)(2,1)S(1)}, bf16[32,1024]{1,0:T(8,128)(2,1)S(1)}, u32[]{:S(2)}, u32[]{:S(2)}) collective-permute-start(bf16[32,1024]{1,0:T(8,128)(2,1)S(1)} %get-tuple-element.22.refs_4_), channel_id=1, source_target_pairs={{4,8},{12,16},{20,24},{8,4},{16,12},{24,20},{5,9},{13,17},{21,25},... | collective-permute-start | bytes 196616 | tf_op jit(solution)/shard_map/ppermute | solution.py:529
  61.0 0.0 collective-permute-done.5.swap_ref
  61.0 2.1 %collective-permute-done.6.cross_ref = bf16[32,1024]{1,0:T(8,128)(2,1)S(1)} collective-permute-done((bf16[32,1024]{1,0:T(8,128)(2,1)S(1)}, bf16[32,1024]{1,0:T(8,128)(2,1)S(1)}, u32[]{:S(2)}, u32[]{:S(2)}) %collective-permute-start.6) | collective-permute-done | bytes 65568 | tf_op jit(solution)/shard_map/ppermute | solution.py:529
  63.2 1.8 %collective-permute-start.9 = (bf16[64,1024]{1,0:T(8,128)(2,1)S(1)}, bf16[64,1024]{1,0:T(8,128)(2,1)S(1)}, u32[]{:S(2)}, u32[]{:S(2)}) collective-permute-start(bf16[64,1024]{1,0:T(8,128)(2,1)S(1)} %join.3.refs_8_), channel_id=1, source_target_pairs={{0,3},{1,2},{2,1},{3,0},{4,7},{5,6},{6,5},{7,4},{8,11},{9,10},{10,... | collective-permute-start | bytes 393224 | tf_op jit(solution)/shard_map/ppermute | solution.py:537
  65.0 1.0 %collective-permute-start.8 = (bf16[64,1024]{1,0:T(8,128)(2,1)S(1)}, bf16[64,1024]{1,0:T(8,128)(2,1)S(1)}, u32[]{:S(2)}, u32[]{:S(2)}) collective-permute-start(bf16[64,1024]{1,0:T(8,128)(2,1)S(1)} %join.3.refs_8_), channel_id=1, source_target_pairs={{0,2},{1,3},{2,0},{3,1},{4,6},{5,7},{6,4},{7,5},{8,10},{9,11},{10,... | collective-permute-start | bytes 393224 | tf_op jit(solution)/shard_map/ppermute | solution.py:537
  66.0 1.1 %collective-permute-start.7 = (bf16[64,1024]{1,0:T(8,128)(2,1)S(1)}, bf16[64,1024]{1,0:T(8,128)(2,1)S(1)}, u32[]{:S(2)}, u32[]{:S(2)}) collective-permute-start(bf16[64,1024]{1,0:T(8,128)(2,1)S(1)} %join.3.refs_8_), channel_id=1, source_target_pairs={{0,1},{1,0},{2,3},{3,2},{4,5},{5,4},{6,7},{7,6},{8,9},{9,8},{10,11... | collective-permute-start | bytes 393224 | tf_op jit(solution)/shard_map/ppermute | solution.py:537
  67.1 3.4 %own_sweep.1.refs_11_ = f32[2,64,1024]{2,1,0:T(8,128)S(1)} custom-call(f32[16,1024]{1,0:T(8,128)S(1)} %get-tuple-element.17.pack_ref.before_ref.refs_0_, f32[16,1024]{1,0:T(8,128)S(1)} %get-tuple-element.18.after_ref.refs_1_, bf16[64,1024]{1,0:T(8,128)(2,1)S(1)} %bitcast.4, bf16[32,1024]{1,0:T(8,128)(2,1)S(1)} %get-tuple-element.21.refs_3_, ...), custom_call_target="tpu_custom_call" | custom-call | flops 536870912 | bytes 8388608 | tf_op jit(solution)/shard_map/own_sweep/pallas_call | solution.py:478
  70.5 0.0 collective-permute-done.9.refs_10_
  70.6 1.9 %collective-permute-done.8.refs_9_ = bf16[64,1024]{1,0:T(8,128)(2,1)S(1)} collective-permute-done((bf16[64,1024]{1,0:T(8,128)(2,1)S(1)}, bf16[64,1024]{1,0:T(8,128)(2,1)S(1)}, u32[]{:S(2)}, u32[]{:S(2)}) %collective-permute-start.8) | collective-permute-done | bytes 131104 | tf_op jit(solution)/shard_map/ppermute | solution.py:537
  72.5 1.1 %collective-permute-done.7.refs_8_ = bf16[64,1024]{1,0:T(8,128)(2,1)S(1)} collective-permute-done((bf16[64,1024]{1,0:T(8,128)(2,1)S(1)}, bf16[64,1024]{1,0:T(8,128)(2,1)S(1)}, u32[]{:S(2)}, u32[]{:S(2)}) %collective-permute-start.7) | collective-permute-done | bytes 131104 | tf_op jit(solution)/shard_map/ppermute | solution.py:537
  73.5 8.5 %sweep.1 = bf16[64,1024]{1,0:T(8,128)(2,1)} custom-call(f32[16,1024]{1,0:T(8,128)S(1)} %get-tuple-element.17.pack_ref.before_ref.refs_0_, f32[16,1024]{1,0:T(8,128)S(1)} %get-tuple-element.18.after_ref.refs_1_, bf16[64,1024]{1,0:T(8,128)(2,1)S(1)} %bitcast.5, bf16[32,1024]{1,0:T(8,128)(2,1)S(1)} %get-tuple-element.21.refs_3_, ...), custom_call_target="tpu_custom_call" | custom-call | flops 1610612736 | bytes 25165824 | tf_op jit(solution)/shard_map/sweep/pallas_call | solution.py:478
  (2 shorter events, 0.1 us)
Async XLA Ops:
  0.0 29.1 %copy-start = (bf16[1,64,1024]{2,1,0:T(8,128)(2,1)S(1)}, bf16[1,64,1024]{2,1,0:T(8,128)(2,1)}, u32[]{:S(2)}) copy-start(bf16[1,64,1024]{2,1,0:T(8,128)(2,1)} %param.6) | copy-start | bytes 393220
  0.0 29.1 %copy-start.1 = (f32[2,32]{1,0:T(2,128)S(1)}, f32[2,32]{1,0:T(2,128)}, u32[]{:S(2)}) copy-start(f32[2,32]{1,0:T(2,128)} %refs_5_.3) | copy-start | bytes 772
  1.6 7.3 %collective-permute-start.1 = (f32[48,1024]{1,0:T(8,128)S(1)}, f32[48,1024]{1,0:T(8,128)S(1)}, u32[]{:S(2)}, u32[]{:S(2)}) collective-permute-start(f32[48,1024]{1,0:T(8,128)S(1)} %get-tuple-element.16), channel_id=1, source_target_pairs={{4,8},{12,16},{20,24},{8,4},{16,12},{24,20},{5,9},{13,17},{21,25},... | collective-permute-start | bytes 589832 | tf_op jit(solution)/shard_map/ppermute | solution.py:529
  5.4 3.5 %collective-permute-start = (f32[48,1024]{1,0:T(8,128)S(1)}, f32[48,1024]{1,0:T(8,128)S(1)}, u32[]{:S(2)}, u32[]{:S(2)}) collective-permute-start(f32[48,1024]{1,0:T(8,128)S(1)} %get-tuple-element.15.own_ref), channel_id=1, source_target_pairs={{0,4},{8,12},{16,20},{24,28},{4,0},{12,8},{20,16},{28,24},{1,5},{9... | collective-permute-start | bytes 589832 | tf_op jit(solution)/shard_map/ppermute | solution.py:529
  8.9 20.2 %collective-permute-start.4 = (bf16[64,1024]{1,0:T(8,128)(2,1)S(1)}, bf16[64,1024]{1,0:T(8,128)(2,1)S(1)}, u32[]{:S(2)}, u32[]{:S(2)}) collective-permute-start(bf16[64,1024]{1,0:T(8,128)(2,1)S(1)} %get-tuple-element.20.rest_0_), channel_id=1, source_target_pairs={{0,3},{1,2},{2,1},{3,0},{4,7},{5,6},{6,5},{7,4},{8,11},{9,10},{10,... | collective-permute-start | bytes 393224 | tf_op jit(solution)/shard_map/ppermute | solution.py:537
  11.2 17.9 %collective-permute-start.3 = (bf16[64,1024]{1,0:T(8,128)(2,1)S(1)}, bf16[64,1024]{1,0:T(8,128)(2,1)S(1)}, u32[]{:S(2)}, u32[]{:S(2)}) collective-permute-start(bf16[64,1024]{1,0:T(8,128)(2,1)S(1)} %get-tuple-element.20.rest_0_), channel_id=1, source_target_pairs={{0,2},{1,3},{2,0},{3,1},{4,6},{5,7},{6,4},{7,5},{8,10},{9,11},{10,... | collective-permute-start | bytes 393224 | tf_op jit(solution)/shard_map/ppermute | solution.py:537
  11.4 17.7 %collective-permute-start.2 = (bf16[64,1024]{1,0:T(8,128)(2,1)S(1)}, bf16[64,1024]{1,0:T(8,128)(2,1)S(1)}, u32[]{:S(2)}, u32[]{:S(2)}) collective-permute-start(bf16[64,1024]{1,0:T(8,128)(2,1)S(1)} %get-tuple-element.20.rest_0_), channel_id=1, source_target_pairs={{0,1},{1,0},{2,3},{3,2},{4,5},{5,4},{6,7},{7,6},{8,9},{9,8},{10,11... | collective-permute-start | bytes 393224 | tf_op jit(solution)/shard_map/ppermute | solution.py:537
  55.7 5.3 %collective-permute-start.5 = (bf16[32,1024]{1,0:T(8,128)(2,1)S(1)}, bf16[32,1024]{1,0:T(8,128)(2,1)S(1)}, u32[]{:S(2)}, u32[]{:S(2)}) collective-permute-start(bf16[32,1024]{1,0:T(8,128)(2,1)S(1)} %get-tuple-element.21.refs_3_), channel_id=1, source_target_pairs={{0,4},{8,12},{16,20},{24,28},{4,0},{12,8},{20,16},{28,24},{1,5},{9... | collective-permute-start | bytes 196616 | tf_op jit(solution)/shard_map/ppermute | solution.py:529
  57.6 5.6 %collective-permute-start.6 = (bf16[32,1024]{1,0:T(8,128)(2,1)S(1)}, bf16[32,1024]{1,0:T(8,128)(2,1)S(1)}, u32[]{:S(2)}, u32[]{:S(2)}) collective-permute-start(bf16[32,1024]{1,0:T(8,128)(2,1)S(1)} %get-tuple-element.22.refs_4_), channel_id=1, source_target_pairs={{4,8},{12,16},{20,24},{8,4},{16,12},{24,20},{5,9},{13,17},{21,25},... | collective-permute-start | bytes 196616 | tf_op jit(solution)/shard_map/ppermute | solution.py:529
  63.2 7.4 %collective-permute-start.9 = (bf16[64,1024]{1,0:T(8,128)(2,1)S(1)}, bf16[64,1024]{1,0:T(8,128)(2,1)S(1)}, u32[]{:S(2)}, u32[]{:S(2)}) collective-permute-start(bf16[64,1024]{1,0:T(8,128)(2,1)S(1)} %join.3.refs_8_), channel_id=1, source_target_pairs={{0,3},{1,2},{2,1},{3,0},{4,7},{5,6},{6,5},{7,4},{8,11},{9,10},{10,... | collective-permute-start | bytes 393224 | tf_op jit(solution)/shard_map/ppermute | solution.py:537
  65.0 7.5 %collective-permute-start.8 = (bf16[64,1024]{1,0:T(8,128)(2,1)S(1)}, bf16[64,1024]{1,0:T(8,128)(2,1)S(1)}, u32[]{:S(2)}, u32[]{:S(2)}) collective-permute-start(bf16[64,1024]{1,0:T(8,128)(2,1)S(1)} %join.3.refs_8_), channel_id=1, source_target_pairs={{0,2},{1,3},{2,0},{3,1},{4,6},{5,7},{6,4},{7,5},{8,10},{9,11},{10,... | collective-permute-start | bytes 393224 | tf_op jit(solution)/shard_map/ppermute | solution.py:537
  66.0 7.5 %collective-permute-start.7 = (bf16[64,1024]{1,0:T(8,128)(2,1)S(1)}, bf16[64,1024]{1,0:T(8,128)(2,1)S(1)}, u32[]{:S(2)}, u32[]{:S(2)}) collective-permute-start(bf16[64,1024]{1,0:T(8,128)(2,1)S(1)} %join.3.refs_8_), channel_id=1, source_target_pairs={{0,1},{1,0},{2,3},{3,2},{4,5},{5,4},{6,7},{7,6},{8,9},{9,8},{10,11... | collective-permute-start | bytes 393224 | tf_op jit(solution)/shard_map/ppermute | solution.py:537

commit v8 on v7

--- a/solution.py
+++ b/solution.py
@@ -346,7 +346,7 @@
             acc_ref[d, :, lanes] = jnp.where(chunk == 0, part, acc_ref[d, :, lanes] + part)
         return carry
 
-    lax.fori_loop(0, targets // group, body, 0)
+    lax.fori_loop(0, targets // group, body, 0, unroll=True)
 
 
 def build_sweep_kernel(
@@ -455,7 +455,7 @@
                 acc_ref[d, :, lanes] = part if first and g == 0 else acc_ref[d, :, lanes] + part
                 return carry
 
-            lax.fori_loop(0, targets // unit, body, 0)
+            lax.fori_loop(0, targets // unit, body, 0, unroll=2)
     if last:
         half = out_ref.shape[0] // 2
 

time: 82.2 us -> 79 us (0.961)
  Pallas kernels: 57.5 us -> 54.2 us
  starting transfers between devices: 15.8 us -> 14.7 us
    pallas_call x2, Pallas kernels: 11.9 us -> 10.2 us  [call_sweep(): pl.pallas_call(functools.partial(sweep_kernel, groups, block, scale, base...]
    ppermute x6, starting transfers between devices: 6.65 us -> 5.43 us  [gather_patches(): lax.ppermute(value, 'patch', [(i, i ^ k) for i in range(count)])]
    pallas_call x1, Pallas kernels: 26.5 us -> 25.3 us  [call_build_sweep(): pl.pallas_call(functools.partial(build_sweep_kernel, block, per_chunk, le...]
  transfers between devices with their start and end apart: 10 -> 10, of which waited for: 4 -> 4; matrix products, arithmetic and copies ran while one was open for 0% -> 0% of each run, Pallas kernels for 25% -> 26%
where the time goes in v8:
time: 79 us; the launch traced here: 78.1 us
  Pallas kernels  54.2 us (69%)
  starting transfers between devices  14.7 us (19%)
  waiting for transfers between devices  9.13 us (12%)
    pallas_call x1, Pallas kernels, call_build_sweep(): pl.pallas_call(functools.partial(build_sweep_kernel, block, per_chunk, le...  25.3 us
    pallas_call x1, Pallas kernels, call_build(): pl.pallas_call(functools.partial(build_kernel, direction, block, per_chun...  17 us
    pallas_call x2, Pallas kernels, call_sweep(): pl.pallas_call(functools.partial(sweep_kernel, groups, block, scale, base...  10.2 us
    ppermute x2, starting transfers between devices, neighbours(): lax.ppermute(second, 'seg', moves[1])  6.93 us
    ppermute x2, waiting for transfers between devices, neighbours(): lax.ppermute(second, 'seg', moves[1])  5.81 us
    ppermute x6, starting transfers between devices, gather_patches(): lax.ppermute(value, 'patch', [(i, i ^ k) for i in range(count)])  5.43 us
    ppermute x6, waiting for transfers between devices, gather_patches(): lax.ppermute(value, 'patch', [(i, i ^ k) for i in range(count)])  3.32 us
    ppermute x2, starting transfers between devices, neighbours(): lax.ppermute(first, 'seg', moves[0])  2.3 us
  transfers between devices with their start and end apart: 10, of which 4 were waited for; matrix products, arithmetic and copies ran while one was open for 0% of the time, Pallas kernels for 26%

profile of v8, /device:TPU:17, one launch (start us, length us, event | category | flops | bytes accessed | tf_op | source)
XLA Modules:
  0.0 78.1 jit_solution(11466028978056228702)
XLA Ops:
  0.0 0.0 copy-start
  0.0 0.0 copy-start.1
  0.0 1.6 %prep.1 = (f32[48,1024]{1,0:T(8,128)S(1)}, f32[48,1024]{1,0:T(8,128)S(1)}, s32[2,72,4]{2,1,0:T(8,128)S(1)}) custom-call(f32[1,4096]{1,0:T(1,128)} %axial_ref.1, f32[1,4096]{1,0:T(1,128)} %angle_ref.1, f32[1,4096]{1,0:T(1,128)} %area_ref.1, bf16[64,1024]{1,0:T(8,128)(2,1)} %bitcast.2, s32[1,2,8,32]{3,2,1,0:T(8,128)} %vis_ref.1), custom_call_target="tpu_custom_call" | custom-call | tf_op jit(solution)/shard_map/prep/pallas_call | solution.py:159
  1.6 3.8 %collective-permute-start.1 = (f32[48,1024]{1,0:T(8,128)S(1)}, f32[48,1024]{1,0:T(8,128)S(1)}, u32[]{:S(2)}, u32[]{:S(2)}) collective-permute-start(f32[48,1024]{1,0:T(8,128)S(1)} %get-tuple-element.16), channel_id=1, source_target_pairs={{4,8},{12,16},{20,24},{8,4},{16,12},{24,20},{5,9},{13,17},{21,25},... | collective-permute-start | bytes 589832 | tf_op jit(solution)/shard_map/ppermute | solution.py:529
  5.4 0.1 collective-permute-start
  5.5 3.4 %collective-permute-done.1.cross_ref = f32[48,1024]{1,0:T(8,128)S(1)} collective-permute-done((f32[48,1024]{1,0:T(8,128)S(1)}, f32[48,1024]{1,0:T(8,128)S(1)}, u32[]{:S(2)}, u32[]{:S(2)}) %collective-permute-start.1) | collective-permute-done | bytes 196640 | tf_op jit(solution)/shard_map/ppermute | solution.py:529
  8.9 0.0 collective-permute-done.swap_ref
  8.9 2.2 %collective-permute-start.4 = (bf16[64,1024]{1,0:T(8,128)(2,1)S(1)}, bf16[64,1024]{1,0:T(8,128)(2,1)S(1)}, u32[]{:S(2)}, u32[]{:S(2)}) collective-permute-start(bf16[64,1024]{1,0:T(8,128)(2,1)S(1)} %get-tuple-element.20.rest_0_), channel_id=1, source_target_pairs={{0,3},{1,2},{2,1},{3,0},{4,7},{5,6},{6,5},{7,4},{8,11},{9,10},{10,... | collective-permute-start | bytes 393224 | tf_op jit(solution)/shard_map/ppermute | solution.py:537
  11.2 0.2 collective-permute-start.3
  11.4 0.3 collective-permute-start.2
  11.6 17.0 %build0.1.k0_ref = bf16[8,8192,128]{2,1,0:T(8,128)(2,1)S(1)} custom-call(s32[2,72,4]{2,1,0:T(8,128)S(1)} %get-tuple-element.19.list_ref, f32[48,1024]{1,0:T(8,128)S(1)} %get-tuple-element.15.own_ref, f32[16,1024]{1,0:T(8,128)S(1)} %get-tuple-element.17.pack_ref.before_ref.refs_0_), custom_call_target="tpu_custom_call" | custom-call | tf_op jit(solution)/shard_map/build0/pallas_call | solution.py:275
  28.7 0.0 collective-permute-done.4.rest_3_
  28.7 0.0 collective-permute-done.3.rest_2_
  28.7 0.0 collective-permute-done.2.rest_1_
  28.7 0.0 copy-done
  28.7 0.0 copy-done.1
  28.7 25.3 %build_sweep.1 = (bf16[8,8192,128]{2,1,0:T(8,128)(2,1)S(1)}, bf16[8,8192,128]{2,1,0:T(8,128)(2,1)}, bf16[32,1024]{1,0:T(8,128)(2,1)S(1)}, bf16[32,1024]{1,0:T(8,128)(2,1)S(1)}) custom-call(s32[2,72,4]{2,1,0:T(8,128)S(1)} %get-tuple-element.19.list_ref, f32[48,1024]{1,0:T(8,128)S(1)} %get-tuple-element.15.own_ref, ...), custom_call_target="tpu_custom_call" | custom-call | tf_op jit(solution)/shard_map/build_sweep/pallas_call | solution.py:396
  54.0 2.2 %collective-permute-start.5 = (bf16[32,1024]{1,0:T(8,128)(2,1)S(1)}, bf16[32,1024]{1,0:T(8,128)(2,1)S(1)}, u32[]{:S(2)}, u32[]{:S(2)}) collective-permute-start(bf16[32,1024]{1,0:T(8,128)(2,1)S(1)} %get-tuple-element.21.refs_3_), channel_id=1, source_target_pairs={{0,4},{8,12},{16,20},{24,28},{4,0},{12,8},{20,16},{28,24},{1,5},{9... | collective-permute-start | bytes 196616 | tf_op jit(solution)/shard_map/ppermute | solution.py:529
  56.3 3.2 %collective-permute-start.6 = (bf16[32,1024]{1,0:T(8,128)(2,1)S(1)}, bf16[32,1024]{1,0:T(8,128)(2,1)S(1)}, u32[]{:S(2)}, u32[]{:S(2)}) collective-permute-start(bf16[32,1024]{1,0:T(8,128)(2,1)S(1)} %get-tuple-element.22.refs_4_), channel_id=1, source_target_pairs={{4,8},{12,16},{20,24},{8,4},{16,12},{24,20},{5,9},{13,17},{21,25},... | collective-permute-start | bytes 196616 | tf_op jit(solution)/shard_map/ppermute | solution.py:529
  59.5 0.0 collective-permute-done.5.swap_ref
  59.5 2.4 %collective-permute-done.6.cross_ref = bf16[32,1024]{1,0:T(8,128)(2,1)S(1)} collective-permute-done((bf16[32,1024]{1,0:T(8,128)(2,1)S(1)}, bf16[32,1024]{1,0:T(8,128)(2,1)S(1)}, u32[]{:S(2)}, u32[]{:S(2)}) %collective-permute-start.6) | collective-permute-done | bytes 65568 | tf_op jit(solution)/shard_map/ppermute | solution.py:529
  61.9 2.1 %collective-permute-start.9 = (bf16[64,1024]{1,0:T(8,128)(2,1)S(1)}, bf16[64,1024]{1,0:T(8,128)(2,1)S(1)}, u32[]{:S(2)}, u32[]{:S(2)}) collective-permute-start(bf16[64,1024]{1,0:T(8,128)(2,1)S(1)} %join.3.refs_8_), channel_id=1, source_target_pairs={{0,3},{1,2},{2,1},{3,0},{4,7},{5,6},{6,5},{7,4},{8,11},{9,10},{10,... | collective-permute-start | bytes 393224 | tf_op jit(solution)/shard_map/ppermute | solution.py:537
  64.0 0.0 collective-permute-start.8
  64.0 0.6 collective-permute-start.7
  64.6 3.2 %own_sweep.1.refs_11_ = f32[2,64,1024]{2,1,0:T(8,128)S(1)} custom-call(f32[16,1024]{1,0:T(8,128)S(1)} %get-tuple-element.17.pack_ref.before_ref.refs_0_, f32[16,1024]{1,0:T(8,128)S(1)} %get-tuple-element.18.after_ref.refs_1_, bf16[64,1024]{1,0:T(8,128)(2,1)S(1)} %bitcast.4, bf16[32,1024]{1,0:T(8,128)(2,1)S(1)} %get-tuple-element.21.refs_3_, ...), custom_call_target="tpu_custom_call" | custom-call | flops 536870912 | bytes 8388608 | tf_op jit(solution)/shard_map/own_sweep/pallas_call | solution.py:478
  67.8 0.1 collective-permute-done.9.refs_10_
  67.9 3.2 %collective-permute-done.8.refs_9_ = bf16[64,1024]{1,0:T(8,128)(2,1)S(1)} collective-permute-done((bf16[64,1024]{1,0:T(8,128)(2,1)S(1)}, bf16[64,1024]{1,0:T(8,128)(2,1)S(1)}, u32[]{:S(2)}, u32[]{:S(2)}) %collective-permute-start.8) | collective-permute-done | bytes 131104 | tf_op jit(solution)/shard_map/ppermute | solution.py:537
  71.1 0.0 collective-permute-done.7.refs_8_
  71.1 7.0 %sweep.1 = bf16[64,1024]{1,0:T(8,128)(2,1)} custom-call(f32[16,1024]{1,0:T(8,128)S(1)} %get-tuple-element.17.pack_ref.before_ref.refs_0_, f32[16,1024]{1,0:T(8,128)S(1)} %get-tuple-element.18.after_ref.refs_1_, bf16[64,1024]{1,0:T(8,128)(2,1)S(1)} %bitcast.5, bf16[32,1024]{1,0:T(8,128)(2,1)S(1)} %get-tuple-element.21.refs_3_, ...), custom_call_target="tpu_custom_call" | custom-call | flops 1610612736 | bytes 25165824 | tf_op jit(solution)/shard_map/sweep/pallas_call | solution.py:478
  (2 shorter events, 0.1 us)
Async XLA Ops:
  0.0 28.7 %copy-start = (bf16[1,64,1024]{2,1,0:T(8,128)(2,1)S(1)}, bf16[1,64,1024]{2,1,0:T(8,128)(2,1)}, u32[]{:S(2)}) copy-start(bf16[1,64,1024]{2,1,0:T(8,128)(2,1)} %param.6) | copy-start | bytes 393220
  0.0 28.7 %copy-start.1 = (f32[2,32]{1,0:T(2,128)S(1)}, f32[2,32]{1,0:T(2,128)}, u32[]{:S(2)}) copy-start(f32[2,32]{1,0:T(2,128)} %refs_5_.3) | copy-start | bytes 772
  1.6 7.3 %collective-permute-start.1 = (f32[48,1024]{1,0:T(8,128)S(1)}, f32[48,1024]{1,0:T(8,128)S(1)}, u32[]{:S(2)}, u32[]{:S(2)}) collective-permute-start(f32[48,1024]{1,0:T(8,128)S(1)} %get-tuple-element.16), channel_id=1, source_target_pairs={{4,8},{12,16},{20,24},{8,4},{16,12},{24,20},{5,9},{13,17},{21,25},... | collective-permute-start | bytes 589832 | tf_op jit(solution)/shard_map/ppermute | solution.py:529
  5.4 3.5 %collective-permute-start = (f32[48,1024]{1,0:T(8,128)S(1)}, f32[48,1024]{1,0:T(8,128)S(1)}, u32[]{:S(2)}, u32[]{:S(2)}) collective-permute-start(f32[48,1024]{1,0:T(8,128)S(1)} %get-tuple-element.15.own_ref), channel_id=1, source_target_pairs={{0,4},{8,12},{16,20},{24,28},{4,0},{12,8},{20,16},{28,24},{1,5},{9... | collective-permute-start | bytes 589832 | tf_op jit(solution)/shard_map/ppermute | solution.py:529
  8.9 19.8 %collective-permute-start.4 = (bf16[64,1024]{1,0:T(8,128)(2,1)S(1)}, bf16[64,1024]{1,0:T(8,128)(2,1)S(1)}, u32[]{:S(2)}, u32[]{:S(2)}) collective-permute-start(bf16[64,1024]{1,0:T(8,128)(2,1)S(1)} %get-tuple-element.20.rest_0_), channel_id=1, source_target_pairs={{0,3},{1,2},{2,1},{3,0},{4,7},{5,6},{6,5},{7,4},{8,11},{9,10},{10,... | collective-permute-start | bytes 393224 | tf_op jit(solution)/shard_map/ppermute | solution.py:537
  11.2 17.5 %collective-permute-start.3 = (bf16[64,1024]{1,0:T(8,128)(2,1)S(1)}, bf16[64,1024]{1,0:T(8,128)(2,1)S(1)}, u32[]{:S(2)}, u32[]{:S(2)}) collective-permute-start(bf16[64,1024]{1,0:T(8,128)(2,1)S(1)} %get-tuple-element.20.rest_0_), channel_id=1, source_target_pairs={{0,2},{1,3},{2,0},{3,1},{4,6},{5,7},{6,4},{7,5},{8,10},{9,11},{10,... | collective-permute-start | bytes 393224 | tf_op jit(solution)/shard_map/ppermute | solution.py:537
  11.4 17.3 %collective-permute-start.2 = (bf16[64,1024]{1,0:T(8,128)(2,1)S(1)}, bf16[64,1024]{1,0:T(8,128)(2,1)S(1)}, u32[]{:S(2)}, u32[]{:S(2)}) collective-permute-start(bf16[64,1024]{1,0:T(8,128)(2,1)S(1)} %get-tuple-element.20.rest_0_), channel_id=1, source_target_pairs={{0,1},{1,0},{2,3},{3,2},{4,5},{5,4},{6,7},{7,6},{8,9},{9,8},{10,11... | collective-permute-start | bytes 393224 | tf_op jit(solution)/shard_map/ppermute | solution.py:537
  54.0 5.4 %collective-permute-start.5 = (bf16[32,1024]{1,0:T(8,128)(2,1)S(1)}, bf16[32,1024]{1,0:T(8,128)(2,1)S(1)}, u32[]{:S(2)}, u32[]{:S(2)}) collective-permute-start(bf16[32,1024]{1,0:T(8,128)(2,1)S(1)} %get-tuple-element.21.refs_3_), channel_id=1, source_target_pairs={{0,4},{8,12},{16,20},{24,28},{4,0},{12,8},{20,16},{28,24},{1,5},{9... | collective-permute-start | bytes 196616 | tf_op jit(solution)/shard_map/ppermute | solution.py:529
  56.3 5.6 %collective-permute-start.6 = (bf16[32,1024]{1,0:T(8,128)(2,1)S(1)}, bf16[32,1024]{1,0:T(8,128)(2,1)S(1)}, u32[]{:S(2)}, u32[]{:S(2)}) collective-permute-start(bf16[32,1024]{1,0:T(8,128)(2,1)S(1)} %get-tuple-element.22.refs_4_), channel_id=1, source_target_pairs={{4,8},{12,16},{20,24},{8,4},{16,12},{24,20},{5,9},{13,17},{21,25},... | collective-permute-start | bytes 196616 | tf_op jit(solution)/shard_map/ppermute | solution.py:529
  61.9 6.0 %collective-permute-start.9 = (bf16[64,1024]{1,0:T(8,128)(2,1)S(1)}, bf16[64,1024]{1,0:T(8,128)(2,1)S(1)}, u32[]{:S(2)}, u32[]{:S(2)}) collective-permute-start(bf16[64,1024]{1,0:T(8,128)(2,1)S(1)} %join.3.refs_8_), channel_id=1, source_target_pairs={{0,3},{1,2},{2,1},{3,0},{4,7},{5,6},{6,5},{7,4},{8,11},{9,10},{10,... | collective-permute-start | bytes 393224 | tf_op jit(solution)/shard_map/ppermute | solution.py:537
  64.0 7.1 %collective-permute-start.8 = (bf16[64,1024]{1,0:T(8,128)(2,1)S(1)}, bf16[64,1024]{1,0:T(8,128)(2,1)S(1)}, u32[]{:S(2)}, u32[]{:S(2)}) collective-permute-start(bf16[64,1024]{1,0:T(8,128)(2,1)S(1)} %join.3.refs_8_), channel_id=1, source_target_pairs={{0,2},{1,3},{2,0},{3,1},{4,6},{5,7},{6,4},{7,5},{8,10},{9,11},{10,... | collective-permute-start | bytes 393224 | tf_op jit(solution)/shard_map/ppermute | solution.py:537
  64.0 7.1 %collective-permute-start.7 = (bf16[64,1024]{1,0:T(8,128)(2,1)S(1)}, bf16[64,1024]{1,0:T(8,128)(2,1)S(1)}, u32[]{:S(2)}, u32[]{:S(2)}) collective-permute-start(bf16[64,1024]{1,0:T(8,128)(2,1)S(1)} %join.3.refs_8_), channel_id=1, source_target_pairs={{0,1},{1,0},{2,3},{3,2},{4,5},{5,4},{6,7},{7,6},{8,9},{9,8},{10,11... | collective-permute-start | bytes 393224 | tf_op jit(solution)/shard_map/ppermute | solution.py:537

commit v9 on v8

--- a/solution.py
+++ b/solution.py
@@ -214,14 +214,15 @@
 
     lax.fori_loop(0, lax.div(count + PAIR - 1, jnp.int32(PAIR)), body, 0)
 
-    def clear(n, carry):
-        code = list_ref[direction, n, chunk]
-        src, tgt = lax.div(code, jnp.int32(targets)), lax.rem(code, jnp.int32(targets))
-        rows = pl.ds(pl.multiple_of(src * (2 * block), 2 * block), 2 * block)
-        k_ref[tgt, rows, :] = jnp.zeros((2 * block, block), BF)
+    def clear(step, carry):
+        for u in range(4):
+            code = list_ref[direction, jnp.minimum(count + step * 4 + u, size - 1), chunk]
+            src, tgt = lax.div(code, jnp.int32(targets)), lax.rem(code, jnp.int32(targets))
+            rows = pl.ds(pl.multiple_of(src * (2 * block), 2 * block), 2 * block)
+            k_ref[tgt, rows, :] = jnp.zeros((2 * block, block), BF)
         return carry
 
-    lax.fori_loop(count, size, clear, 0)
+    lax.fori_loop(0, lax.div(size - count + 3, jnp.int32(4)), clear, 0)
 
 
 def quarters(pack_ref, channels):

time: 79 us -> 78.2 us (0.990)
    ppermute x6, starting transfers between devices: 5.43 us -> 6.71 us  [gather_patches(): lax.ppermute(value, 'patch', [(i, i ^ k) for i in range(count)])]
    pallas_call x1, Pallas kernels: 25.3 us -> 24.2 us  [call_build_sweep(): pl.pallas_call(functools.partial(build_sweep_kernel, block, per_chunk, le...]
    ppermute x2, starting transfers between devices: 2.3 us -> 1.37 us  [neighbours(): lax.ppermute(first, 'seg', moves[0])]
  transfers between devices with their start and end apart: 10 -> 10, of which waited for: 4 -> 4; matrix products, arithmetic and copies ran while one was open for 0% -> 0% of each run, Pallas kernels for 26% -> 27%
where the time goes in v9:
time: 78.2 us; the launch traced here: 77.8 us
  Pallas kernels  53.6 us (69%)
  starting transfers between devices  14.5 us (19%)
  waiting for transfers between devices  9.62 us (12%)
    pallas_call x1, Pallas kernels, call_build_sweep(): pl.pallas_call(functools.partial(build_sweep_kernel, block, per_chunk, le...  24.2 us
    pallas_call x1, Pallas kernels, call_build(): pl.pallas_call(functools.partial(build_kernel, direction, block, per_chun...  17.6 us
    pallas_call x2, Pallas kernels, call_sweep(): pl.pallas_call(functools.partial(sweep_kernel, groups, block, scale, base...  10.2 us
    ppermute x6, starting transfers between devices, gather_patches(): lax.ppermute(value, 'patch', [(i, i ^ k) for i in range(count)])  6.71 us
    ppermute x2, starting transfers between devices, neighbours(): lax.ppermute(second, 'seg', moves[1])  6.38 us
    ppermute x2, waiting for transfers between devices, neighbours(): lax.ppermute(second, 'seg', moves[1])  6.36 us
    ppermute x6, waiting for transfers between devices, gather_patches(): lax.ppermute(value, 'patch', [(i, i ^ k) for i in range(count)])  3.26 us
    pallas_call x1, Pallas kernels, call_prep(): pl.pallas_call(functools.partial(prep_kernel, per_chunk), out_shape=(pack...  1.59 us
  transfers between devices with their start and end apart: 10, of which 4 were waited for; matrix products, arithmetic and copies ran while one was open for 0% of the time, Pallas kernels for 27%

profile of v9, /device:TPU:17, one launch (start us, length us, event | category | flops | bytes accessed | tf_op | source)
XLA Modules:
  0.0 77.8 jit_solution(7402103774136517285)
XLA Ops:
  0.0 0.0 copy-start
  0.0 0.0 copy-start.1
  0.0 1.6 %prep.1 = (f32[48,1024]{1,0:T(8,128)S(1)}, f32[48,1024]{1,0:T(8,128)S(1)}, s32[2,72,4]{2,1,0:T(8,128)S(1)}) custom-call(f32[1,4096]{1,0:T(1,128)} %axial_ref.1, f32[1,4096]{1,0:T(1,128)} %angle_ref.1, f32[1,4096]{1,0:T(1,128)} %area_ref.1, bf16[64,1024]{1,0:T(8,128)(2,1)} %bitcast.2, s32[1,2,8,32]{3,2,1,0:T(8,128)} %vis_ref.1), custom_call_target="tpu_custom_call" | custom-call | tf_op jit(solution)/shard_map/prep/pallas_call | solution.py:159
  1.6 3.8 %collective-permute-start.1 = (f32[48,1024]{1,0:T(8,128)S(1)}, f32[48,1024]{1,0:T(8,128)S(1)}, u32[]{:S(2)}, u32[]{:S(2)}) collective-permute-start(f32[48,1024]{1,0:T(8,128)S(1)} %get-tuple-element.16), channel_id=1, source_target_pairs={{4,8},{12,16},{20,24},{8,4},{16,12},{24,20},{5,9},{13,17},{21,25},... | collective-permute-start | bytes 589832 | tf_op jit(solution)/shard_map/ppermute | solution.py:530
  5.4 0.1 collective-permute-start
  5.5 3.4 %collective-permute-done.1.cross_ref = f32[48,1024]{1,0:T(8,128)S(1)} collective-permute-done((f32[48,1024]{1,0:T(8,128)S(1)}, f32[48,1024]{1,0:T(8,128)S(1)}, u32[]{:S(2)}, u32[]{:S(2)}) %collective-permute-start.1) | collective-permute-done | bytes 196640 | tf_op jit(solution)/shard_map/ppermute | solution.py:530
  8.9 0.0 collective-permute-done.swap_ref
  8.9 2.2 %collective-permute-start.4 = (bf16[64,1024]{1,0:T(8,128)(2,1)S(1)}, bf16[64,1024]{1,0:T(8,128)(2,1)S(1)}, u32[]{:S(2)}, u32[]{:S(2)}) collective-permute-start(bf16[64,1024]{1,0:T(8,128)(2,1)S(1)} %get-tuple-element.20.rest_0_), channel_id=1, source_target_pairs={{0,3},{1,2},{2,1},{3,0},{4,7},{5,6},{6,5},{7,4},{8,11},{9,10},{10,... | collective-permute-start | bytes 393224 | tf_op jit(solution)/shard_map/ppermute | solution.py:538
  11.2 0.2 collective-permute-start.3
  11.4 0.3 collective-permute-start.2
  11.6 17.6 %build0.1.k0_ref = bf16[8,8192,128]{2,1,0:T(8,128)(2,1)S(1)} custom-call(s32[2,72,4]{2,1,0:T(8,128)S(1)} %get-tuple-element.19.list_ref, f32[48,1024]{1,0:T(8,128)S(1)} %get-tuple-element.15.own_ref, f32[16,1024]{1,0:T(8,128)S(1)} %get-tuple-element.17.pack_ref.before_ref.refs_0_), custom_call_target="tpu_custom_call" | custom-call | tf_op jit(solution)/shard_map/build0/pallas_call | solution.py:276
  29.2 0.0 collective-permute-done.4.rest_3_
  29.2 0.0 collective-permute-done.3.rest_2_
  29.2 0.0 collective-permute-done.2.rest_1_
  29.3 0.0 copy-done
  29.3 0.0 copy-done.1
  29.3 24.2 %build_sweep.1 = (bf16[8,8192,128]{2,1,0:T(8,128)(2,1)S(1)}, bf16[8,8192,128]{2,1,0:T(8,128)(2,1)}, bf16[32,1024]{1,0:T(8,128)(2,1)S(1)}, bf16[32,1024]{1,0:T(8,128)(2,1)S(1)}) custom-call(s32[2,72,4]{2,1,0:T(8,128)S(1)} %get-tuple-element.19.list_ref, f32[48,1024]{1,0:T(8,128)S(1)} %get-tuple-element.15.own_ref, ...), custom_call_target="tpu_custom_call" | custom-call | tf_op jit(solution)/shard_map/build_sweep/pallas_call | solution.py:397
  53.5 1.3 %collective-permute-start.5 = (bf16[32,1024]{1,0:T(8,128)(2,1)S(1)}, bf16[32,1024]{1,0:T(8,128)(2,1)S(1)}, u32[]{:S(2)}, u32[]{:S(2)}) collective-permute-start(bf16[32,1024]{1,0:T(8,128)(2,1)S(1)} %get-tuple-element.21.refs_3_), channel_id=1, source_target_pairs={{0,4},{8,12},{16,20},{24,28},{4,0},{12,8},{20,16},{28,24},{1,5},{9... | collective-permute-start | bytes 196616 | tf_op jit(solution)/shard_map/ppermute | solution.py:530
  54.8 2.6 %collective-permute-start.6 = (bf16[32,1024]{1,0:T(8,128)(2,1)S(1)}, bf16[32,1024]{1,0:T(8,128)(2,1)S(1)}, u32[]{:S(2)}, u32[]{:S(2)}) collective-permute-start(bf16[32,1024]{1,0:T(8,128)(2,1)S(1)} %get-tuple-element.22.refs_4_), channel_id=1, source_target_pairs={{4,8},{12,16},{20,24},{8,4},{16,12},{24,20},{5,9},{13,17},{21,25},... | collective-permute-start | bytes 196616 | tf_op jit(solution)/shard_map/ppermute | solution.py:530
  57.4 0.0 collective-permute-done.5.swap_ref
  57.4 2.9 %collective-permute-done.6.cross_ref = bf16[32,1024]{1,0:T(8,128)(2,1)S(1)} collective-permute-done((bf16[32,1024]{1,0:T(8,128)(2,1)S(1)}, bf16[32,1024]{1,0:T(8,128)(2,1)S(1)}, u32[]{:S(2)}, u32[]{:S(2)}) %collective-permute-start.6) | collective-permute-done | bytes 65568 | tf_op jit(solution)/shard_map/ppermute | solution.py:530
  60.4 3.6 %collective-permute-start.9 = (bf16[64,1024]{1,0:T(8,128)(2,1)S(1)}, bf16[64,1024]{1,0:T(8,128)(2,1)S(1)}, u32[]{:S(2)}, u32[]{:S(2)}) collective-permute-start(bf16[64,1024]{1,0:T(8,128)(2,1)S(1)} %join.3.refs_8_), channel_id=1, source_target_pairs={{0,3},{1,2},{2,1},{3,0},{4,7},{5,6},{6,5},{7,4},{8,11},{9,10},{10,... | collective-permute-start | bytes 393224 | tf_op jit(solution)/shard_map/ppermute | solution.py:538
  64.0 0.0 collective-permute-start.8
  64.0 0.4 collective-permute-start.7
  64.4 3.2 %own_sweep.1.refs_11_ = f32[2,64,1024]{2,1,0:T(8,128)S(1)} custom-call(f32[16,1024]{1,0:T(8,128)S(1)} %get-tuple-element.17.pack_ref.before_ref.refs_0_, f32[16,1024]{1,0:T(8,128)S(1)} %get-tuple-element.18.after_ref.refs_1_, bf16[64,1024]{1,0:T(8,128)(2,1)S(1)} %bitcast.4, bf16[32,1024]{1,0:T(8,128)(2,1)S(1)} %get-tuple-element.21.refs_3_, ...), custom_call_target="tpu_custom_call" | custom-call | flops 536870912 | bytes 8388608 | tf_op jit(solution)/shard_map/own_sweep/pallas_call | solution.py:479
  67.6 0.3 collective-permute-done.9.refs_10_
  67.9 2.9 %collective-permute-done.8.refs_9_ = bf16[64,1024]{1,0:T(8,128)(2,1)S(1)} collective-permute-done((bf16[64,1024]{1,0:T(8,128)(2,1)S(1)}, bf16[64,1024]{1,0:T(8,128)(2,1)S(1)}, u32[]{:S(2)}, u32[]{:S(2)}) %collective-permute-start.8) | collective-permute-done | bytes 131104 | tf_op jit(solution)/shard_map/ppermute | solution.py:538
  70.8 0.0 collective-permute-done.7.refs_8_
  70.8 7.0 %sweep.1 = bf16[64,1024]{1,0:T(8,128)(2,1)} custom-call(f32[16,1024]{1,0:T(8,128)S(1)} %get-tuple-element.17.pack_ref.before_ref.refs_0_, f32[16,1024]{1,0:T(8,128)S(1)} %get-tuple-element.18.after_ref.refs_1_, bf16[64,1024]{1,0:T(8,128)(2,1)S(1)} %bitcast.5, bf16[32,1024]{1,0:T(8,128)(2,1)S(1)} %get-tuple-element.21.refs_3_, ...), custom_call_target="tpu_custom_call" | custom-call | flops 1610612736 | bytes 25165824 | tf_op jit(solution)/shard_map/sweep/pallas_call | solution.py:479
  (2 shorter events, 0.1 us)
Async XLA Ops:
  0.0 29.3 %copy-start = (bf16[1,64,1024]{2,1,0:T(8,128)(2,1)S(1)}, bf16[1,64,1024]{2,1,0:T(8,128)(2,1)}, u32[]{:S(2)}) copy-start(bf16[1,64,1024]{2,1,0:T(8,128)(2,1)} %param.6) | copy-start | bytes 393220
  0.0 29.3 %copy-start.1 = (f32[2,32]{1,0:T(2,128)S(1)}, f32[2,32]{1,0:T(2,128)}, u32[]{:S(2)}) copy-start(f32[2,32]{1,0:T(2,128)} %refs_5_.3) | copy-start | bytes 772
  1.6 7.3 %collective-permute-start.1 = (f32[48,1024]{1,0:T(8,128)S(1)}, f32[48,1024]{1,0:T(8,128)S(1)}, u32[]{:S(2)}, u32[]{:S(2)}) collective-permute-start(f32[48,1024]{1,0:T(8,128)S(1)} %get-tuple-element.16), channel_id=1, source_target_pairs={{4,8},{12,16},{20,24},{8,4},{16,12},{24,20},{5,9},{13,17},{21,25},... | collective-permute-start | bytes 589832 | tf_op jit(solution)/shard_map/ppermute | solution.py:530
  5.4 3.5 %collective-permute-start = (f32[48,1024]{1,0:T(8,128)S(1)}, f32[48,1024]{1,0:T(8,128)S(1)}, u32[]{:S(2)}, u32[]{:S(2)}) collective-permute-start(f32[48,1024]{1,0:T(8,128)S(1)} %get-tuple-element.15.own_ref), channel_id=1, source_target_pairs={{0,4},{8,12},{16,20},{24,28},{4,0},{12,8},{20,16},{28,24},{1,5},{9... | collective-permute-start | bytes 589832 | tf_op jit(solution)/shard_map/ppermute | solution.py:530
  8.9 20.3 %collective-permute-start.4 = (bf16[64,1024]{1,0:T(8,128)(2,1)S(1)}, bf16[64,1024]{1,0:T(8,128)(2,1)S(1)}, u32[]{:S(2)}, u32[]{:S(2)}) collective-permute-start(bf16[64,1024]{1,0:T(8,128)(2,1)S(1)} %get-tuple-element.20.rest_0_), channel_id=1, source_target_pairs={{0,3},{1,2},{2,1},{3,0},{4,7},{5,6},{6,5},{7,4},{8,11},{9,10},{10,... | collective-permute-start | bytes 393224 | tf_op jit(solution)/shard_map/ppermute | solution.py:538
  11.2 18.1 %collective-permute-start.3 = (bf16[64,1024]{1,0:T(8,128)(2,1)S(1)}, bf16[64,1024]{1,0:T(8,128)(2,1)S(1)}, u32[]{:S(2)}, u32[]{:S(2)}) collective-permute-start(bf16[64,1024]{1,0:T(8,128)(2,1)S(1)} %get-tuple-element.20.rest_0_), channel_id=1, source_target_pairs={{0,2},{1,3},{2,0},{3,1},{4,6},{5,7},{6,4},{7,5},{8,10},{9,11},{10,... | collective-permute-start | bytes 393224 | tf_op jit(solution)/shard_map/ppermute | solution.py:538
  11.4 17.9 %collective-permute-start.2 = (bf16[64,1024]{1,0:T(8,128)(2,1)S(1)}, bf16[64,1024]{1,0:T(8,128)(2,1)S(1)}, u32[]{:S(2)}, u32[]{:S(2)}) collective-permute-start(bf16[64,1024]{1,0:T(8,128)(2,1)S(1)} %get-tuple-element.20.rest_0_), channel_id=1, source_target_pairs={{0,1},{1,0},{2,3},{3,2},{4,5},{5,4},{6,7},{7,6},{8,9},{9,8},{10,11... | collective-permute-start | bytes 393224 | tf_op jit(solution)/shard_map/ppermute | solution.py:538
  53.5 3.9 %collective-permute-start.5 = (bf16[32,1024]{1,0:T(8,128)(2,1)S(1)}, bf16[32,1024]{1,0:T(8,128)(2,1)S(1)}, u32[]{:S(2)}, u32[]{:S(2)}) collective-permute-start(bf16[32,1024]{1,0:T(8,128)(2,1)S(1)} %get-tuple-element.21.refs_3_), channel_id=1, source_target_pairs={{0,4},{8,12},{16,20},{24,28},{4,0},{12,8},{20,16},{28,24},{1,5},{9... | collective-permute-start | bytes 196616 | tf_op jit(solution)/shard_map/ppermute | solution.py:530
  54.8 5.6 %collective-permute-start.6 = (bf16[32,1024]{1,0:T(8,128)(2,1)S(1)}, bf16[32,1024]{1,0:T(8,128)(2,1)S(1)}, u32[]{:S(2)}, u32[]{:S(2)}) collective-permute-start(bf16[32,1024]{1,0:T(8,128)(2,1)S(1)} %get-tuple-element.22.refs_4_), channel_id=1, source_target_pairs={{4,8},{12,16},{20,24},{8,4},{16,12},{24,20},{5,9},{13,17},{21,25},... | collective-permute-start | bytes 196616 | tf_op jit(solution)/shard_map/ppermute | solution.py:530
  60.4 7.5 %collective-permute-start.9 = (bf16[64,1024]{1,0:T(8,128)(2,1)S(1)}, bf16[64,1024]{1,0:T(8,128)(2,1)S(1)}, u32[]{:S(2)}, u32[]{:S(2)}) collective-permute-start(bf16[64,1024]{1,0:T(8,128)(2,1)S(1)} %join.3.refs_8_), channel_id=1, source_target_pairs={{0,3},{1,2},{2,1},{3,0},{4,7},{5,6},{6,5},{7,4},{8,11},{9,10},{10,... | collective-permute-start | bytes 393224 | tf_op jit(solution)/shard_map/ppermute | solution.py:538
  64.0 6.8 %collective-permute-start.8 = (bf16[64,1024]{1,0:T(8,128)(2,1)S(1)}, bf16[64,1024]{1,0:T(8,128)(2,1)S(1)}, u32[]{:S(2)}, u32[]{:S(2)}) collective-permute-start(bf16[64,1024]{1,0:T(8,128)(2,1)S(1)} %join.3.refs_8_), channel_id=1, source_target_pairs={{0,2},{1,3},{2,0},{3,1},{4,6},{5,7},{6,4},{7,5},{8,10},{9,11},{10,... | collective-permute-start | bytes 393224 | tf_op jit(solution)/shard_map/ppermute | solution.py:538
  64.0 6.8 %collective-permute-start.7 = (bf16[64,1024]{1,0:T(8,128)(2,1)S(1)}, bf16[64,1024]{1,0:T(8,128)(2,1)S(1)}, u32[]{:S(2)}, u32[]{:S(2)}) collective-permute-start(bf16[64,1024]{1,0:T(8,128)(2,1)S(1)} %join.3.refs_8_), channel_id=1, source_target_pairs={{0,1},{1,0},{2,3},{3,2},{4,5},{5,4},{6,7},{7,6},{8,9},{9,8},{10,11... | collective-permute-start | bytes 393224 | tf_op jit(solution)/shard_map/ppermute | solution.py:538
